TPU v7x, 512 devices: a whole 4x4x16 slice. The times are simulated.
512 devices in a mesh: slab: 128 (over x, z, core), ctrl: 4 (over y).
Axes of the slice: x: 4, y: 4, z: 16, core: 2. Of those that a mesh axis runs over, the one named last changes fastest.
Arguments:
- face_pressure: float32 [2097152], P(('slab', 'ctrl')), may hold values from 0 to 18
- face_area: float32 [3, 2097152], P(None, ('slab', 'ctrl')), may hold values from -0.00390625 to 0.00390625
- face_center: float32 [3, 2097152], P(None, ('slab', 'ctrl')), may hold values from -6 to 6
- motion: float32 [6], replicated, may hold values from -1 to 1
- inverse_mass: float32 [6], replicated, may hold values from 0.5 to 2
- control_points: float32 [3, 8192], P(None, ('slab', 'ctrl')), may hold values from -4 to 4
- control_modes: float32 [18, 8192], P(None, ('slab', 'ctrl')), may hold values from -0.25 to 0.25
- node_points: float32 [3, 1024, 32, 128], P(None, 'slab', 'ctrl'), may hold values from -5 to 5
- tile_list: int32 [1024, 32, 16], P('slab', 'ctrl'), may hold values from 0 to 63, as said below
- tile_count: int32 [1024, 32], P('slab', 'ctrl'), may hold values from 0 to 16, as said below
Outputs:
- node_shift: float32 [3, 1024, 32, 128], P(None, 'slab', 'ctrl')
- cell_volume: float32 [1024, 32, 128], P('slab', 'ctrl')
- volume_change: float32 [1024, 32, 128], P('slab', 'ctrl')
- new_state: float32 [6], replicated
Inputs may be any that keep to these rules, and one draw needn't show every extreme that they name: `tile_list`: the entries of one line are distinct tile numbers; only the first tile_count entries of a line are live, the others are to be ignored. `tile_count`: every line in the planes x with 3072 <= 8 x < 5120 has 16 live entries; every other line has at most 4.
All inputs are finite; a program needn't handle non-finite values.
Results may differ from a plain program's by a relative error of at most 0.0003.
Values sent between devices are 32-bit elements; how exact they have to be, the bound alone decides.
A program may use at most 64 MiB of HBM per device.

v0:
```python
import jax
import jax.numpy as jnp
from jax import lax
from jax.sharding import PartitionSpec as P

TILE = 128


TIME_STEP = 0.5
RADIUS = 4.0
GRAVITY = (0.0, 0.0, -0.5, 0.0, 0.0, 0.0)


def shifted(value, axis, by):
    devices = lax.axis_size(axis)
    pairs = [(i, i + by) for i in range(devices) if 0 <= i + by < devices]
    return lax.ppermute(value, axis, pairs)


def surface_loads(pressure, area, center):
    pushed = pressure[None, :] * area
    forces = jnp.sum(pushed, axis=1)
    moment_x = jnp.sum(center[1] * pushed[2] - center[2] * pushed[1])
    moment_y = jnp.sum(center[2] * pushed[0] - center[0] * pushed[2])
    moment_z = jnp.sum(center[0] * pushed[1] - center[1] * pushed[0])
    return jnp.concatenate([forces, jnp.stack([moment_x, moment_y, moment_z])])


def advance(total_loads, motion, inverse_mass):
    acceleration = inverse_mass * total_loads + jnp.array(GRAVITY, dtype=jnp.float32)
    new_state = motion + TIME_STEP * acceleration
    rigid_step = TIME_STEP * motion + 0.5 * TIME_STEP * TIME_STEP * acceleration
    return (new_state, rigid_step)


def mode_mix(rigid_step, modes):
    shaped = modes.reshape(6, 3, modes.shape[1])
    return jnp.einsum("k,kcj->cj", rigid_step, shaped, precision=lax.Precision.HIGHEST)


def kernel_sum(points, tile_ids, counts, center_tiles, coeff_tiles):
    longest = jnp.max(counts)

    def accumulate(entry_id, running):
        picked = jnp.take(tile_ids, entry_id, axis=1)
        centers = jnp.take(center_tiles, picked, axis=1)
        coeffs = jnp.take(coeff_tiles, picked, axis=1)
        square = jnp.zeros((points.shape[1], points.shape[2], centers.shape[2]), jnp.float32)
        for axis_id in range(3):
            offset = points[axis_id][:, :, None] - centers[axis_id][:, None, :]
            square = square + offset * offset
        radial = jnp.sqrt(square) / RADIUS
        falloff = jnp.maximum(1.0 - radial, 0.0)
        fourth = falloff * falloff
        fourth = fourth * fourth
        kernel = fourth * (4.0 * radial + 1.0)
        alive_mask = (entry_id < counts)[:, None, None]
        kernel = jnp.where(alive_mask, kernel, 0.0)
        return running + jnp.einsum("lnj,clj->cln", kernel, coeffs, precision=lax.Precision.HIGHEST)

    start = jnp.zeros((3, points.shape[1], points.shape[2]), jnp.float32)
    return lax.fori_loop(0, longest, accumulate, start)


def cell_volumes(lattice):
    span_x = lattice.shape[-3] - 1
    span_y = lattice.shape[-2] - 1
    corners = {}
    for shift_x in range(2):
        for shift_y in range(2):
            for shift_z in range(2):
                sliced = lattice[..., shift_x : shift_x + span_x, shift_y : shift_y + span_y, :]
                if shift_z == 1:
                    sliced = jnp.concatenate(
                        [sliced[..., 1:], jnp.zeros_like(sliced[..., :1])], axis=-1
                    )
                corners[shift_x, shift_y, shift_z] = sliced
    edge_x = 0.0
    edge_y = 0.0
    edge_z = 0.0
    for first in range(2):
        for second in range(2):
            edge_x = edge_x + corners[1, first, second] - corners[0, first, second]
            edge_y = edge_y + corners[first, 1, second] - corners[first, 0, second]
            edge_z = edge_z + corners[first, second, 1] - corners[first, second, 0]
    edge_x = 0.25 * edge_x
    edge_y = 0.25 * edge_y
    edge_z = 0.25 * edge_z
    ex0, ex1, ex2 = (edge_x[..., 0, :, :, :], edge_x[..., 1, :, :, :], edge_x[..., 2, :, :, :])
    ey0, ey1, ey2 = (edge_y[..., 0, :, :, :], edge_y[..., 1, :, :, :], edge_y[..., 2, :, :, :])
    ez0, ez1, ez2 = (edge_z[..., 0, :, :, :], edge_z[..., 1, :, :, :], edge_z[..., 2, :, :, :])
    return (
        ex0 * (ey1 * ez2 - ey2 * ez1)
        + ex1 * (ey2 * ez0 - ey0 * ez2)
        + ex2 * (ey0 * ez1 - ey1 * ez0)
    )


def local(
    face_pressure,
    face_area,
    face_center,
    motion,
    inverse_mass,
    control_points,
    control_modes,
    node_points,
    tile_list,
    tile_count,
):
    local_loads = surface_loads(face_pressure, face_area, face_center)
    centers_all, modes_all = (
        lax.all_gather(control_points, ("slab", "ctrl"), axis=1, tiled=True),
        lax.all_gather(control_modes, ("slab", "ctrl"), axis=1, tiled=True),
    )
    total_loads = lax.psum(local_loads, ("slab", "ctrl"))
    new_state, rigid_step = advance(total_loads, motion, inverse_mass)
    coeffs_all = mode_mix(rigid_step, modes_all)
    center_tiles = centers_all.reshape(3, -1, TILE)
    coeff_tiles = coeffs_all.reshape(3, -1, TILE)
    plane_count = node_points.shape[1]
    row_count = node_points.shape[2]
    line_nodes = node_points.shape[3]
    slots = tile_list.shape[2]
    node_shift = kernel_sum(
        node_points.reshape(3, -1, line_nodes),
        tile_list.reshape(-1, slots),
        tile_count.reshape(-1),
        center_tiles,
        coeff_tiles,
    ).reshape(node_points.shape)
    displaced = node_points + node_shift
    stacked = jnp.stack([node_points, displaced])
    next_plane = shifted(stacked[:, :, :1], "slab", -1)
    widened = jnp.concatenate([stacked, next_plane], axis=2)
    next_row = shifted(widened[:, :, :, :1], "ctrl", -1)
    extended = jnp.concatenate([widened, next_row], axis=3)
    volumes = cell_volumes(extended)
    plane_total = plane_count * lax.axis_size("slab")
    row_total = row_count * lax.axis_size("ctrl")
    plane_ids = lax.axis_index("slab") * plane_count + jnp.arange(plane_count, dtype=jnp.int32)
    row_ids = lax.axis_index("ctrl") * row_count + jnp.arange(row_count, dtype=jnp.int32)
    depth_ids = jnp.arange(line_nodes, dtype=jnp.int32)
    inside = (plane_ids < plane_total - 1)[:, None, None]
    inside = inside & (row_ids < row_total - 1)[None, :, None]
    inside = inside & (depth_ids < line_nodes - 1)[None, None, :]
    volumes = jnp.where(inside[None], volumes, 0.0)
    return (node_shift, volumes[1], volumes[1] - volumes[0], new_state)


def solution(mesh):
    placed = (
        P(("slab", "ctrl")),
        P(None, ("slab", "ctrl")),
        P(None, ("slab", "ctrl")),
        P(),
        P(),
        P(None, ("slab", "ctrl")),
        P(None, ("slab", "ctrl")),
        P(None, "slab", "ctrl", None),
        P("slab", "ctrl", None),
        P("slab", "ctrl"),
    )
    return jax.shard_map(
        local,
        mesh=mesh,
        in_specs=placed,
        out_specs=(
            P(None, "slab", "ctrl", None),
            P("slab", "ctrl", None),
            P("slab", "ctrl", None),
            P(),
        ),
        check_vma=False,
    )
```

profile of v0, /device:TPU:4, one launch (start us, length us, event | category | flops | bytes accessed | tf_op | source)
XLA Modules:
  0.0 821.4 jit_solution(15603495582386284360)
XLA Ops:
  0.6 1.0 fusion.60
  1.6 1.7 subtract_reduce_fusion.2
  3.3 2.0 pad_maximum_fusion.4
  5.3 108.6 %psum.7 = f32[6]{0:T(128)S(1)} all-reduce(f32[6]{0:T(128)S(1)} %pad_maximum_fusion.4), channel_id=1, replica_groups=mesh['slab'=128,'ctrl'=4] {'slab','ctrl'}, use_global_device_ids=true, to_apply=%region_5.0 | all-reduce | flops 6 | bytes 48 | tf_op jit(solution)/shard_map/psum | solution.py:116
  113.9 250.8 %all_gather.6 = f32[18,8192]{0,1:T(8,128)} all-gather(f32[18,16]{0,1:T(8,128)} %param.21), channel_id=1, replica_groups=mesh['slab'=128,'ctrl'=4] {'slab','ctrl'}, dimensions={1}, use_global_device_ids=true | all-gather | bytes 590976 | tf_op jit(solution)/shard_map/all_gather | solution.py:114
  364.8 2.9 copy.23
  368.4 1.1 fusion.43
  369.6 229.6 %all-gather = f32[512,16,3]{1,2,0:T(4,128)S(1)} all-gather(f32[1,16,3]{1,2,0:T(4,128)S(1)} %bitcast.94), channel_id=1, replica_groups=mesh['slab'=128,'ctrl'=4] {'slab','ctrl'}, dimensions={0}, use_global_device_ids=true | all-gather | bytes 98496 | tf_op jit(solution)/shard_map/all_gather | solution.py:113
  599.8 0.6 reduce_max.9
  600.5 207.6 %while.13 = (s32[]{:T(128)}, f32[3,64,128]{2,0,1:T(4,128)S(1)}, s32[]{:T(128)}, s32[64,16]{0,1:T(8,128)S(1)}, f32[3,64,128]{2,0,1:T(4,128)S(1)}, /*index=5*/s32[...) while((s32[]{:T(128)}, f32[3,64,128]{2,0,1:T(4,128)S(1)}, ...), condition=%wide.region_7.9_spmd, body=%wide.region_6.8_spmd.sunk | while | flops 54601224 | bytes 1480693 | solution.py:62
  601.2 0.7 gather_fusion
  602.1 0.7 gather_fusion.1
  602.7 10.6 %fusion.70 = f32[3,64,128]{2,0,1:T(4,128)S(1)} fusion(f32[3,64,128]{2,0,1:T(4,128)S(1)} %get-tuple-element.258, f32[64,128]{1,0:T(8,128)S(1)} %bitcast.91, f32[64,128]{1,0:T(8,128)S(1)} %get-tuple-element.239, f32[64,128]{1,0:T(8,128)S(1)} %bitcast.92, f32[64,128]{1,0:T(8,128)S(1)} %get-tuple-element.241, f32[64,128]{1,0:T(8,128)S(1)} %bitcast.90, ...), kind=kOutput, calls=%fused_computation.31.clone.1 | convolution fusion | flops 54575104 | bytes 491648 | tf_op jit(solution)/shard_map/while/body/lnj,clj->cln/dot_general | solution.py:59
  614.1 0.7 gather_fusion
  615.0 0.7 gather_fusion.1
  615.7 10.6 %fusion.70 = f32[3,64,128]{2,0,1:T(4,128)S(1)} fusion(f32[3,64,128]{2,0,1:T(4,128)S(1)} %get-tuple-element.258, f32[64,128]{1,0:T(8,128)S(1)} %bitcast.91, f32[64,128]{1,0:T(8,128)S(1)} %get-tuple-element.239, f32[64,128]{1,0:T(8,128)S(1)} %bitcast.92, f32[64,128]{1,0:T(8,128)S(1)} %get-tuple-element.241, f32[64,128]{1,0:T(8,128)S(1)} %bitcast.90, ...), kind=kOutput, calls=%fused_computation.31.clone.1 | convolution fusion | flops 54575104 | bytes 491648 | tf_op jit(solution)/shard_map/while/body/lnj,clj->cln/dot_general | solution.py:59
  627.1 0.7 gather_fusion
  627.9 0.7 gather_fusion.1
  628.6 10.6 %fusion.70 = f32[3,64,128]{2,0,1:T(4,128)S(1)} fusion(f32[3,64,128]{2,0,1:T(4,128)S(1)} %get-tuple-element.258, f32[64,128]{1,0:T(8,128)S(1)} %bitcast.91, f32[64,128]{1,0:T(8,128)S(1)} %get-tuple-element.239, f32[64,128]{1,0:T(8,128)S(1)} %bitcast.92, f32[64,128]{1,0:T(8,128)S(1)} %get-tuple-element.241, f32[64,128]{1,0:T(8,128)S(1)} %bitcast.90, ...), kind=kOutput, calls=%fused_computation.31.clone.1 | convolution fusion | flops 54575104 | bytes 491648 | tf_op jit(solution)/shard_map/while/body/lnj,clj->cln/dot_general | solution.py:59
  640.0 0.7 gather_fusion
  640.9 0.7 gather_fusion.1
  641.5 10.6 %fusion.70 = f32[3,64,128]{2,0,1:T(4,128)S(1)} fusion(f32[3,64,128]{2,0,1:T(4,128)S(1)} %get-tuple-element.258, f32[64,128]{1,0:T(8,128)S(1)} %bitcast.91, f32[64,128]{1,0:T(8,128)S(1)} %get-tuple-element.239, f32[64,128]{1,0:T(8,128)S(1)} %bitcast.92, f32[64,128]{1,0:T(8,128)S(1)} %get-tuple-element.241, f32[64,128]{1,0:T(8,128)S(1)} %bitcast.90, ...), kind=kOutput, calls=%fused_computation.31.clone.1 | convolution fusion | flops 54575104 | bytes 491648 | tf_op jit(solution)/shard_map/while/body/lnj,clj->cln/dot_general | solution.py:59
  652.9 0.7 gather_fusion
  653.8 0.7 gather_fusion.1
  654.5 10.6 %fusion.70 = f32[3,64,128]{2,0,1:T(4,128)S(1)} fusion(f32[3,64,128]{2,0,1:T(4,128)S(1)} %get-tuple-element.258, f32[64,128]{1,0:T(8,128)S(1)} %bitcast.91, f32[64,128]{1,0:T(8,128)S(1)} %get-tuple-element.239, f32[64,128]{1,0:T(8,128)S(1)} %bitcast.92, f32[64,128]{1,0:T(8,128)S(1)} %get-tuple-element.241, f32[64,128]{1,0:T(8,128)S(1)} %bitcast.90, ...), kind=kOutput, calls=%fused_computation.31.clone.1 | convolution fusion | flops 54575104 | bytes 491648 | tf_op jit(solution)/shard_map/while/body/lnj,clj->cln/dot_general | solution.py:59
  665.8 0.7 gather_fusion
  666.7 0.7 gather_fusion.1
  667.4 10.6 %fusion.70 = f32[3,64,128]{2,0,1:T(4,128)S(1)} fusion(f32[3,64,128]{2,0,1:T(4,128)S(1)} %get-tuple-element.258, f32[64,128]{1,0:T(8,128)S(1)} %bitcast.91, f32[64,128]{1,0:T(8,128)S(1)} %get-tuple-element.239, f32[64,128]{1,0:T(8,128)S(1)} %bitcast.92, f32[64,128]{1,0:T(8,128)S(1)} %get-tuple-element.241, f32[64,128]{1,0:T(8,128)S(1)} %bitcast.90, ...), kind=kOutput, calls=%fused_computation.31.clone.1 | convolution fusion | flops 54575104 | bytes 491648 | tf_op jit(solution)/shard_map/while/body/lnj,clj->cln/dot_general | solution.py:59
  678.8 0.7 gather_fusion
  679.7 0.7 gather_fusion.1
  680.3 10.6 %fusion.70 = f32[3,64,128]{2,0,1:T(4,128)S(1)} fusion(f32[3,64,128]{2,0,1:T(4,128)S(1)} %get-tuple-element.258, f32[64,128]{1,0:T(8,128)S(1)} %bitcast.91, f32[64,128]{1,0:T(8,128)S(1)} %get-tuple-element.239, f32[64,128]{1,0:T(8,128)S(1)} %bitcast.92, f32[64,128]{1,0:T(8,128)S(1)} %get-tuple-element.241, f32[64,128]{1,0:T(8,128)S(1)} %bitcast.90, ...), kind=kOutput, calls=%fused_computation.31.clone.1 | convolution fusion | flops 54575104 | bytes 491648 | tf_op jit(solution)/shard_map/while/body/lnj,clj->cln/dot_general | solution.py:59
  691.7 0.7 gather_fusion
  692.6 0.7 gather_fusion.1
  693.3 10.6 %fusion.70 = f32[3,64,128]{2,0,1:T(4,128)S(1)} fusion(f32[3,64,128]{2,0,1:T(4,128)S(1)} %get-tuple-element.258, f32[64,128]{1,0:T(8,128)S(1)} %bitcast.91, f32[64,128]{1,0:T(8,128)S(1)} %get-tuple-element.239, f32[64,128]{1,0:T(8,128)S(1)} %bitcast.92, f32[64,128]{1,0:T(8,128)S(1)} %get-tuple-element.241, f32[64,128]{1,0:T(8,128)S(1)} %bitcast.90, ...), kind=kOutput, calls=%fused_computation.31.clone.1 | convolution fusion | flops 54575104 | bytes 491648 | tf_op jit(solution)/shard_map/while/body/lnj,clj->cln/dot_general | solution.py:59
  704.6 0.7 gather_fusion
  705.5 0.7 gather_fusion.1
  706.2 10.6 %fusion.70 = f32[3,64,128]{2,0,1:T(4,128)S(1)} fusion(f32[3,64,128]{2,0,1:T(4,128)S(1)} %get-tuple-element.258, f32[64,128]{1,0:T(8,128)S(1)} %bitcast.91, f32[64,128]{1,0:T(8,128)S(1)} %get-tuple-element.239, f32[64,128]{1,0:T(8,128)S(1)} %bitcast.92, f32[64,128]{1,0:T(8,128)S(1)} %get-tuple-element.241, f32[64,128]{1,0:T(8,128)S(1)} %bitcast.90, ...), kind=kOutput, calls=%fused_computation.31.clone.1 | convolution fusion | flops 54575104 | bytes 491648 | tf_op jit(solution)/shard_map/while/body/lnj,clj->cln/dot_general | solution.py:59
  717.6 0.7 gather_fusion
  718.5 0.7 gather_fusion.1
  719.1 10.6 %fusion.70 = f32[3,64,128]{2,0,1:T(4,128)S(1)} fusion(f32[3,64,128]{2,0,1:T(4,128)S(1)} %get-tuple-element.258, f32[64,128]{1,0:T(8,128)S(1)} %bitcast.91, f32[64,128]{1,0:T(8,128)S(1)} %get-tuple-element.239, f32[64,128]{1,0:T(8,128)S(1)} %bitcast.92, f32[64,128]{1,0:T(8,128)S(1)} %get-tuple-element.241, f32[64,128]{1,0:T(8,128)S(1)} %bitcast.90, ...), kind=kOutput, calls=%fused_computation.31.clone.1 | convolution fusion | flops 54575104 | bytes 491648 | tf_op jit(solution)/shard_map/while/body/lnj,clj->cln/dot_general | solution.py:59
  730.5 0.7 gather_fusion
  731.4 0.7 gather_fusion.1
  732.1 10.6 %fusion.70 = f32[3,64,128]{2,0,1:T(4,128)S(1)} fusion(f32[3,64,128]{2,0,1:T(4,128)S(1)} %get-tuple-element.258, f32[64,128]{1,0:T(8,128)S(1)} %bitcast.91, f32[64,128]{1,0:T(8,128)S(1)} %get-tuple-element.239, f32[64,128]{1,0:T(8,128)S(1)} %bitcast.92, f32[64,128]{1,0:T(8,128)S(1)} %get-tuple-element.241, f32[64,128]{1,0:T(8,128)S(1)} %bitcast.90, ...), kind=kOutput, calls=%fused_computation.31.clone.1 | convolution fusion | flops 54575104 | bytes 491648 | tf_op jit(solution)/shard_map/while/body/lnj,clj->cln/dot_general | solution.py:59
  743.4 0.7 gather_fusion
  744.3 0.7 gather_fusion.1
  745.0 10.6 %fusion.70 = f32[3,64,128]{2,0,1:T(4,128)S(1)} fusion(f32[3,64,128]{2,0,1:T(4,128)S(1)} %get-tuple-element.258, f32[64,128]{1,0:T(8,128)S(1)} %bitcast.91, f32[64,128]{1,0:T(8,128)S(1)} %get-tuple-element.239, f32[64,128]{1,0:T(8,128)S(1)} %bitcast.92, f32[64,128]{1,0:T(8,128)S(1)} %get-tuple-element.241, f32[64,128]{1,0:T(8,128)S(1)} %bitcast.90, ...), kind=kOutput, calls=%fused_computation.31.clone.1 | convolution fusion | flops 54575104 | bytes 491648 | tf_op jit(solution)/shard_map/while/body/lnj,clj->cln/dot_general | solution.py:59
  756.4 0.7 gather_fusion
  757.3 0.7 gather_fusion.1
  757.9 10.6 %fusion.70 = f32[3,64,128]{2,0,1:T(4,128)S(1)} fusion(f32[3,64,128]{2,0,1:T(4,128)S(1)} %get-tuple-element.258, f32[64,128]{1,0:T(8,128)S(1)} %bitcast.91, f32[64,128]{1,0:T(8,128)S(1)} %get-tuple-element.239, f32[64,128]{1,0:T(8,128)S(1)} %bitcast.92, f32[64,128]{1,0:T(8,128)S(1)} %get-tuple-element.241, f32[64,128]{1,0:T(8,128)S(1)} %bitcast.90, ...), kind=kOutput, calls=%fused_computation.31.clone.1 | convolution fusion | flops 54575104 | bytes 491648 | tf_op jit(solution)/shard_map/while/body/lnj,clj->cln/dot_general | solution.py:59
  769.3 0.7 gather_fusion
  770.2 0.7 gather_fusion.1
  770.9 10.6 %fusion.70 = f32[3,64,128]{2,0,1:T(4,128)S(1)} fusion(f32[3,64,128]{2,0,1:T(4,128)S(1)} %get-tuple-element.258, f32[64,128]{1,0:T(8,128)S(1)} %bitcast.91, f32[64,128]{1,0:T(8,128)S(1)} %get-tuple-element.239, f32[64,128]{1,0:T(8,128)S(1)} %bitcast.92, f32[64,128]{1,0:T(8,128)S(1)} %get-tuple-element.241, f32[64,128]{1,0:T(8,128)S(1)} %bitcast.90, ...), kind=kOutput, calls=%fused_computation.31.clone.1 | convolution fusion | flops 54575104 | bytes 491648 | tf_op jit(solution)/shard_map/while/body/lnj,clj->cln/dot_general | solution.py:59
  782.2 0.7 gather_fusion
  783.1 0.7 gather_fusion.1
  783.8 10.6 %fusion.70 = f32[3,64,128]{2,0,1:T(4,128)S(1)} fusion(f32[3,64,128]{2,0,1:T(4,128)S(1)} %get-tuple-element.258, f32[64,128]{1,0:T(8,128)S(1)} %bitcast.91, f32[64,128]{1,0:T(8,128)S(1)} %get-tuple-element.239, f32[64,128]{1,0:T(8,128)S(1)} %bitcast.92, f32[64,128]{1,0:T(8,128)S(1)} %get-tuple-element.241, f32[64,128]{1,0:T(8,128)S(1)} %bitcast.90, ...), kind=kOutput, calls=%fused_computation.31.clone.1 | convolution fusion | flops 54575104 | bytes 491648 | tf_op jit(solution)/shard_map/while/body/lnj,clj->cln/dot_general | solution.py:59
  795.2 0.7 gather_fusion
  796.0 0.7 gather_fusion.1
  796.7 10.6 %fusion.70 = f32[3,64,128]{2,0,1:T(4,128)S(1)} fusion(f32[3,64,128]{2,0,1:T(4,128)S(1)} %get-tuple-element.258, f32[64,128]{1,0:T(8,128)S(1)} %bitcast.91, f32[64,128]{1,0:T(8,128)S(1)} %get-tuple-element.239, f32[64,128]{1,0:T(8,128)S(1)} %bitcast.92, f32[64,128]{1,0:T(8,128)S(1)} %get-tuple-element.241, f32[64,128]{1,0:T(8,128)S(1)} %bitcast.90, ...), kind=kOutput, calls=%fused_computation.31.clone.1 | convolution fusion | flops 54575104 | bytes 491648 | tf_op jit(solution)/shard_map/while/body/lnj,clj->cln/dot_general | solution.py:59
  808.0 0.7 add_bitcast_fusion
  808.7 4.2 collective-permute-start
  813.8 0.7 collective-permute-done
  814.5 1.3 collective-permute-start.1
  815.9 4.3 collective-permute-done.1
  820.8 0.6 fusion.50
  (117 shorter events, 6.7 us)
Async XLA Ops:
  364.7 3.7 copy-start.3
  364.7 3.7 copy-start.4
  364.7 3.7 copy-start.5
  364.7 4.9 copy-start.6
  367.6 232.0 %copy-start.1 = (s32[8,8,16]{2,1,0:T(8,128)S(1)}, s32[8,8,16]{2,1,0:T(8,128)}, u32[]{:S(2)}) copy-start(s32[8,8,16]{2,1,0:T(8,128)} %param.23) | copy-start | bytes 12292
  367.6 232.1 %copy-start.2 = (s32[8,8]{1,0:T(8,128)S(1)}, s32[8,8]{1,0:T(8,128)}, u32[]{:S(2)}) copy-start(s32[8,8]{1,0:T(8,128)} %param.24) | copy-start | bytes 772
  367.7 232.8 %copy-start = (f32[3,8,8,128]{3,2,1,0:T(8,128)S(1)}, f32[3,8,8,128]{3,2,1,0:T(8,128)}, u32[]{:S(2)}) copy-start(f32[3,8,8,128]{3,2,1,0:T(8,128)} %param.22) | copy-start | bytes 294916
  808.7 5.7 collective-permute-start
  814.5 5.8 collective-permute-start.1
where the time goes:
time: 822 us; the launch traced here: 821 us
  blocking collectives  589 us (72%)
  matrix products  171 us (21%)
  local copies, waits for them, and re-layouts  26.9 us (3%)
  loops' own time  12.4 us (2%)
  other arithmetic  10.3 us (1%)
    all_gather x1, blocking collectives, local(): lax.all_gather(control_modes, ('slab', 'ctrl'), axis=1, tiled=True)  251 us
    all_gather x1, blocking collectives, local(): lax.all_gather(control_points, ('slab', 'ctrl'), axis=1, tiled=True)  230 us
    dot_general x16, matrix products, accumulate(): jnp.einsum('lnj,clj->cln', kernel, coeffs, precision=lax.Precision.HIGHEST)  170 us
    psum x1, blocking collectives, local(): total_loads = lax.psum(local_loads, ('slab', 'ctrl'))  109 us
  transfers between devices with their start and end apart: 2, of which 2 were waited for; matrix products, arithmetic and copies ran while one was open for 0% of the time, Pallas kernels for 0%

commit v1 on v0

v1 whole, which is shorter than its diff:
```python
import functools

import jax
import jax.numpy as jnp
from jax import lax
from jax.experimental import pallas as pl
from jax.experimental.pallas import tpu as pltpu
from jax.sharding import PartitionSpec as P

MESH = pl.DeviceIdType.MESH
TILE = 128
NTILE = 64
F32 = jnp.float32
BF16 = jnp.bfloat16
TIME_STEP = 0.5
GRAVITY = (0.0, 0.0, -0.5, 0.0, 0.0, 0.0)
XS, YS, ZS, CORES = 4, 4, 16, 2
LOAD_LANE = 80


def iota(shape, axis):
    return lax.broadcasted_iota(jnp.int32, shape, axis)


def place():
    slab = lax.axis_index("slab")
    return slab // (ZS * CORES), lax.axis_index("ctrl"), (slab // CORES) % ZS, slab % CORES


def device(x, y, z, core):
    return {"slab": (x % XS * ZS + z % ZS) * CORES + core, "ctrl": y % YS}


def gather_kernel(packed, pressure, area, center, buf, own, send, recv):
    x, y, z, core = place()
    group = core * YS + y
    plane = [(i * core, i * (1 - core)) for i in range(1, 4)]
    turned = [(i * (1 - core), i * core) for i in range(1, 4)]

    barrier = pltpu.get_barrier_semaphore()
    greet = [device(x, y, z + d, core) for d in (1, -1, 2, -2, 3, -3, 4, -4)]
    greet += [device(x + dx, y + dy, z, core) for dx, dy in plane + turned]
    greet += [device(x, y, z, 1 - core)]
    for target in greet:
        pl.semaphore_signal(barrier, inc=1, device_id=target, device_id_type=MESH)

    force = jnp.zeros((3, 128), F32)
    moment = jnp.zeros((3, 128), F32)
    for i in range(pressure.shape[1] // 128):
        at = pl.ds(i * 128, 128)
        pushed = area[:, at] * pressure[:, at]
        c = center[:, at]
        force = force + pushed
        moment = moment + jnp.concatenate(
            [
                c[1:2] * pushed[2:3] - c[2:3] * pushed[1:2],
                c[2:3] * pushed[0:1] - c[0:1] * pushed[2:3],
                c[0:1] * pushed[1:2] - c[1:2] * pushed[0:1],
            ],
            axis=0,
        )
    sums = jnp.sum(jnp.concatenate([force, moment], axis=0), axis=1, keepdims=True)
    lane = iota((6, 128), 1)
    row = iota((6, 128), 0)
    loads = jnp.sum(jnp.where(lane == row + LOAD_LANE, sums, 0.0), axis=0, keepdims=True)
    own[0] = packed[0]
    own[1] = packed[1]
    own[2] = packed[2] + loads
    for r in range(3):
        buf[x, z, r, group] = own[r]

    pl.semaphore_wait(barrier, len(greet))

    pending = []

    def put(src, dst, slot, target):
        copy = pltpu.make_async_remote_copy(
            src_ref=src,
            dst_ref=dst,
            send_sem=send.at[slot],
            recv_sem=recv.at[slot],
            device_id=target,
            device_id_type=MESH,
        )
        copy.start()
        pending.append(copy)
        return copy

    def block(zz):
        return buf.at[x, zz % ZS, :, group]

    near = {}
    for d in (4, 3, 2, 1):
        near[d] = put(own, block(z), d - 1, device(x, y, z + d, core))
        near[-d] = put(own, block(z), d + 3, device(x, y, z - d, core))
    far = []
    for d in (1, 2, 3, 4):
        near[d].wait_recv()
        far.append(put(block(z - d), block(z - d), d + 7, device(x, y, z + 4, core)))
        near[-d].wait_recv()
        if d < 4:
            far.append(put(block(z + d), block(z + d), d + 11, device(x, y, z - 4, core)))
    for copy in far:
        copy.wait_recv()

    first = [
        put(buf.at[x, :, :, group], buf.at[x, :, :, group], 15 + i, device(x + dx, y + dy, z, core))
        for i, (dx, dy) in enumerate(plane)
    ]
    for copy in first:
        copy.wait_recv()

    def cross(i, dx, dy, start):
        target = device(x + dx, y + dy, z, core)

        def make(ref):
            return pltpu.make_async_remote_copy(
                src_ref=ref,
                dst_ref=ref,
                send_sem=send.at[18 + i],
                recv_sem=recv.at[18 + i],
                device_id=target,
                device_id_type=MESH,
            )

        @pl.when(core == 0)
        def _():
            copy = make(buf.at[x, :, :, pl.ds(0, YS)])
            copy.start() if start else copy.wait()

        @pl.when(core == 1)
        def _():
            copy = make(buf.at[:, :, :, group])
            copy.start() if start else copy.wait()

    for i, (dx, dy) in enumerate(turned):
        cross(i, dx, dy, True)
    for i, (dx, dy) in enumerate(turned):
        cross(i, dx, dy, False)

    half = buf.at[:, :, :, pl.ds(core * YS, YS)]
    put(half, half, 21, device(x, y, z, 1 - core)).wait_recv()
    for copy in pending:
        copy.wait_send()


def gather(packed, pressure, area, center):
    vmem = pl.BlockSpec(memory_space=pltpu.VMEM)
    return pl.pallas_call(
        gather_kernel,
        out_shape=jax.ShapeDtypeStruct((XS, ZS, 3, 8, 1, 128), F32),
        in_specs=[vmem] * 4,
        out_specs=vmem,
        scratch_shapes=[
            pltpu.VMEM((3, 1, 128), F32),
            pltpu.SemaphoreType.DMA((22,)),
            pltpu.SemaphoreType.DMA((22,)),
        ],
        compiler_params=pltpu.CompilerParams(collective_id=0, has_side_effects=True),
        name="gather",
    )(packed, pressure, area, center)


def split3(value):
    hi = value.astype(BF16).astype(F32)
    rest = value - hi
    mid = rest.astype(BF16).astype(F32)
    return hi, mid, rest - mid


def regroup(v):
    sub = iota((8, 128), 0)
    grp = iota((8, 128), 1) // 16
    for bit in (1, 2, 4):
        below = pltpu.roll(pltpu.roll(v, 8 - bit, 0), 16 * bit, 1)
        above = pltpu.roll(pltpu.roll(v, bit, 0), 128 - 16 * bit, 1) if bit < 4 else below
        low = (sub & bit) == 0
        same = low == ((grp & bit) == 0)
        v = jnp.where(same, v, jnp.where(low, below, above))
    return v


def pair_kernel(ids, counts, motion, inverse_mass, raw, nodes, shift, state, feats, left, mix):
    def unpack(t, total):
        v = [regroup(raw[t, r]) for r in range(3)]
        for r in range(3):
            feats[t, pl.ds(8 * r, 8), :] = v[r]
        return total + v[2]

    total = lax.fori_loop(0, NTILE, unpack, jnp.zeros((8, 128), F32))
    total = jnp.broadcast_to(total[5:6, :], (8, 128))
    for by in (16, 32, 64):
        total = total + pltpu.roll(total, by, 1)
    rigid = []
    for k in range(6):
        load = jnp.broadcast_to(total[:, k : k + 1], (8, 128))
        acceleration = inverse_mass[k] * load + GRAVITY[k]
        state[k, :, :] = motion[k] + TIME_STEP * acceleration
        rigid.append((TIME_STEP * motion[k] + 0.5 * TIME_STEP * TIME_STEP * acceleration)[0:3])

    sub = iota((8, 128), 0)

    def prepare(t, _):
        p = feats[t, 0:8, :]
        p = jnp.where(sub < 3, p, 0.0)
        square = jnp.sum(p * p, axis=0, keepdims=True)
        hi, mid, lo = split3(jnp.where(sub < 3, p, jnp.where(sub == 3, square, jnp.where(sub == 4, 1.0, 0.0))))
        columns = jnp.concatenate([hi, hi, mid, mid, hi, lo], axis=0)
        left[t] = jnp.transpose(columns, (1, 0)).astype(BF16)
        c = jnp.zeros((3, 128), F32)
        for k in range(6):
            c = c + rigid[k] * feats[t, 3 + 3 * k : 6 + 3 * k, :]
        c = jnp.concatenate([c * (1.0 / 256.0), jnp.zeros((5, 128), F32)], axis=0)
        c_hi = c.astype(BF16).astype(F32)
        mix[t] = jnp.concatenate([c_hi, c - c_hi], axis=0).astype(BF16)
        return 0

    lax.fori_loop(0, NTILE, prepare, 0)

    unroll = 4

    def line(i, _):
        p, r = i // 8, i % 8
        x0 = nodes[0, p, pl.ds(r, 1), :]
        x1 = nodes[1, p, pl.ds(r, 1), :]
        x2 = nodes[2, p, pl.ds(r, 1), :]
        square = x0 * x0 + x1 * x1 + x2 * x2
        rows = jnp.where(sub == 0, -2.0 * x0, 0.0)
        rows = jnp.where(sub == 1, -2.0 * x1, rows)
        rows = jnp.where(sub == 2, -2.0 * x2, rows)
        rows = jnp.where(sub == 3, 1.0, rows)
        rows = jnp.where(sub == 4, square, rows)
        hi, mid, lo = split3(rows)
        right = jnp.concatenate([hi, mid, hi, mid, lo, hi], axis=0).astype(BF16)
        count = counts[p, r]

        def some(g, acc):
            for u in range(unroll):
                e = g * unroll + u
                t = ids[p, r, e]
                s = jnp.dot(left[t], right, preferred_element_type=F32)
                s = jnp.minimum(jnp.maximum(s, 1e-30), 16.0)
                d = s * lax.rsqrt(s)
                v = 4.0 - d
                v = v * v
                k = v * v * (1.0 + d)
                k_hi = k.astype(BF16)
                k_lo = (k - k_hi.astype(F32)).astype(BF16)
                m = mix[t] * jnp.where(e < count, 1.0, 0.0).astype(BF16)
                acc = acc + jnp.dot(m, k_hi, preferred_element_type=F32)
                acc = acc + jnp.dot(m, k_lo, preferred_element_type=F32)
            return acc

        acc = lax.fori_loop(0, (count + unroll - 1) // unroll, some, jnp.zeros((16, 128), F32))
        acc = acc[0:8] + acc[8:16]
        for c in range(3):
            shift[c, p, pl.ds(r, 1), :] = acc[c : c + 1, :]
        return 0

    lax.fori_loop(0, 64, line, 0)


def pair_sums(ids, counts, motion, inverse_mass, raw, nodes):
    vmem = pl.BlockSpec(memory_space=pltpu.VMEM)
    smem = pl.BlockSpec(memory_space=pltpu.SMEM)
    return pl.pallas_call(
        pair_kernel,
        out_shape=(
            jax.ShapeDtypeStruct(nodes.shape, F32),
            jax.ShapeDtypeStruct((6, 8, 128), F32),
        ),
        in_specs=[smem, smem, smem, smem, vmem, vmem],
        out_specs=(vmem, vmem),
        scratch_shapes=[
            pltpu.VMEM((NTILE, 24, 128), F32),
            pltpu.VMEM((NTILE, 128, 48), BF16),
            pltpu.VMEM((NTILE, 16, 128), BF16),
        ],
        name="pairs",
    )(ids, counts, motion, inverse_mass, raw, nodes)


def shifted(value, axis, by):
    devices = lax.axis_size(axis)
    pairs = [(i, i + by) for i in range(devices) if 0 <= i + by < devices]
    return lax.ppermute(value, axis, pairs)


def cell_volumes(lattice):
    span_x = lattice.shape[-3] - 1
    span_y = lattice.shape[-2] - 1
    corners = {}
    for shift_x in range(2):
        for shift_y in range(2):
            for shift_z in range(2):
                sliced = lattice[..., shift_x : shift_x + span_x, shift_y : shift_y + span_y, :]
                if shift_z == 1:
                    sliced = jnp.concatenate([sliced[..., 1:], jnp.zeros_like(sliced[..., :1])], axis=-1)
                corners[shift_x, shift_y, shift_z] = sliced
    edge_x = 0.0
    edge_y = 0.0
    edge_z = 0.0
    for first in range(2):
        for second in range(2):
            edge_x = edge_x + corners[1, first, second] - corners[0, first, second]
            edge_y = edge_y + corners[first, 1, second] - corners[first, 0, second]
            edge_z = edge_z + corners[first, second, 1] - corners[first, second, 0]
    edge_x = 0.25 * edge_x
    edge_y = 0.25 * edge_y
    edge_z = 0.25 * edge_z
    ex0, ex1, ex2 = (edge_x[..., 0, :, :, :], edge_x[..., 1, :, :, :], edge_x[..., 2, :, :, :])
    ey0, ey1, ey2 = (edge_y[..., 0, :, :, :], edge_y[..., 1, :, :, :], edge_y[..., 2, :, :, :])
    ez0, ez1, ez2 = (edge_z[..., 0, :, :, :], edge_z[..., 1, :, :, :], edge_z[..., 2, :, :, :])
    return (
        ex0 * (ey1 * ez2 - ey2 * ez1)
        + ex1 * (ey2 * ez0 - ey0 * ez2)
        + ex2 * (ey0 * ez1 - ey1 * ez0)
    )


def local(
    face_pressure,
    face_area,
    face_center,
    motion,
    inverse_mass,
    control_points,
    control_modes,
    node_points,
    tile_list,
    tile_count,
):
    packed = jnp.concatenate([control_points, control_modes, jnp.zeros((3, 16), F32)], axis=0).reshape(3, 1, 128)
    raw = gather(packed, face_pressure.reshape(1, -1), face_area, face_center)
    node_shift, state = pair_sums(
        tile_list, tile_count, motion, inverse_mass, raw.reshape(NTILE, 3, 8, 128), node_points
    )
    new_state = state[:, 0, 0]

    plane_count = node_points.shape[1]
    row_count = node_points.shape[2]
    line_nodes = node_points.shape[3]
    displaced = node_points + node_shift
    stacked = jnp.stack([node_points, displaced])
    next_plane = shifted(stacked[:, :, :1], "slab", -1)
    widened = jnp.concatenate([stacked, next_plane], axis=2)
    next_row = shifted(widened[:, :, :, :1], "ctrl", -1)
    extended = jnp.concatenate([widened, next_row], axis=3)
    volumes = cell_volumes(extended)
    plane_total = plane_count * lax.axis_size("slab")
    row_total = row_count * lax.axis_size("ctrl")
    plane_ids = lax.axis_index("slab") * plane_count + jnp.arange(plane_count, dtype=jnp.int32)
    row_ids = lax.axis_index("ctrl") * row_count + jnp.arange(row_count, dtype=jnp.int32)
    depth_ids = jnp.arange(line_nodes, dtype=jnp.int32)
    inside = (plane_ids < plane_total - 1)[:, None, None]
    inside = inside & (row_ids < row_total - 1)[None, :, None]
    inside = inside & (depth_ids < line_nodes - 1)[None, None, :]
    volumes = jnp.where(inside[None], volumes, 0.0)
    return (node_shift, volumes[1], volumes[1] - volumes[0], new_state)


def solution(mesh):
    placed = (
        P(("slab", "ctrl")),
        P(None, ("slab", "ctrl")),
        P(None, ("slab", "ctrl")),
        P(),
        P(),
        P(None, ("slab", "ctrl")),
        P(None, ("slab", "ctrl")),
        P(None, "slab", "ctrl", None),
        P("slab", "ctrl", None),
        P("slab", "ctrl"),
    )
    return jax.shard_map(
        local,
        mesh=mesh,
        in_specs=placed,
        out_specs=(
            P(None, "slab", "ctrl", None),
            P("slab", "ctrl", None),
            P("slab", "ctrl", None),
            P(),
        ),
        check_vma=False,
    )
```

time: 822 us -> 208 us (0.25)
  blocking collectives: 589 us -> 0 us
  Pallas kernels: 0 us -> 191 us
  matrix products: 171 us -> 0 us
  local copies, waits for them, and re-layouts: 26.9 us -> 3.23 us
  loops' own time: 12.4 us -> 0 us
    all_gather x2 -> x0, blocking collectives: 480 us -> none  [the longest x1 251 us: local(): lax.all_gather(control_modes, ('slab', 'ctrl'), axis=1, tiled=True)]
    pallas_call x0 -> x2, Pallas kernels: none -> 191 us  [the longest x1 156 us: pair_sums(): pl.pallas_call(pair_kernel, out_shape=(jax.ShapeDtypeStruct(nodes.shape,...]
    dot_general x17 -> x0, matrix products: 171 us -> none  [the longest x16 170 us: accumulate(): jnp.einsum('lnj,clj->cln', kernel, coeffs, precision=lax.Precision.HIGHEST)]
    psum x1 -> x0, blocking collectives: 109 us -> none  [local(): total_loads = lax.psum(local_loads, ('slab', 'ctrl'))]
    gather x32 -> x0, local copies, waits for them, and re-layouts: 21 us -> none  [the longest x16 10.5 us: accumulate(): coeffs = jnp.take(coeff_tiles, picked, axis=1)]
    another operation x1 -> x0, loops' own time: 12.4 us -> none  [kernel_sum(): return lax.fori_loop(0, longest, accumulate, start)]
  transfers between devices with their start and end apart: 2 -> 2, of which waited for: 2 -> 1; matrix products, arithmetic and copies ran while one was open for 0% -> 1% of each run, Pallas kernels for 0% -> 0%
where the time goes in v1:
time: 208 us
  Pallas kernels  191 us (92%)
  starting transfers between devices  5.65 us (3%)
  waiting for transfers between devices  4.32 us (2%)
  local copies, waits for them, and re-layouts  3.23 us (2%)
  other arithmetic  2.29 us (1%)
    pallas_call x1, Pallas kernels, pair_sums(): pl.pallas_call(pair_kernel, out_shape=(jax.ShapeDtypeStruct(nodes.shape,...  156 us
    pallas_call x1, Pallas kernels, gather(): pl.pallas_call(gather_kernel, out_shape=jax.ShapeDtypeStruct((XS, ZS, 3,...  34.8 us
    ppermute x2, starting transfers between devices, shifted(): return lax.ppermute(value, axis, pairs)  5.65 us
    ppermute x2, waiting for transfers between devices, shifted(): return lax.ppermute(value, axis, pairs)  4.32 us
  transfers between devices with their start and end apart: 2, of which 1 were waited for; matrix products, arithmetic and copies ran while one was open for 1% of the time, Pallas kernels for 0%

profile of v1, /device:TPU:4, one launch (start us, length us, event | category | flops | bytes accessed | tf_op | source)
XLA Modules:
  0.0 207.5 jit_solution(15156467757030536581)
XLA Ops:
  0.6 0.0 copy-start.1
  0.6 0.8 copy.16
  1.4 0.1 pad.15.clone
  1.5 0.0 copy-done.1
  1.5 0.1 maximum_maximum_fusion
  1.6 0.1 copy.17
  1.6 0.6 reshape.81.packed
  2.3 34.8 %gather.1 = f32[4,16,3,8,1,128]{5,4,3,2,1,0:T(1,128)} custom-call(f32[3,1,128]{2,1,0:T(1,128)} %reshape.81.packed, f32[1,4096]{1,0:T(1,128)} %bitcast.24, f32[3,4096]{1,0:T(4,128)} %area.1, f32[3,4096]{1,0:T(4,128)} %center.1), custom_call_target="tpu_custom_call" | custom-call | tf_op jit(solution)/shard_map/gather/pallas_call | solution.py:149
  37.1 0.0 copy-start
  37.1 156.5 %pairs.1 = (f32[3,8,8,128]{3,2,1,0:T(8,128)}, f32[6,8,128]{2,1,0:T(8,128)}) custom-call(s32[8,8,16]{2,1,0:T(8,128)} %ids.1, s32[8,8]{1,0:T(8,128)} %counts.1, f32[6]{0:T(128)} %motion.1, f32[6]{0:T(128)} %inverse_mass.1, f32[64,3,8,128]{3,2,1,0:T(8,128)} %bitcast.23, f32[3,8,8,128]{3,2,1,0:T(8,128)} %nodes.1), custom_call_target="tpu_custom_call" | custom-call | tf_op jit(solution)/shard_map/pairs/pallas_call | solution.py:266
  193.6 0.0 copy-done
  193.6 0.9 add_bitcast_fusion
  194.5 4.4 %collective-permute-start = (f32[2,3,1,8,128]{4,3,2,1,0:T(8,128)S(1)}, f32[2,3,1,8,128]{4,3,2,1,0:T(8,128)S(1)}, u32[]{:S(2)}, u32[]{:S(2)}) collective-permute-start(f32[2,3,1,8,128]{4,3,2,1,0:T(8,128)S(1)} %fusion.6), channel_id=1, source_target_pairs={{4,0},{8,4},{12,8},{16,12},{20,16},{24,20},{28,24},{32,28},{36,32}... | collective-permute-start | bytes 73736 | tf_op jit(solution)/shard_map/ppermute | solution.py:286
  198.9 0.1 fusion
  199.0 0.1 broadcast_and_fusion.1
  199.1 0.1 broadcast_and_fusion
  199.2 1.4 slice_reduce_fusion
  200.5 0.0 collective-permute-done
  200.6 1.3 collective-permute-start.1
  201.9 0.1 slice.94
  202.0 4.3 %collective-permute-done.1 = f32[2,3,9,1,128]{4,3,2,1,0:T(1,128)S(1)} collective-permute-done((f32[2,3,9,1,128]{4,3,2,1,0:T(1,128)S(1)}, f32[2,3,9,1,128]{4,3,2,1,0:T(1,128)S(1)}, u32[]{:S(2)}, u32[]{:S(2)}) %collective-permute-start.1) | collective-permute-done | bytes 27680 | tf_op jit(solution)/shard_map/ppermute | solution.py:286
  206.4 0.2 fusion.7
  206.5 0.1 subtract_multiply_fusion.1
  206.7 0.2 subtract_multiply_fusion
  206.9 0.6 fusion.5
  (8 shorter events, 0.1 us)
Async XLA Ops:
  0.6 0.9 copy-start.1
  37.1 156.5 %copy-start = (f32[3,8,8,128]{3,2,1,0:T(8,128)S(1)}, f32[3,8,8,128]{3,2,1,0:T(8,128)}, u32[]{:S(2)}) copy-start(f32[3,8,8,128]{3,2,1,0:T(8,128)} %nodes.1) | copy-start | bytes 294916
  194.5 6.1 %collective-permute-start = (f32[2,3,1,8,128]{4,3,2,1,0:T(8,128)S(1)}, f32[2,3,1,8,128]{4,3,2,1,0:T(8,128)S(1)}, u32[]{:S(2)}, u32[]{:S(2)}) collective-permute-start(f32[2,3,1,8,128]{4,3,2,1,0:T(8,128)S(1)} %fusion.6), channel_id=1, source_target_pairs={{4,0},{8,4},{12,8},{16,12},{20,16},{24,20},{28,24},{32,28},{36,32}... | collective-permute-start | bytes 73736 | tf_op jit(solution)/shard_map/ppermute | solution.py:286
  200.6 5.8 %collective-permute-start.1 = (f32[2,3,9,1,128]{4,3,2,1,0:T(1,128)S(1)}, f32[2,3,9,1,128]{4,3,2,1,0:T(1,128)S(1)}, u32[]{:S(2)}, u32[]{:S(2)}) collective-permute-start(f32[2,3,9,1,128]{4,3,2,1,0:T(1,128)S(1)} %pad_maximum_fusion.3), channel_id=1, source_target_pairs={{1,0},{2,1},{3,2},{5,4},{6,5},{7,6},{9,8},{10,9},{11,10},{13,12},{... | collective-permute-start | bytes 82952 | tf_op jit(solution)/shard_map/ppermute | solution.py:286

commit v2 on v1

--- a/solution.py
+++ b/solution.py
@@ -180,14 +180,66 @@
     return v
 
 
-def pair_kernel(ids, counts, motion, inverse_mass, raw, nodes, shift, state, feats, left, mix):
-    def unpack(t, total):
+def node_rows(nodes, p, r):
+    sub = iota((8, 128), 0)
+    x = [nodes[c, p, pl.ds(r, 1), :] for c in range(3)]
+    square = x[0] * x[0] + x[1] * x[1] + x[2] * x[2]
+    rows = jnp.where((sub == 0) | (sub == 3), -2.0 * x[0], 0.0)
+    rows = jnp.where((sub == 1) | (sub == 4), -2.0 * x[1], rows)
+    rows = jnp.where((sub == 2) | (sub == 5), -2.0 * x[2], rows)
+    rows = jnp.where(sub == 7, square, rows)
+    hi, mid, lo = split3(rows)
+    one = sub == 6
+    second = (sub >= 3) & (sub < 6)
+    parts = [
+        jnp.where(one, 1.0, jnp.where(second, mid, hi)),
+        jnp.where(one, 1.0, jnp.where(sub < 3, hi, mid)),
+        jnp.where(one, 1.0, jnp.where(second, hi, lo)),
+        jnp.zeros((8, 128), F32),
+    ]
+    return jnp.concatenate(parts, axis=0).astype(BF16)
+
+
+def control_rows(p):
+    sub = iota((8, 128), 0)
+    p = jnp.where(sub < 3, p, 0.0)
+    square = jnp.sum(p * p, axis=0, keepdims=True)
+    rows = p + pltpu.roll(p, 3, 0) + jnp.where(sub == 6, square, 0.0)
+    hi, mid, lo = split3(rows)
+    one = sub == 7
+    parts = [
+        jnp.where(one, 1.0, hi),
+        jnp.where(one, 1.0, mid),
+        jnp.where(one, 1.0, jnp.where(sub < 3, hi, lo)),
+        jnp.zeros((8, 128), F32),
+    ]
+    return parts
+
+
+BLOCK = 32
+
+
+def pair_kernel(
+    ids, counts, motion, inverse_mass, raw, nodes, shift, state, feats, left_a, left_b, mix_a, mix_b, right, sums, tile_of, line_of
+):
+    lines = nodes.shape[1] * 8
+    sub = iota((8, 128), 0)
+
+    def unpack(t, carry):
+        total, n = carry
         v = [regroup(raw[t, r]) for r in range(3)]
         for r in range(3):
             feats[t, pl.ds(8 * r, 8), :] = v[r]
-        return total + v[2]
-
-    total = lax.fori_loop(0, NTILE, unpack, jnp.zeros((8, 128), F32))
+        p, r = t // 8, t % 8
+        for e in range(16):
+            tile_of[n + e] = ids[p, r, e]
+            line_of[n + e] = t
+        return total + v[2], n + counts[p, r]
+
+    total, n = lax.fori_loop(0, NTILE, unpack, (jnp.zeros((8, 128), F32), 0), unroll=4)
+    for e in range(BLOCK):
+        tile_of[n + e] = 0
+        line_of[n + e] = lines
     total = jnp.broadcast_to(total[5:6, :], (8, 128))
     for by in (16, 32, 64):
         total = total + pltpu.roll(total, by, 1)
@@ -198,71 +250,73 @@
         state[k, :, :] = motion[k] + TIME_STEP * acceleration
         rigid.append((TIME_STEP * motion[k] + 0.5 * TIME_STEP * TIME_STEP * acceleration)[0:3])
 
-    sub = iota((8, 128), 0)
+    wide = iota((128, 64), 1) < 32
 
     def prepare(t, _):
-        p = feats[t, 0:8, :]
-        p = jnp.where(sub < 3, p, 0.0)
-        square = jnp.sum(p * p, axis=0, keepdims=True)
-        hi, mid, lo = split3(jnp.where(sub < 3, p, jnp.where(sub == 3, square, jnp.where(sub == 4, 1.0, 0.0))))
-        columns = jnp.concatenate([hi, hi, mid, mid, hi, lo], axis=0)
-        left[t] = jnp.transpose(columns, (1, 0)).astype(BF16)
+        parts = control_rows(feats[t, 0:8, :])
+        columns = jnp.transpose(jnp.concatenate(parts + parts, axis=0), (1, 0))
+        left_a[t] = jnp.where(wide, columns, 0.0).astype(BF16)
+        left_b[t] = jnp.where(wide, 0.0, columns).astype(BF16)
         c = jnp.zeros((3, 128), F32)
         for k in range(6):
             c = c + rigid[k] * feats[t, 3 + 3 * k : 6 + 3 * k, :]
-        c = jnp.concatenate([c * (1.0 / 256.0), jnp.zeros((5, 128), F32)], axis=0)
+        c = c * (1.0 / 256.0)
+        c = jnp.concatenate([c, c, jnp.zeros((2, 128), F32)], axis=0)
         c_hi = c.astype(BF16).astype(F32)
-        mix[t] = jnp.concatenate([c_hi, c - c_hi], axis=0).astype(BF16)
+        c = jnp.where(sub < 3, c_hi, c - c_hi)
+        zero = jnp.zeros((8, 128), F32)
+        mix_a[t] = jnp.concatenate([c, zero], axis=0).astype(BF16)
+        mix_b[t] = jnp.concatenate([zero, c], axis=0).astype(BF16)
+        right[t] = node_rows(nodes, t // 8, t % 8)
+        sums[t] = zero
         return 0
 
-    lax.fori_loop(0, NTILE, prepare, 0)
-
-    unroll = 4
-
-    def line(i, _):
-        p, r = i // 8, i % 8
-        x0 = nodes[0, p, pl.ds(r, 1), :]
-        x1 = nodes[1, p, pl.ds(r, 1), :]
-        x2 = nodes[2, p, pl.ds(r, 1), :]
-        square = x0 * x0 + x1 * x1 + x2 * x2
-        rows = jnp.where(sub == 0, -2.0 * x0, 0.0)
-        rows = jnp.where(sub == 1, -2.0 * x1, rows)
-        rows = jnp.where(sub == 2, -2.0 * x2, rows)
-        rows = jnp.where(sub == 3, 1.0, rows)
-        rows = jnp.where(sub == 4, square, rows)
-        hi, mid, lo = split3(rows)
-        right = jnp.concatenate([hi, mid, hi, mid, lo, hi], axis=0).astype(BF16)
-        count = counts[p, r]
-
-        def some(g, acc):
-            for u in range(unroll):
-                e = g * unroll + u
-                t = ids[p, r, e]
-                s = jnp.dot(left[t], right, preferred_element_type=F32)
-                s = jnp.minimum(jnp.maximum(s, 1e-30), 16.0)
-                d = s * lax.rsqrt(s)
-                v = 4.0 - d
-                v = v * v
-                k = v * v * (1.0 + d)
-                k_hi = k.astype(BF16)
-                k_lo = (k - k_hi.astype(F32)).astype(BF16)
-                m = mix[t] * jnp.where(e < count, 1.0, 0.0).astype(BF16)
-                acc = acc + jnp.dot(m, k_hi, preferred_element_type=F32)
-                acc = acc + jnp.dot(m, k_lo, preferred_element_type=F32)
-            return acc
-
-        acc = lax.fori_loop(0, (count + unroll - 1) // unroll, some, jnp.zeros((16, 128), F32))
-        acc = acc[0:8] + acc[8:16]
+    lax.fori_loop(0, NTILE, prepare, 0, unroll=4)
+    right[lines] = jnp.zeros((32, 128), BF16)
+    sums[lines] = jnp.zeros((8, 128), F32)
+
+    gap = jnp.zeros((32, 128), BF16)
+
+    def block(g, _):
+        for u in range(0, BLOCK, 2):
+            i = g * BLOCK + u
+            t1, t2 = tile_of[i], tile_of[i + 1]
+            l1, l2 = line_of[i], line_of[i + 1]
+            rhs = jnp.concatenate(
+                [jnp.concatenate([right[l1], gap], axis=1), jnp.concatenate([gap, right[l2]], axis=1)], axis=0
+            )
+            s = jnp.dot(left_a[t1] + left_b[t2], rhs, preferred_element_type=F32)
+            s = jnp.minimum(jnp.maximum(s, 1e-30), 16.0)
+            d = s * lax.rsqrt(s)
+            v = 4.0 - d
+            v = v * v
+            k = v * v * (1.0 + d)
+            hi = k.astype(BF16)
+            lo = (k - hi.astype(F32)).astype(BF16)
+            m = mix_a[t1] + mix_b[t2]
+            out = jnp.dot(
+                jnp.concatenate([m, m], axis=1), jnp.concatenate([hi, lo], axis=0), preferred_element_type=F32
+            )
+            sums[l1] += out[0:8, 0:128]
+            sums[l2] += out[8:16, 128:256]
+        return 0
+
+    lax.fori_loop(0, (n + BLOCK - 1) // BLOCK, block, 0)
+
+    def finish(i, _):
+        v = sums[i]
+        v = v + pltpu.roll(v, 5, 0)
         for c in range(3):
-            shift[c, p, pl.ds(r, 1), :] = acc[c : c + 1, :]
+            shift[c, i // 8, pl.ds(i % 8, 1), :] = v[c : c + 1, :]
         return 0
 
-    lax.fori_loop(0, 64, line, 0)
+    lax.fori_loop(0, lines, finish, 0, unroll=8)
 
 
 def pair_sums(ids, counts, motion, inverse_mass, raw, nodes):
     vmem = pl.BlockSpec(memory_space=pltpu.VMEM)
     smem = pl.BlockSpec(memory_space=pltpu.SMEM)
+    lines = nodes.shape[1] * 8
     return pl.pallas_call(
         pair_kernel,
         out_shape=(
@@ -273,8 +327,14 @@
         out_specs=(vmem, vmem),
         scratch_shapes=[
             pltpu.VMEM((NTILE, 24, 128), F32),
-            pltpu.VMEM((NTILE, 128, 48), BF16),
+            pltpu.VMEM((NTILE, 128, 64), BF16),
+            pltpu.VMEM((NTILE, 128, 64), BF16),
             pltpu.VMEM((NTILE, 16, 128), BF16),
+            pltpu.VMEM((NTILE, 16, 128), BF16),
+            pltpu.VMEM((lines + 1, 32, 128), BF16),
+            pltpu.VMEM((lines + 1, 8, 128), F32),
+            pltpu.SMEM((16 * lines + BLOCK,), jnp.int32),
+            pltpu.SMEM((16 * lines + BLOCK,), jnp.int32),
         ],
         name="pairs",
     )(ids, counts, motion, inverse_mass, raw, nodes)

time: 208 us -> 98.8 us (0.47)
  Pallas kernels: 191 us -> 82.1 us
    pallas_call x1, Pallas kernels: 156 us -> 47.4 us  [pair_sums(): pl.pallas_call(pair_kernel, out_shape=(jax.ShapeDtypeStruct(nodes.shape,...]
  transfers between devices with their start and end apart: 2 -> 2, of which waited for: 1 -> 1; matrix products, arithmetic and copies ran while one was open for 1% -> 2% of each run, Pallas kernels for 0% -> 0%
where the time goes in v2:
time: 98.8 us; the launch traced here: 98.4 us
  Pallas kernels  82.1 us (83%)
  starting transfers between devices  5.65 us (6%)
  waiting for transfers between devices  4.32 us (4%)
  local copies, waits for them, and re-layouts  3.23 us (3%)
  other arithmetic  2.29 us (2%)
    pallas_call x1, Pallas kernels, pair_sums(): pl.pallas_call(pair_kernel, out_shape=(jax.ShapeDtypeStruct(nodes.shape,...  47.4 us
    pallas_call x1, Pallas kernels, gather(): pl.pallas_call(gather_kernel, out_shape=jax.ShapeDtypeStruct((XS, ZS, 3,...  34.8 us
    ppermute x2, starting transfers between devices, shifted(): return lax.ppermute(value, axis, pairs)  5.65 us
    ppermute x2, waiting for transfers between devices, shifted(): return lax.ppermute(value, axis, pairs)  4.32 us
  transfers between devices with their start and end apart: 2, of which 1 were waited for; matrix products, arithmetic and copies ran while one was open for 2% of the time, Pallas kernels for 0%

profile of v2, /device:TPU:4, one launch (start us, length us, event | category | flops | bytes accessed | tf_op | source)
XLA Modules:
  0.0 98.4 jit_solution(12159195663278727186)
XLA Ops:
  0.6 0.0 copy-start.1
  0.6 0.8 copy.16
  1.4 0.1 pad.15.clone
  1.5 0.0 copy-done.1
  1.5 0.1 maximum_maximum_fusion
  1.6 0.1 copy.17
  1.6 0.6 reshape.81.packed
  2.3 34.8 %gather.1 = f32[4,16,3,8,1,128]{5,4,3,2,1,0:T(1,128)} custom-call(f32[3,1,128]{2,1,0:T(1,128)} %reshape.81.packed, f32[1,4096]{1,0:T(1,128)} %bitcast.24, f32[3,4096]{1,0:T(4,128)} %area.1, f32[3,4096]{1,0:T(4,128)} %center.1), custom_call_target="tpu_custom_call" | custom-call | tf_op jit(solution)/shard_map/gather/pallas_call | solution.py:149
  37.1 0.0 copy-start
  37.1 47.4 %pairs.1 = (f32[3,8,8,128]{3,2,1,0:T(8,128)}, f32[6,8,128]{2,1,0:T(8,128)}) custom-call(s32[8,8,16]{2,1,0:T(8,128)} %ids.1, s32[8,8]{1,0:T(8,128)} %counts.1, f32[6]{0:T(128)} %motion.1, f32[6]{0:T(128)} %inverse_mass.1, f32[64,3,8,128]{3,2,1,0:T(8,128)} %bitcast.23, f32[3,8,8,128]{3,2,1,0:T(8,128)} %nodes.1), custom_call_target="tpu_custom_call" | custom-call | tf_op jit(solution)/shard_map/pairs/pallas_call | solution.py:320
  84.4 0.0 copy-done
  84.4 0.9 add_bitcast_fusion
  85.4 4.4 %collective-permute-start = (f32[2,3,1,8,128]{4,3,2,1,0:T(8,128)S(1)}, f32[2,3,1,8,128]{4,3,2,1,0:T(8,128)S(1)}, u32[]{:S(2)}, u32[]{:S(2)}) collective-permute-start(f32[2,3,1,8,128]{4,3,2,1,0:T(8,128)S(1)} %fusion.6), channel_id=1, source_target_pairs={{4,0},{8,4},{12,8},{16,12},{20,16},{24,20},{28,24},{32,28},{36,32}... | collective-permute-start | bytes 73736 | tf_op jit(solution)/shard_map/ppermute | solution.py:346
  89.7 0.1 fusion
  89.9 0.1 broadcast_and_fusion.1
  89.9 0.1 broadcast_and_fusion
  90.0 1.4 %slice_reduce_fusion = f32[6]{0:T(128)} fusion(f32[6,8,128]{2,1,0:T(8,128)} %get-tuple-element.7), kind=kLoop, calls=%fused_computation.26 | loop fusion | bytes 48 | tf_op jit(solution)/shard_map/slice | solution.py:398
  91.4 0.0 collective-permute-done
  91.4 1.3 %collective-permute-start.1 = (f32[2,3,9,1,128]{4,3,2,1,0:T(1,128)S(1)}, f32[2,3,9,1,128]{4,3,2,1,0:T(1,128)S(1)}, u32[]{:S(2)}, u32[]{:S(2)}) collective-permute-start(f32[2,3,9,1,128]{4,3,2,1,0:T(1,128)S(1)} %pad_maximum_fusion.3), channel_id=1, source_target_pairs={{1,0},{2,1},{3,2},{5,4},{6,5},{7,6},{9,8},{10,9},{11,10},{13,12},{... | collective-permute-start | bytes 82952 | tf_op jit(solution)/shard_map/ppermute | solution.py:346
  92.8 0.1 slice.94
  92.9 4.3 %collective-permute-done.1 = f32[2,3,9,1,128]{4,3,2,1,0:T(1,128)S(1)} collective-permute-done((f32[2,3,9,1,128]{4,3,2,1,0:T(1,128)S(1)}, f32[2,3,9,1,128]{4,3,2,1,0:T(1,128)S(1)}, u32[]{:S(2)}, u32[]{:S(2)}) %collective-permute-start.1) | collective-permute-done | bytes 27680 | tf_op jit(solution)/shard_map/ppermute | solution.py:346
  97.2 0.2 fusion.7
  97.4 0.1 subtract_multiply_fusion.1
  97.5 0.2 subtract_multiply_fusion
  97.7 0.6 fusion.5
  (8 shorter events, 0.1 us)
Async XLA Ops:
  0.6 0.9 copy-start.1
  37.1 47.4 %copy-start = (f32[3,8,8,128]{3,2,1,0:T(8,128)S(1)}, f32[3,8,8,128]{3,2,1,0:T(8,128)}, u32[]{:S(2)}) copy-start(f32[3,8,8,128]{3,2,1,0:T(8,128)} %nodes.1) | copy-start | bytes 294916
  85.4 6.1 %collective-permute-start = (f32[2,3,1,8,128]{4,3,2,1,0:T(8,128)S(1)}, f32[2,3,1,8,128]{4,3,2,1,0:T(8,128)S(1)}, u32[]{:S(2)}, u32[]{:S(2)}) collective-permute-start(f32[2,3,1,8,128]{4,3,2,1,0:T(8,128)S(1)} %fusion.6), channel_id=1, source_target_pairs={{4,0},{8,4},{12,8},{16,12},{20,16},{24,20},{28,24},{32,28},{36,32}... | collective-permute-start | bytes 73736 | tf_op jit(solution)/shard_map/ppermute | solution.py:346
  91.4 5.8 %collective-permute-start.1 = (f32[2,3,9,1,128]{4,3,2,1,0:T(1,128)S(1)}, f32[2,3,9,1,128]{4,3,2,1,0:T(1,128)S(1)}, u32[]{:S(2)}, u32[]{:S(2)}) collective-permute-start(f32[2,3,9,1,128]{4,3,2,1,0:T(1,128)S(1)} %pad_maximum_fusion.3), channel_id=1, source_target_pairs={{1,0},{2,1},{3,2},{5,4},{6,5},{7,6},{9,8},{10,9},{11,10},{13,12},{... | collective-permute-start | bytes 82952 | tf_op jit(solution)/shard_map/ppermute | solution.py:346

commit v3 on v2

--- a/solution.py
+++ b/solution.py
@@ -31,7 +31,16 @@
     return {"slab": (x % XS * ZS + z % ZS) * CORES + core, "ctrl": y % YS}
 
 
-def gather_kernel(packed, pressure, area, center, buf, own, send, recv):
+def is_heavy():
+    slab = lax.axis_index("slab")
+    return jnp.logical_and(slab >= 48, slab < 80)
+
+
+def heavy_x(z):
+    return 2 - z // 8
+
+
+def gather_kernel(packed, pressure, area, center, nodes, ids, buf, more_nodes, more_ids, own, send, recv):
     x, y, z, core = place()
     group = core * YS + y
     plane = [(i * core, i * (1 - core)) for i in range(1, 4)]
@@ -71,6 +80,26 @@
 
     pl.semaphore_wait(barrier, len(greet))
 
+    heavy = is_heavy()
+
+    def hand(h, src_plane):
+        target = device(heavy_x(z) + 1 + h, y, z, core)
+        parts = []
+        for i, (src, dst) in enumerate(
+            ((nodes.at[:, pl.ds(src_plane, 2)], more_nodes), (ids.at[pl.ds(src_plane, 2)], more_ids))
+        ):
+            parts.append(
+                pltpu.make_async_remote_copy(
+                    src_ref=src,
+                    dst_ref=dst,
+                    send_sem=send.at[22 + 2 * h + i],
+                    recv_sem=recv.at[22 + i],
+                    device_id=target,
+                    device_id_type=MESH,
+                )
+            )
+        return parts
+
     pending = []
 
     def put(src, dst, slot, target):
@@ -93,6 +122,15 @@
     for d in (4, 3, 2, 1):
         near[d] = put(own, block(z), d - 1, device(x, y, z + d, core))
         near[-d] = put(own, block(z), d + 3, device(x, y, z - d, core))
+
+    @pl.when(heavy)
+    def _():
+        more_nodes[...] = jnp.zeros(more_nodes.shape, F32)
+        more_ids[...] = jnp.zeros(more_ids.shape, jnp.int32)
+        for h in range(3):
+            for copy in hand(h, 1 + 2 * h):
+                copy.start()
+
     far = []
     for d in (1, 2, 3, 4):
         near[d].wait_recv()
@@ -143,22 +181,37 @@
     for copy in pending:
         copy.wait_send()
 
-
-def gather(packed, pressure, area, center):
+    @pl.when(heavy)
+    def _():
+        for h in range(3):
+            for copy in hand(h, 1 + 2 * h):
+                copy.wait_send()
+
+    @pl.when(jnp.logical_not(heavy))
+    def _():
+        for copy in hand(0, 1):
+            copy.wait_recv()
+
+
+def gather(packed, pressure, area, center, nodes, ids):
     vmem = pl.BlockSpec(memory_space=pltpu.VMEM)
     return pl.pallas_call(
         gather_kernel,
-        out_shape=jax.ShapeDtypeStruct((XS, ZS, 3, 8, 1, 128), F32),
-        in_specs=[vmem] * 4,
-        out_specs=vmem,
+        out_shape=(
+            jax.ShapeDtypeStruct((XS, ZS, 3, 8, 1, 128), F32),
+            jax.ShapeDtypeStruct((3, 2, 8, 128), F32),
+            jax.ShapeDtypeStruct((2, 8, 16), jnp.int32),
+        ),
+        in_specs=[vmem] * 6,
+        out_specs=(vmem, vmem, vmem),
         scratch_shapes=[
             pltpu.VMEM((3, 1, 128), F32),
-            pltpu.SemaphoreType.DMA((22,)),
-            pltpu.SemaphoreType.DMA((22,)),
+            pltpu.SemaphoreType.DMA((28,)),
+            pltpu.SemaphoreType.DMA((24,)),
         ],
         compiler_params=pltpu.CompilerParams(collective_id=0, has_side_effects=True),
         name="gather",
-    )(packed, pressure, area, center)
+    )(packed, pressure, area, center, nodes, ids)
 
 
 def split3(value):
@@ -220,9 +273,32 @@
 
 
 def pair_kernel(
-    ids, counts, motion, inverse_mass, raw, nodes, shift, state, feats, left_a, left_b, mix_a, mix_b, right, sums, tile_of, line_of
+    role,
+    ids,
+    more_ids,
+    counts,
+    motion,
+    inverse_mass,
+    raw,
+    nodes,
+    more_nodes,
+    shift,
+    more_shift,
+    plane_edge,
+    row_edge,
+    state,
+    feats,
+    left_a,
+    left_b,
+    mix_a,
+    mix_b,
+    right,
+    sums,
+    tile_of,
+    line_of,
 ):
-    lines = nodes.shape[1] * 8
+    lines = LINES + MORE
+    heavy = role[0] == 1
     sub = iota((8, 128), 0)
 
     def unpack(t, carry):
@@ -230,11 +306,23 @@
         v = [regroup(raw[t, r]) for r in range(3)]
         for r in range(3):
             feats[t, pl.ds(8 * r, 8), :] = v[r]
-        p, r = t // 8, t % 8
-        for e in range(16):
-            tile_of[n + e] = ids[p, r, e]
-            line_of[n + e] = t
-        return total + v[2], n + counts[p, r]
+        i = t // 2
+        kept = jnp.minimum(jnp.where(i < 8, i, jnp.where(i < 15, (i - 7) * 8, i + 42)), LINES - 1)
+        q = t // 4
+        hp, hr = jnp.minimum(q // 7, 1), q % 7 + 1
+        line1 = jnp.where(heavy, kept, t)
+        line2 = jnp.where(heavy, kept, LINES + hp * 8 + hr)
+        start1 = jnp.where(heavy, 8 * (t % 2), 0)
+        keep = jnp.where(t < 44, 4, 0)
+        for e in range(4):
+            tile_of[n + e] = ids[line1 // 8, line1 % 8, start1 + e]
+            line_of[n + e] = line1
+        n = n + jnp.where(heavy, keep, counts[t // 8, t % 8])
+        for e in range(4):
+            tile_of[n + e] = jnp.where(heavy, ids[kept // 8, kept % 8, start1 + 4 + e], more_ids[hp, hr, 4 * (t % 4) + e])
+            line_of[n + e] = line2
+        n = n + jnp.where(heavy, keep, jnp.where(t < 56, 4, 0))
+        return total + v[2], n
 
     total, n = lax.fori_loop(0, NTILE, unpack, (jnp.zeros((8, 128), F32), 0), unroll=4)
     for e in range(BLOCK):
@@ -272,6 +360,13 @@
         return 0
 
     lax.fori_loop(0, NTILE, prepare, 0, unroll=4)
+
+    def prepare_more(i, _):
+        right[LINES + i] = node_rows(more_nodes, i // 8, i % 8)
+        sums[LINES + i] = jnp.zeros((8, 128), F32)
+        return 0
+
+    lax.fori_loop(0, MORE, prepare_more, 0, unroll=4)
     right[lines] = jnp.zeros((32, 128), BF16)
     sums[lines] = jnp.zeros((8, 128), F32)
 
@@ -310,21 +405,44 @@
             shift[c, i // 8, pl.ds(i % 8, 1), :] = v[c : c + 1, :]
         return 0
 
-    lax.fori_loop(0, lines, finish, 0, unroll=8)
-
-
-def pair_sums(ids, counts, motion, inverse_mass, raw, nodes):
+    lax.fori_loop(0, LINES, finish, 0, unroll=8)
+
+    def finish_more(i, _):
+        v = sums[LINES + i]
+        v = v + pltpu.roll(v, 5, 0)
+        for c in range(3):
+            more_shift[c, i // 8, pl.ds(i % 8, 1), :] = v[c : c + 1, :]
+        return 0
+
+    lax.fori_loop(0, MORE, finish_more, 0, unroll=8)
+    for c in range(3):
+        plane_edge[0, c] = nodes[c, 0]
+        plane_edge[1, c] = nodes[c, 0] + shift[c, 0]
+        for p in range(8):
+            row_edge[0, c, p : p + 1, :] = nodes[c, p, 0:1, :]
+            row_edge[1, c, p : p + 1, :] = nodes[c, p, 0:1, :] + shift[c, p, 0:1, :]
+
+
+LINES = 64
+MORE = 16
+
+
+def pair_sums(role, ids, more_ids, counts, motion, inverse_mass, raw, nodes, more_nodes):
     vmem = pl.BlockSpec(memory_space=pltpu.VMEM)
     smem = pl.BlockSpec(memory_space=pltpu.SMEM)
-    lines = nodes.shape[1] * 8
+    lines = LINES + MORE
+    units = 4 * LINES + 14 * 16 + 2 * BLOCK
     return pl.pallas_call(
         pair_kernel,
         out_shape=(
-            jax.ShapeDtypeStruct(nodes.shape, F32),
+            jax.ShapeDtypeStruct((3, 8, 8, 128), F32),
+            jax.ShapeDtypeStruct((3, 2, 8, 128), F32),
+            jax.ShapeDtypeStruct((2, 3, 8, 128), F32),
+            jax.ShapeDtypeStruct((2, 3, 8, 128), F32),
             jax.ShapeDtypeStruct((6, 8, 128), F32),
         ),
-        in_specs=[smem, smem, smem, smem, vmem, vmem],
-        out_specs=(vmem, vmem),
+        in_specs=[smem] * 6 + [vmem] * 3,
+        out_specs=(vmem,) * 5,
         scratch_shapes=[
             pltpu.VMEM((NTILE, 24, 128), F32),
             pltpu.VMEM((NTILE, 128, 64), BF16),
@@ -333,49 +451,150 @@
             pltpu.VMEM((NTILE, 16, 128), BF16),
             pltpu.VMEM((lines + 1, 32, 128), BF16),
             pltpu.VMEM((lines + 1, 8, 128), F32),
-            pltpu.SMEM((16 * lines + BLOCK,), jnp.int32),
-            pltpu.SMEM((16 * lines + BLOCK,), jnp.int32),
+            pltpu.SMEM((units,), jnp.int32),
+            pltpu.SMEM((units,), jnp.int32),
         ],
         name="pairs",
-    )(ids, counts, motion, inverse_mass, raw, nodes)
-
-
-def shifted(value, axis, by):
-    devices = lax.axis_size(axis)
-    pairs = [(i, i + by) for i in range(devices) if 0 <= i + by < devices]
-    return lax.ppermute(value, axis, pairs)
-
-
-def cell_volumes(lattice):
-    span_x = lattice.shape[-3] - 1
-    span_y = lattice.shape[-2] - 1
-    corners = {}
-    for shift_x in range(2):
-        for shift_y in range(2):
-            for shift_z in range(2):
-                sliced = lattice[..., shift_x : shift_x + span_x, shift_y : shift_y + span_y, :]
-                if shift_z == 1:
-                    sliced = jnp.concatenate([sliced[..., 1:], jnp.zeros_like(sliced[..., :1])], axis=-1)
-                corners[shift_x, shift_y, shift_z] = sliced
-    edge_x = 0.0
-    edge_y = 0.0
-    edge_z = 0.0
-    for first in range(2):
-        for second in range(2):
-            edge_x = edge_x + corners[1, first, second] - corners[0, first, second]
-            edge_y = edge_y + corners[first, 1, second] - corners[first, 0, second]
-            edge_z = edge_z + corners[first, second, 1] - corners[first, second, 0]
-    edge_x = 0.25 * edge_x
-    edge_y = 0.25 * edge_y
-    edge_z = 0.25 * edge_z
-    ex0, ex1, ex2 = (edge_x[..., 0, :, :, :], edge_x[..., 1, :, :, :], edge_x[..., 2, :, :, :])
-    ey0, ey1, ey2 = (edge_y[..., 0, :, :, :], edge_y[..., 1, :, :, :], edge_y[..., 2, :, :, :])
-    ez0, ez1, ez2 = (edge_z[..., 0, :, :, :], edge_z[..., 1, :, :, :], edge_z[..., 2, :, :, :])
-    return (
-        ex0 * (ey1 * ez2 - ey2 * ez1)
-        + ex1 * (ey2 * ez0 - ey0 * ez2)
-        + ex2 * (ey0 * ez1 - ey1 * ez0)
-    )
+    )(role, ids, more_ids, counts, motion, inverse_mass, raw, nodes, more_nodes)
+
+
+def volume_kernel(
+    nodes, shift, more_shift, plane_edge, row_edge, out_shift, volume, change, back, planes, rows, corners, send, recv
+):
+    x, y, z, core = place()
+    slab = lax.axis_index("slab")
+    heavy = is_heavy()
+    last = XS * ZS * CORES
+
+    def at(ds, dy):
+        return {"slab": (slab + ds + last) % last, "ctrl": (y + dy + YS) % YS}
+
+    barrier = pltpu.get_barrier_semaphore()
+    greet = [at(1, 0), at(-1, 0), at(0, 1), at(0, -1), at(1, 1), at(-1, -1)]
+    greet += [device(x + i, y, z, core) for i in (1, 2, 3)]
+    for target in greet:
+        pl.semaphore_signal(barrier, inc=1, device_id=target, device_id_type=MESH)
+    pl.semaphore_wait(barrier, len(greet))
+
+    def put(src, dst, slot, target):
+        return pltpu.make_async_remote_copy(
+            src_ref=src,
+            dst_ref=dst,
+            send_sem=send.at[slot],
+            recv_sem=recv.at[slot],
+            device_id=target,
+            device_id_type=MESH,
+        )
+
+    def give(h):
+        return pltpu.make_async_remote_copy(
+            src_ref=more_shift,
+            dst_ref=back.at[h],
+            send_sem=send.at[3],
+            recv_sem=recv.at[3 + h],
+            device_id=device(heavy_x(z), y, z, core),
+            device_id_type=MESH,
+        )
+
+    mine = (x - heavy_x(z) + 3) % XS
+
+    @pl.when(jnp.logical_not(heavy))
+    def _():
+        give(jnp.minimum(mine, 2)).start()
+
+    edges = [
+        put(plane_edge, corners, 2, at(-1, -1)),
+        put(plane_edge, planes, 0, at(-1, 0)),
+        put(row_edge, rows, 1, at(0, -1)),
+    ]
+    for copy in edges:
+        copy.start()
+    out_shift[...] = shift[...]
+
+    @pl.when(heavy)
+    def _():
+        row = iota((8, 128), 0)
+        for h in range(3):
+            give(h).wait_recv()
+            for c in range(3):
+                for i in range(2):
+                    p = 1 + 2 * h + i
+                    out_shift[c, p] = jnp.where(row == 0, shift[c, p], back[h, c, i])
+
+    @pl.when(jnp.logical_not(heavy))
+    def _():
+        give(jnp.minimum(mine, 2)).wait_send()
+
+    for copy in edges:
+        copy.wait()
+
+    bottom = iota((8, 128), 0) == 7
+
+    def faces(field, c, p):
+        if p < 8:
+            a = nodes[c, p]
+            if field:
+                a = a + out_shift[c, p]
+            edge = rows[field, c, p : p + 1, :]
+        else:
+            a = planes[field, c]
+            edge = corners[field, c, 0:1, :]
+        b = jnp.where(bottom, edge, pltpu.roll(a, 7, 0))
+        az = pltpu.roll(a, 127, 1)
+        bz = pltpu.roll(b, 127, 1)
+        near, far = a + b, az + bz
+        return near + far, (b + bz) - (a + az), far - near
+
+    row = iota((8, 128), 0) + y * 8
+    inside = jnp.logical_and(row < 31, iota((8, 128), 1) < 127)
+    held = {}
+    for p in range(9):
+        for field in range(2):
+            for c in range(3):
+                held[field, c, p % 2] = faces(field, c, p)
+        if p == 0:
+            continue
+        both = []
+        for field in range(2):
+            now = [held[field, c, p % 2] for c in range(3)]
+            before = [held[field, c, (p - 1) % 2] for c in range(3)]
+            ex = [0.25 * (n[0] - b[0]) for n, b in zip(now, before)]
+            ey = [0.25 * (n[1] + b[1]) for n, b in zip(now, before)]
+            ez = [0.25 * (n[2] + b[2]) for n, b in zip(now, before)]
+            both.append(
+                ex[0] * (ey[1] * ez[2] - ey[2] * ez[1])
+                + ex[1] * (ey[2] * ez[0] - ey[0] * ez[2])
+                + ex[2] * (ey[0] * ez[1] - ey[1] * ez[0])
+            )
+        ok = jnp.logical_and(inside, slab * 8 + p - 1 < 1023)
+        old, new = (jnp.where(ok, v, 0.0) for v in both)
+        volume[p - 1] = new
+        change[p - 1] = new - old
+
+
+def volumes(nodes, shift, more_shift, plane_edge, row_edge):
+    vmem = pl.BlockSpec(memory_space=pltpu.VMEM)
+    edge = pltpu.VMEM((2, 3, 8, 128), F32)
+    return pl.pallas_call(
+        volume_kernel,
+        out_shape=(
+            jax.ShapeDtypeStruct((3, 8, 8, 128), F32),
+            jax.ShapeDtypeStruct((8, 8, 128), F32),
+            jax.ShapeDtypeStruct((8, 8, 128), F32),
+        ),
+        in_specs=[vmem] * 5,
+        out_specs=(vmem,) * 3,
+        scratch_shapes=[
+            pltpu.VMEM((3, 3, 2, 8, 128), F32),
+            edge,
+            edge,
+            edge,
+            pltpu.SemaphoreType.DMA((4,)),
+            pltpu.SemaphoreType.DMA((6,)),
+        ],
+        compiler_params=pltpu.CompilerParams(collective_id=1, has_side_effects=True),
+        name="volumes",
+    )(nodes, shift, more_shift, plane_edge, row_edge)
 
 
 def local(
@@ -391,32 +610,23 @@
     tile_count,
 ):
     packed = jnp.concatenate([control_points, control_modes, jnp.zeros((3, 16), F32)], axis=0).reshape(3, 1, 128)
-    raw = gather(packed, face_pressure.reshape(1, -1), face_area, face_center)
-    node_shift, state = pair_sums(
-        tile_list, tile_count, motion, inverse_mass, raw.reshape(NTILE, 3, 8, 128), node_points
+    raw, more_nodes, more_ids = gather(
+        packed, face_pressure.reshape(1, -1), face_area, face_center, node_points, tile_list
     )
-    new_state = state[:, 0, 0]
-
-    plane_count = node_points.shape[1]
-    row_count = node_points.shape[2]
-    line_nodes = node_points.shape[3]
-    displaced = node_points + node_shift
-    stacked = jnp.stack([node_points, displaced])
-    next_plane = shifted(stacked[:, :, :1], "slab", -1)
-    widened = jnp.concatenate([stacked, next_plane], axis=2)
-    next_row = shifted(widened[:, :, :, :1], "ctrl", -1)
-    extended = jnp.concatenate([widened, next_row], axis=3)
-    volumes = cell_volumes(extended)
-    plane_total = plane_count * lax.axis_size("slab")
-    row_total = row_count * lax.axis_size("ctrl")
-    plane_ids = lax.axis_index("slab") * plane_count + jnp.arange(plane_count, dtype=jnp.int32)
-    row_ids = lax.axis_index("ctrl") * row_count + jnp.arange(row_count, dtype=jnp.int32)
-    depth_ids = jnp.arange(line_nodes, dtype=jnp.int32)
-    inside = (plane_ids < plane_total - 1)[:, None, None]
-    inside = inside & (row_ids < row_total - 1)[None, :, None]
-    inside = inside & (depth_ids < line_nodes - 1)[None, None, :]
-    volumes = jnp.where(inside[None], volumes, 0.0)
-    return (node_shift, volumes[1], volumes[1] - volumes[0], new_state)
+    role = is_heavy().astype(jnp.int32).reshape(1)
+    shift, more_shift, plane_edge, row_edge, state = pair_sums(
+        role,
+        tile_list,
+        more_ids,
+        tile_count,
+        motion,
+        inverse_mass,
+        raw.reshape(NTILE, 3, 8, 128),
+        node_points,
+        more_nodes,
+    )
+    node_shift, volume, change = volumes(node_points, shift, more_shift, plane_edge, row_edge)
+    return node_shift, volume, change, state[:, 0, 0]
 
 
 def solution(mesh):

time: 98.8 us -> 80 us (0.81)
  the two profiles are of different devices: /device:TPU:4 before, /device:TPU:1 now
where the time goes in v3:
time: 80 us; the launch traced here: 79.5 us
  Pallas kernels  73 us (91%)
  local copies, waits for them, and re-layouts  5.78 us (7%)
    pallas_call x1, Pallas kernels, gather(): pl.pallas_call(gather_kernel, out_shape=(jax.ShapeDtypeStruct((XS, ZS, 3,...  38.1 us
    pallas_call x1, Pallas kernels, pair_sums(): pl.pallas_call(pair_kernel, out_shape=(jax.ShapeDtypeStruct((3, 8, 8, 128...  28.1 us
    pallas_call x1, Pallas kernels, volumes(): pl.pallas_call(volume_kernel, out_shape=(jax.ShapeDtypeStruct((3, 8, 8, 1...  6.74 us
    unnamed x12, local copies, waits for them, and re-layouts  3.6 us

profile of v3, /device:TPU:1, one launch (start us, length us, event | category | flops | bytes accessed | tf_op | source)
XLA Modules:
  0.0 79.5 jit_solution(11763553583780051534)
XLA Ops:
  0.6 0.0 copy-start.3
  0.7 0.0 copy-start.2
  0.7 0.1 pad.2.clone
  0.7 0.6 copy-done.3
  1.3 0.1 copy.16
  1.4 0.0 copy-done.2
  1.4 0.1 maximum_maximum_fusion
  1.5 0.1 copy.17
  1.6 0.6 reshape.29.packed
  2.2 38.1 %gather.1 = (f32[4,16,3,8,1,128]{5,4,3,2,1,0:T(1,128)}, f32[3,2,8,128]{3,2,1,0:T(8,128)}, s32[2,8,16]{2,1,0:T(8,128)}) custom-call(f32[3,1,128]{2,1,0:T(1,128)} %reshape.29.packed, f32[1,4096]{1,0:T(1,128)} %bitcast.4, f32[3,4096]{1,0:T(4,128)} %area.1, f32[3,4096]{1,0:T(4,128)} %center.1, f32[3,8,8,128]{3,2,1,0:T(8,128)} %nodes.5, s32[8,8,16]{2,1,0:T(8,128)} %ids.3), custom_call_target="tpu_custom_call" | custom-call | tf_op jit(solution)/shard_map/gather/pallas_call | solution.py:198
  40.3 28.1 %pairs.1 = (f32[3,8,8,128]{3,2,1,0:T(8,128)}, f32[3,2,8,128]{3,2,1,0:T(8,128)}, f32[2,3,8,128]{3,2,1,0:T(8,128)}, f32[2,3,8,128]{3,2,1,0:T(8,128)}, f32[6,8,128]{2,1,0:T(8,128)}) custom-call(s32[1]{0:T(128)} %bitcast.role, s32[8,8,16]{2,1,0:T(8,128)} %ids.3, s32[2,8,16]{2,1,0:T(8,128)} %get-tuple-element.15.more_ids, s32[8,8]{1,0:T(8,128)} %counts.1, ...), custom_call_target="tpu_custom_call" | custom-call | tf_op jit(solution)/shard_map/pairs/pallas_call | solution.py:435
  68.5 6.7 %volumes.1 = (f32[3,8,8,128]{3,2,1,0:T(8,128)}, f32[8,8,128]{2,1,0:T(8,128)}, f32[8,8,128]{2,1,0:T(8,128)}) custom-call(f32[3,8,8,128]{3,2,1,0:T(8,128)} %nodes.5, f32[3,8,8,128]{3,2,1,0:T(8,128)} %get-tuple-element.18.shift, f32[3,2,8,128]{3,2,1,0:T(8,128)} %get-tuple-element.19.more_shift, f32[2,3,8,128]{3,2,1,0:T(8,128)} %get-tuple-element.20.plane_edge, ...), custom_call_target="tpu_custom_call" | custom-call | tf_op jit(solution)/shard_map/volumes/pallas_call | solution.py:578
  75.2 1.4 %slice_reduce_fusion = f32[6]{0:T(128)} fusion(f32[6,8,128]{2,1,0:T(8,128)} %get-tuple-element.25), kind=kLoop, calls=%fused_computation.1 | loop fusion | bytes 48 | tf_op jit(solution)/shard_map/slice | solution.py:629
  76.6 0.0 copy-start.1
  76.6 1.5 %copy.22 = f32[3,8,8,128]{3,2,1,0:T(8,128)} copy(f32[3,8,8,128]{3,2,1,0:T(8,128)} %get-tuple-element.30) | data formatting | bytes 196608
  78.1 0.0 copy-done.1
  78.2 0.0 copy-start
  78.2 0.6 copy.23
  78.8 0.2 copy-done
  78.9 0.6 copy.24
  (1 shorter events, 0.0 us)
Async XLA Ops:
  0.6 0.7 copy-start.3
  0.7 0.8 copy-start.2
  76.6 1.6 %copy-start.1 = (f32[8,8,128]{2,1,0:T(8,128)S(1)}, f32[8,8,128]{2,1,0:T(8,128)}, u32[]{:S(2)}) copy-start(f32[8,8,128]{2,1,0:T(8,128)} %get-tuple-element.31) | copy-start | bytes 98308
  78.2 0.8 copy-start

commit v4 on v3

--- a/solution.py
+++ b/solution.py
@@ -40,7 +40,26 @@
     return 2 - z // 8
 
 
-def gather_kernel(packed, pressure, area, center, nodes, ids, buf, more_nodes, more_ids, own, send, recv):
+def gather_kernel(
+    points,
+    modes,
+    pressure_hbm,
+    area_hbm,
+    center_hbm,
+    nodes,
+    ids,
+    buf,
+    more_nodes,
+    more_ids,
+    pressure,
+    area,
+    center,
+    pack,
+    own,
+    fetch,
+    send,
+    recv,
+):
     x, y, z, core = place()
     group = core * YS + y
     plane = [(i * core, i * (1 - core)) for i in range(1, 4)]
@@ -53,11 +72,30 @@
     for target in greet:
         pl.semaphore_signal(barrier, inc=1, device_id=target, device_id_type=MESH)
 
+    fetches = [
+        pltpu.make_async_copy(src, dst, fetch.at[i])
+        for i, (src, dst) in enumerate(((pressure_hbm, pressure), (area_hbm, area), (center_hbm, center)))
+    ]
+    for copy in fetches:
+        copy.start()
+
+    pack[...] = jnp.zeros((24, 128), F32)
+    pack[0:3, 0:16] = points[...]
+    pack[3:21, 0:16] = modes[...]
+    packed = []
+    for r in range(3):
+        v = pack[8 * r : 8 * r + 8, :]
+        for bit in (1, 2, 4):
+            v = jnp.where((iota((8, 128), 0) & bit) == 0, v, pltpu.roll(v, 16 * bit, 1))
+        packed.append(jnp.sum(v, axis=0, keepdims=True))
+
+    for copy in fetches:
+        copy.wait()
     force = jnp.zeros((3, 128), F32)
     moment = jnp.zeros((3, 128), F32)
-    for i in range(pressure.shape[1] // 128):
+    for i in range(pressure.shape[0]):
         at = pl.ds(i * 128, 128)
-        pushed = area[:, at] * pressure[:, at]
+        pushed = area[:, at] * pressure[i : i + 1, :]
         c = center[:, at]
         force = force + pushed
         moment = moment + jnp.concatenate(
@@ -125,8 +163,6 @@
 
     @pl.when(heavy)
     def _():
-        more_nodes[...] = jnp.zeros(more_nodes.shape, F32)
-        more_ids[...] = jnp.zeros(more_ids.shape, jnp.int32)
         for h in range(3):
             for copy in hand(h, 1 + 2 * h):
                 copy.start()
@@ -193,8 +229,9 @@
             copy.wait_recv()
 
 
-def gather(packed, pressure, area, center, nodes, ids):
+def gather(points, modes, pressure, area, center, nodes, ids):
     vmem = pl.BlockSpec(memory_space=pltpu.VMEM)
+    hbm = pl.BlockSpec(memory_space=pl.ANY)
     return pl.pallas_call(
         gather_kernel,
         out_shape=(
@@ -202,16 +239,26 @@
             jax.ShapeDtypeStruct((3, 2, 8, 128), F32),
             jax.ShapeDtypeStruct((2, 8, 16), jnp.int32),
         ),
-        in_specs=[vmem] * 6,
-        out_specs=(vmem, vmem, vmem),
+        in_specs=[vmem, vmem] + [hbm] * 5,
+        out_specs=(vmem, hbm, hbm),
         scratch_shapes=[
+            pltpu.VMEM(pressure.shape, F32),
+            pltpu.VMEM(area.shape, F32),
+            pltpu.VMEM(center.shape, F32),
+            pltpu.VMEM((24, 128), F32),
             pltpu.VMEM((3, 1, 128), F32),
+            pltpu.SemaphoreType.DMA((3,)),
             pltpu.SemaphoreType.DMA((28,)),
             pltpu.SemaphoreType.DMA((24,)),
         ],
-        compiler_params=pltpu.CompilerParams(collective_id=0, has_side_effects=True),
+        compiler_params=pltpu.CompilerParams(
+            collective_id=0, has_side_effects=True, vmem_limit_bytes=VMEM_LIMIT
+        ),
         name="gather",
-    )(packed, pressure, area, center, nodes, ids)
+    )(points, modes, pressure, area, center, nodes, ids)
+
+
+VMEM_LIMIT = 24 << 20
 
 
 def split3(value):
@@ -294,8 +341,7 @@
     mix_b,
     right,
     sums,
-    tile_of,
-    line_of,
+    unit_of,
 ):
     lines = LINES + MORE
     heavy = role[0] == 1
@@ -314,20 +360,20 @@
         line2 = jnp.where(heavy, kept, LINES + hp * 8 + hr)
         start1 = jnp.where(heavy, 8 * (t % 2), 0)
         keep = jnp.where(t < 44, 4, 0)
+        code1, code2 = line1 * NTILE, line2 * NTILE
         for e in range(4):
-            tile_of[n + e] = ids[line1 // 8, line1 % 8, start1 + e]
-            line_of[n + e] = line1
+            unit_of[n + e] = code1 + ids[line1, start1 + e]
         n = n + jnp.where(heavy, keep, counts[t // 8, t % 8])
+        quarter = 4 * (t % 4)
+        more_line = hp * 8 + hr
         for e in range(4):
-            tile_of[n + e] = jnp.where(heavy, ids[kept // 8, kept % 8, start1 + 4 + e], more_ids[hp, hr, 4 * (t % 4) + e])
-            line_of[n + e] = line2
+            unit_of[n + e] = code2 + jnp.where(heavy, ids[kept, start1 + 4 + e], more_ids[more_line, quarter + e])
         n = n + jnp.where(heavy, keep, jnp.where(t < 56, 4, 0))
         return total + v[2], n
 
     total, n = lax.fori_loop(0, NTILE, unpack, (jnp.zeros((8, 128), F32), 0), unroll=4)
     for e in range(BLOCK):
-        tile_of[n + e] = 0
-        line_of[n + e] = lines
+        unit_of[n + e] = lines * NTILE
     total = jnp.broadcast_to(total[5:6, :], (8, 128))
     for by in (16, 32, 64):
         total = total + pltpu.roll(total, by, 1)
@@ -335,7 +381,7 @@
     for k in range(6):
         load = jnp.broadcast_to(total[:, k : k + 1], (8, 128))
         acceleration = inverse_mass[k] * load + GRAVITY[k]
-        state[k, :, :] = motion[k] + TIME_STEP * acceleration
+        state[k] = (motion[k] + TIME_STEP * acceleration)[0, 0]
         rigid.append((TIME_STEP * motion[k] + 0.5 * TIME_STEP * TIME_STEP * acceleration)[0:3])
 
     wide = iota((128, 64), 1) < 32
@@ -375,8 +421,8 @@
     def block(g, _):
         for u in range(0, BLOCK, 2):
             i = g * BLOCK + u
-            t1, t2 = tile_of[i], tile_of[i + 1]
-            l1, l2 = line_of[i], line_of[i + 1]
+            t1, t2 = unit_of[i] % NTILE, unit_of[i + 1] % NTILE
+            l1, l2 = unit_of[i] // NTILE, unit_of[i + 1] // NTILE
             rhs = jnp.concatenate(
                 [jnp.concatenate([right[l1], gap], axis=1), jnp.concatenate([gap, right[l2]], axis=1)], axis=0
             )
@@ -439,10 +485,10 @@
             jax.ShapeDtypeStruct((3, 2, 8, 128), F32),
             jax.ShapeDtypeStruct((2, 3, 8, 128), F32),
             jax.ShapeDtypeStruct((2, 3, 8, 128), F32),
-            jax.ShapeDtypeStruct((6, 8, 128), F32),
+            jax.ShapeDtypeStruct((6,), F32),
         ),
         in_specs=[smem] * 6 + [vmem] * 3,
-        out_specs=(vmem,) * 5,
+        out_specs=(vmem,) * 4 + (smem,),
         scratch_shapes=[
             pltpu.VMEM((NTILE, 24, 128), F32),
             pltpu.VMEM((NTILE, 128, 64), BF16),
@@ -452,15 +498,13 @@
             pltpu.VMEM((lines + 1, 32, 128), BF16),
             pltpu.VMEM((lines + 1, 8, 128), F32),
             pltpu.SMEM((units,), jnp.int32),
-            pltpu.SMEM((units,), jnp.int32),
         ],
+        compiler_params=pltpu.CompilerParams(vmem_limit_bytes=VMEM_LIMIT),
         name="pairs",
     )(role, ids, more_ids, counts, motion, inverse_mass, raw, nodes, more_nodes)
 
 
-def volume_kernel(
-    nodes, shift, more_shift, plane_edge, row_edge, out_shift, volume, change, back, planes, rows, corners, send, recv
-):
+def exchange_kernel(more_shift, plane_edge, row_edge, back, planes, rows, corners, send, recv):
     x, y, z, core = place()
     slab = lax.axis_index("slab")
     heavy = is_heavy()
@@ -509,24 +553,48 @@
     ]
     for copy in edges:
         copy.start()
+
+    @pl.when(heavy)
+    def _():
+        for h in range(3):
+            give(h).wait_recv()
+
+    @pl.when(jnp.logical_not(heavy))
+    def _():
+        give(jnp.minimum(mine, 2)).wait_send()
+
+    for copy in edges:
+        copy.wait()
+
+
+def exchange(more_shift, plane_edge, row_edge):
+    hbm = pl.BlockSpec(memory_space=pl.ANY)
+    edge = jax.ShapeDtypeStruct((2, 3, 8, 128), F32)
+    return pl.pallas_call(
+        exchange_kernel,
+        out_shape=(jax.ShapeDtypeStruct((3, 3, 2, 8, 128), F32), edge, edge, edge),
+        in_specs=[hbm] * 3,
+        out_specs=(hbm,) * 4,
+        scratch_shapes=[pltpu.SemaphoreType.DMA((4,)), pltpu.SemaphoreType.DMA((6,))],
+        compiler_params=pltpu.CompilerParams(
+            collective_id=1, has_side_effects=True, vmem_limit_bytes=VMEM_LIMIT
+        ),
+        name="exchange",
+    )(more_shift, plane_edge, row_edge)
+
+
+def volume_kernel(role, nodes, shift, back, planes, rows, corners, out_shift, volume, change):
+    slab, y = role[1], role[2]
     out_shift[...] = shift[...]
 
-    @pl.when(heavy)
+    @pl.when(role[0] == 1)
     def _():
         row = iota((8, 128), 0)
         for h in range(3):
-            give(h).wait_recv()
             for c in range(3):
                 for i in range(2):
                     p = 1 + 2 * h + i
                     out_shift[c, p] = jnp.where(row == 0, shift[c, p], back[h, c, i])
-
-    @pl.when(jnp.logical_not(heavy))
-    def _():
-        give(jnp.minimum(mine, 2)).wait_send()
-
-    for copy in edges:
-        copy.wait()
 
     bottom = iota((8, 128), 0) == 7
 
@@ -572,9 +640,8 @@
         change[p - 1] = new - old
 
 
-def volumes(nodes, shift, more_shift, plane_edge, row_edge):
+def volumes(role, nodes, shift, back, planes, rows, corners):
     vmem = pl.BlockSpec(memory_space=pltpu.VMEM)
-    edge = pltpu.VMEM((2, 3, 8, 128), F32)
     return pl.pallas_call(
         volume_kernel,
         out_shape=(
@@ -582,19 +649,11 @@
             jax.ShapeDtypeStruct((8, 8, 128), F32),
             jax.ShapeDtypeStruct((8, 8, 128), F32),
         ),
-        in_specs=[vmem] * 5,
+        in_specs=[pl.BlockSpec(memory_space=pltpu.SMEM)] + [vmem] * 6,
         out_specs=(vmem,) * 3,
-        scratch_shapes=[
-            pltpu.VMEM((3, 3, 2, 8, 128), F32),
-            edge,
-            edge,
-            edge,
-            pltpu.SemaphoreType.DMA((4,)),
-            pltpu.SemaphoreType.DMA((6,)),
-        ],
-        compiler_params=pltpu.CompilerParams(collective_id=1, has_side_effects=True),
+        compiler_params=pltpu.CompilerParams(vmem_limit_bytes=VMEM_LIMIT),
         name="volumes",
-    )(nodes, shift, more_shift, plane_edge, row_edge)
+    )(role, nodes, shift, back, planes, rows, corners)
 
 
 def local(
@@ -609,15 +668,16 @@
     tile_list,
     tile_count,
 ):
-    packed = jnp.concatenate([control_points, control_modes, jnp.zeros((3, 16), F32)], axis=0).reshape(3, 1, 128)
     raw, more_nodes, more_ids = gather(
-        packed, face_pressure.reshape(1, -1), face_area, face_center, node_points, tile_list
+        control_points, control_modes, face_pressure.reshape(-1, 128), face_area, face_center, node_points, tile_list
     )
-    role = is_heavy().astype(jnp.int32).reshape(1)
-    shift, more_shift, plane_edge, row_edge, state = pair_sums(
+    role = jnp.stack(
+        [is_heavy().astype(jnp.int32), lax.axis_index("slab").astype(jnp.int32), lax.axis_index("ctrl").astype(jnp.int32)]
+    )
+    shift, more_shift, plane_edge, row_edge, new_state = pair_sums(
         role,
-        tile_list,
-        more_ids,
+        tile_list.reshape(LINES, 16),
+        more_ids.reshape(MORE, 16),
         tile_count,
         motion,
         inverse_mass,
@@ -625,8 +685,9 @@
         node_points,
         more_nodes,
     )
-    node_shift, volume, change = volumes(node_points, shift, more_shift, plane_edge, row_edge)
-    return node_shift, volume, change, state[:, 0, 0]
+    back, planes, rows, corners = exchange(more_shift, plane_edge, row_edge)
+    node_shift, volume, change = volumes(role, node_points, shift, back, planes, rows, corners)
+    return node_shift, volume, change, new_state
 
 
 def solution(mesh):

time: 80 us -> 75 us (0.938)
  Pallas kernels: 73 us -> 69.8 us
  local copies, waits for them, and re-layouts: 5.78 us -> 4.04 us
    pallas_call x1, Pallas kernels: 6.74 us -> 1.39 us  [volumes(): pl.pallas_call(volume_kernel, out_shape=(jax.ShapeDtypeStruct((3, 8, 8, 1...]
    pallas_call x0 -> x1, Pallas kernels: none -> 5.02 us  [exchange(): pl.pallas_call(exchange_kernel, out_shape=(jax.ShapeDtypeStruct((3, 3, 2,...]
    pallas_call x1, Pallas kernels: 38.1 us -> 36.5 us  [gather(): pl.pallas_call(gather_kernel, out_shape=(jax.ShapeDtypeStruct((XS, ZS, 3,...]
    slice x1 -> x0, local copies, waits for them, and re-layouts: 1.38 us -> none  [local(): return (node_shift, volume, change, state[:, 0, 0])]
    pallas_call x1, Pallas kernels: 28.1 us -> 26.8 us  [pair_sums(): pl.pallas_call(pair_kernel, out_shape=(jax.ShapeDtypeStruct((3, 8, 8, 128...]
    unnamed x12 -> x21, local copies, waits for them, and re-layouts: 3.6 us -> 4.04 us
where the time goes in v4:
time: 75 us; the launch traced here: 74.6 us
  Pallas kernels  69.8 us (93%)
  local copies, waits for them, and re-layouts  4.04 us (5%)
    pallas_call x1, Pallas kernels, gather(): pl.pallas_call(gather_kernel, out_shape=(jax.ShapeDtypeStruct((XS, ZS, 3,...  36.5 us
    pallas_call x1, Pallas kernels, pair_sums(): pl.pallas_call(pair_kernel, out_shape=(jax.ShapeDtypeStruct((3, 8, 8, 128...  26.8 us
    pallas_call x1, Pallas kernels, exchange(): pl.pallas_call(exchange_kernel, out_shape=(jax.ShapeDtypeStruct((3, 3, 2,...  5.02 us
    unnamed x21, local copies, waits for them, and re-layouts  4.04 us

profile of v4, /device:TPU:1, one launch (start us, length us, event | category | flops | bytes accessed | tf_op | source)
XLA Modules:
  0.0 74.6 jit_solution(10723788712567816639)
XLA Ops:
  0.6 0.0 copy-start.2
  0.6 0.0 copy-start.5
  0.7 0.1 pad_add_fusion.role
  0.7 0.0 copy-start.7
  0.7 0.8 %copy.14.modes = f32[18,16]{1,0:T(8,128)S(1)} copy(f32[18,16]{0,1:T(8,128)} %param.16) | data formatting | bytes 2304 | tf_op args[6]
  1.5 0.0 copy-done.2
  1.5 0.0 copy-done.5
  1.5 0.0 copy-done.7
  1.5 0.0 copy-start
  1.6 0.9 %copy-done = f32[3,8,8,128]{3,2,1,0:T(8,128)S(1)} copy-done((f32[3,8,8,128]{3,2,1,0:T(8,128)S(1)}, f32[3,8,8,128]{3,2,1,0:T(8,128)}, u32[]{:S(2)}) %copy-start) | copy-done | bytes 98328
  2.4 0.0 copy-start.3
  2.4 0.8 %copy-done.3 = f32[3,4096]{1,0:T(4,128)S(1)} copy-done((f32[3,4096]{1,0:T(4,128)S(1)}, f32[3,4096]{1,0:T(4,128)}, u32[]{:S(2)}) %copy-start.3) | copy-done | bytes 49176
  3.3 0.0 copy-start.4
  3.3 0.8 %copy-done.4 = f32[3,4096]{1,0:T(4,128)S(1)} copy-done((f32[3,4096]{1,0:T(4,128)S(1)}, f32[3,4096]{1,0:T(4,128)}, u32[]{:S(2)}) %copy-start.4) | copy-done | bytes 49176
  4.1 0.0 copy-start.1
  4.1 36.5 %gather.1 = (f32[4,16,3,8,1,128]{5,4,3,2,1,0:T(1,128)S(1)}, f32[3,2,8,128]{3,2,1,0:T(8,128)S(1)}, s32[2,8,16]{2,1,0:T(8,128)S(1)}) custom-call(f32[3,16]{1,0:T(4,128)S(1)} %copy-done.7, f32[18,16]{1,0:T(8,128)S(1)} %copy.14.modes, f32[32,128]{1,0:T(8,128)S(1)} %bitcast.9, f32[3,4096]{1,0:T(4,128)S(1)} %copy-done.3, f32[3,4096]{1,0:T(4,128)S(1)} %copy-done.4, ...), custom_call_target="tpu_custom_call" | custom-call | tf_op jit(solution)/shard_map/gather/pallas_call | solution.py:235
  40.7 0.0 copy-start.6
  40.7 0.0 copy-start.8
  40.7 0.0 copy-start.9
  40.7 0.0 copy-done.1
  40.7 0.6 copy-done.6
  41.4 0.0 copy-done.8
  41.4 0.0 copy-done.9
  41.4 26.8 %pairs.1 = (f32[3,8,8,128]{3,2,1,0:T(8,128)S(1)}, f32[3,2,8,128]{3,2,1,0:T(8,128)S(1)}, f32[2,3,8,128]{3,2,1,0:T(8,128)S(1)}, f32[2,3,8,128]{3,2,1,0:T(8,128)S(1)}, f32[6]{0:T(128)}) custom-call(s32[3]{0:T(128)S(1)} %pad_add_fusion.role, s32[64,16]{1,0:T(8,128)S(1)} %bitcast.8, s32[16,16]{1,0:T(8,128)S(1)} %bitcast.10, s32[8,8]{1,0:T(8,128)S(1)} %copy-done.6, ...), custom_call_target="tpu_custom_call" | custom-call | tf_op jit(solution)/shard_map/pairs/pallas_call | solution.py:481
  68.2 5.0 %exchange.1 = (f32[3,3,2,8,128]{4,3,2,1,0:T(8,128)S(1)}, f32[2,3,8,128]{3,2,1,0:T(8,128)S(1)}, f32[2,3,8,128]{3,2,1,0:T(8,128)S(1)}, f32[2,3,8,128]{3,2,1,0:T(8,128)S(1)}) custom-call(f32[3,2,8,128]{3,2,1,0:T(8,128)S(1)} %get-tuple-element.23.more_shift, f32[2,3,8,128]{3,2,1,0:T(8,128)S(1)} %get-tuple-element.24.plane_edge, ...), custom_call_target="tpu_custom_call" | custom-call | tf_op jit(solution)/shard_map/exchange/pallas_call | solution.py:573
  73.2 1.4 %volumes.1 = (f32[3,8,8,128]{3,2,1,0:T(8,128)}, f32[8,8,128]{2,1,0:T(8,128)}, f32[8,8,128]{2,1,0:T(8,128)}) custom-call(s32[3]{0:T(128)S(1)} %pad_add_fusion.role, f32[3,8,8,128]{3,2,1,0:T(8,128)S(1)} %copy-done.1, f32[3,8,8,128]{3,2,1,0:T(8,128)S(1)} %get-tuple-element.22.shift, f32[3,3,2,8,128]{4,3,2,1,0:T(8,128)S(1)} %get-tuple-element.26.back, ...), custom_call_target="tpu_custom_call" | custom-call | tf_op jit(solution)/shard_map/volumes/pallas_call | solution.py:645
Async XLA Ops:
  0.6 0.9 %copy-start.2 = (s32[8,8,16]{2,1,0:T(8,128)S(1)}, s32[8,8,16]{2,1,0:T(8,128)}, u32[]{:S(2)}) copy-start(s32[8,8,16]{2,1,0:T(8,128)} %ids.1) | copy-start | bytes 12292
  0.6 0.9 %copy-start.5 = (f32[4096]{0:T(1024)S(1)}, f32[4096]{0:T(1024)}, u32[]{:S(2)}) copy-start(f32[4096]{0:T(1024)} %param.10) | copy-start | bytes 49156
  0.7 0.8 %copy-start.7 = (f32[3,16]{1,0:T(4,128)S(1)}, f32[3,16]{1,0:T(4,128)}, u32[]{:S(2)}) copy-start(f32[3,16]{1,0:T(4,128)} %points.1) | copy-start | bytes 580
  1.5 0.9 %copy-start = (f32[3,8,8,128]{3,2,1,0:T(8,128)S(1)}, f32[3,8,8,128]{3,2,1,0:T(8,128)}, u32[]{:S(2)}) copy-start(f32[3,8,8,128]{3,2,1,0:T(8,128)} %nodes.5) | copy-start | bytes 294916
  2.4 0.8 %copy-start.3 = (f32[3,4096]{1,0:T(4,128)S(1)}, f32[3,4096]{1,0:T(4,128)}, u32[]{:S(2)}) copy-start(f32[3,4096]{1,0:T(4,128)} %area_hbm.1) | copy-start | bytes 147460
  3.3 0.8 %copy-start.4 = (f32[3,4096]{1,0:T(4,128)S(1)}, f32[3,4096]{1,0:T(4,128)}, u32[]{:S(2)}) copy-start(f32[3,4096]{1,0:T(4,128)} %center_hbm.1) | copy-start | bytes 147460
  4.1 36.6 %copy-start.1 = (f32[3,8,8,128]{3,2,1,0:T(8,128)S(1)}, f32[3,8,8,128]{3,2,1,0:T(8,128)}, u32[]{:S(2)}) copy-start(f32[3,8,8,128]{3,2,1,0:T(8,128)} %nodes.5) | copy-start | bytes 294916
  40.7 0.7 copy-start.6
  40.7 0.7 copy-start.8
  40.7 0.7 copy-start.9

commit v5 on v4

--- a/solution.py
+++ b/solution.py
@@ -41,8 +41,8 @@
 
 
 def gather_kernel(
-    points,
-    modes,
+    points_hbm,
+    modes_hbm,
     pressure_hbm,
     area_hbm,
     center_hbm,
@@ -51,10 +51,13 @@
     buf,
     more_nodes,
     more_ids,
+    points,
+    modes,
     pressure,
     area,
     center,
     pack,
+    turn,
     own,
     fetch,
     send,
@@ -65,23 +68,28 @@
     plane = [(i * core, i * (1 - core)) for i in range(1, 4)]
     turned = [(i * (1 - core), i * core) for i in range(1, 4)]
 
+    sources = (points_hbm, modes_hbm, pressure_hbm, area_hbm, center_hbm)
+    fetches = [
+        pltpu.make_async_copy(src, dst, fetch.at[i])
+        for i, (src, dst) in enumerate(zip(sources, (points, modes, pressure, area, center)))
+    ]
+    for copy in fetches:
+        copy.start()
+
     barrier = pltpu.get_barrier_semaphore()
-    greet = [device(x, y, z + d, core) for d in (1, -1, 2, -2, 3, -3, 4, -4)]
+    greet = [device(x, y, z + d, core) for d in (4, -4, 3, -3, 2, -2, 1, -1)]
     greet += [device(x + dx, y + dy, z, core) for dx, dy in plane + turned]
     greet += [device(x, y, z, 1 - core)]
     for target in greet:
         pl.semaphore_signal(barrier, inc=1, device_id=target, device_id_type=MESH)
 
-    fetches = [
-        pltpu.make_async_copy(src, dst, fetch.at[i])
-        for i, (src, dst) in enumerate(((pressure_hbm, pressure), (area_hbm, area), (center_hbm, center)))
-    ]
-    for copy in fetches:
-        copy.start()
-
+    for copy in fetches[:2]:
+        copy.wait()
     pack[...] = jnp.zeros((24, 128), F32)
     pack[0:3, 0:16] = points[...]
-    pack[3:21, 0:16] = modes[...]
+    turn[...] = jnp.zeros((16, 128), F32)
+    turn[:, 0:18] = modes[...]
+    pack[3:21, 0:16] = jnp.transpose(turn[...], (1, 0))[0:18]
     packed = []
     for r in range(3):
         v = pack[8 * r : 8 * r + 8, :]
@@ -89,7 +97,7 @@
             v = jnp.where((iota((8, 128), 0) & bit) == 0, v, pltpu.roll(v, 16 * bit, 1))
         packed.append(jnp.sum(v, axis=0, keepdims=True))
 
-    for copy in fetches:
+    for copy in fetches[2:]:
         copy.wait()
     force = jnp.zeros((3, 128), F32)
     moment = jnp.zeros((3, 128), F32)
@@ -114,7 +122,7 @@
     own[1] = packed[1]
     own[2] = packed[2] + loads
     for r in range(3):
-        buf[x, z, r, group] = own[r]
+        buf[x, 4, r, group] = own[r]
 
     pl.semaphore_wait(barrier, len(greet))
 
@@ -130,8 +138,8 @@
                 pltpu.make_async_remote_copy(
                     src_ref=src,
                     dst_ref=dst,
-                    send_sem=send.at[22 + 2 * h + i],
-                    recv_sem=recv.at[22 + i],
+                    send_sem=send.at[29 + 2 * h + i],
+                    recv_sem=recv.at[29 + i],
                     device_id=target,
                     device_id_type=MESH,
                 )
@@ -153,13 +161,13 @@
         pending.append(copy)
         return copy
 
-    def block(zz):
-        return buf.at[x, zz % ZS, :, group]
+    def slot(j):
+        return buf.at[x, j, :, group]
 
     near = {}
     for d in (4, 3, 2, 1):
-        near[d] = put(own, block(z), d - 1, device(x, y, z + d, core))
-        near[-d] = put(own, block(z), d + 3, device(x, y, z - d, core))
+        near[d] = put(own, slot(4 - d), d - 1, device(x, y, z + d, core))
+        near[-d] = put(own, slot(4 + d), d + 3, device(x, y, z - d, core))
 
     @pl.when(heavy)
     def _():
@@ -170,50 +178,63 @@
     far = []
     for d in (1, 2, 3, 4):
         near[d].wait_recv()
-        far.append(put(block(z - d), block(z - d), d + 7, device(x, y, z + 4, core)))
+        far.append(put(slot(4 - d), slot(16 - d), d + 7, device(x, y, z + 4, core)))
         near[-d].wait_recv()
         if d < 4:
-            far.append(put(block(z + d), block(z + d), d + 11, device(x, y, z - 4, core)))
+            far.append(put(slot(4 + d), slot(8 + d), d + 11, device(x, y, z - 4, core)))
+
+    halves = (pl.ds(0, 9), pl.ds(9, 7))
+
+    def first(part):
+        ref = buf.at[x, halves[part], :, group]
+        return [
+            put(ref, ref, 15 + 3 * part + i, device(x + dx, y + dy, z, core)) for i, (dx, dy) in enumerate(plane)
+        ]
+
+    def second(part, start):
+        for i, (dx, dy) in enumerate(turned):
+            target = device(x + dx, y + dy, z, core)
+
+            def make(ref, i=i, target=target):
+                return pltpu.make_async_remote_copy(
+                    src_ref=ref,
+                    dst_ref=ref,
+                    send_sem=send.at[21 + 3 * part + i],
+                    recv_sem=recv.at[21 + 3 * part + i],
+                    device_id=target,
+                    device_id_type=MESH,
+                )
+
+            @pl.when(core == 0)
+            def _():
+                copy = make(buf.at[x, halves[part], :, pl.ds(0, YS)])
+                copy.start() if start else copy.wait()
+
+            @pl.when(core == 1)
+            def _():
+                copy = make(buf.at[:, halves[part], :, group])
+                copy.start() if start else copy.wait()
+
+    def across(part):
+        ref = buf.at[:, halves[part], :, pl.ds(core * YS, YS)]
+        return put(ref, ref, 27 + part, device(x, y, z, 1 - core))
+
+    first_near = first(0)
+    for copy in first_near:
+        copy.wait_recv()
+    second(0, True)
     for copy in far:
         copy.wait_recv()
-
-    first = [
-        put(buf.at[x, :, :, group], buf.at[x, :, :, group], 15 + i, device(x + dx, y + dy, z, core))
-        for i, (dx, dy) in enumerate(plane)
-    ]
-    for copy in first:
+    first_far = first(1)
+    for copy in first_far:
         copy.wait_recv()
-
-    def cross(i, dx, dy, start):
-        target = device(x + dx, y + dy, z, core)
-
-        def make(ref):
-            return pltpu.make_async_remote_copy(
-                src_ref=ref,
-                dst_ref=ref,
-                send_sem=send.at[18 + i],
-                recv_sem=recv.at[18 + i],
-                device_id=target,
-                device_id_type=MESH,
-            )
-
-        @pl.when(core == 0)
-        def _():
-            copy = make(buf.at[x, :, :, pl.ds(0, YS)])
-            copy.start() if start else copy.wait()
-
-        @pl.when(core == 1)
-        def _():
-            copy = make(buf.at[:, :, :, group])
-            copy.start() if start else copy.wait()
-
-    for i, (dx, dy) in enumerate(turned):
-        cross(i, dx, dy, True)
-    for i, (dx, dy) in enumerate(turned):
-        cross(i, dx, dy, False)
-
-    half = buf.at[:, :, :, pl.ds(core * YS, YS)]
-    put(half, half, 21, device(x, y, z, 1 - core)).wait_recv()
+    second(1, True)
+    second(0, False)
+    across_near = across(0)
+    second(1, False)
+    across_far = across(1)
+    across_near.wait_recv()
+    across_far.wait_recv()
     for copy in pending:
         copy.wait_send()
 
@@ -239,23 +260,26 @@
             jax.ShapeDtypeStruct((3, 2, 8, 128), F32),
             jax.ShapeDtypeStruct((2, 8, 16), jnp.int32),
         ),
-        in_specs=[vmem, vmem] + [hbm] * 5,
+        in_specs=[pl.BlockSpec(memory_space=pltpu.HBM)] * 7,
         out_specs=(vmem, hbm, hbm),
         scratch_shapes=[
+            pltpu.VMEM(points.shape, F32),
+            pltpu.VMEM(modes.shape, F32),
             pltpu.VMEM(pressure.shape, F32),
             pltpu.VMEM(area.shape, F32),
             pltpu.VMEM(center.shape, F32),
             pltpu.VMEM((24, 128), F32),
+            pltpu.VMEM((16, 128), F32),
             pltpu.VMEM((3, 1, 128), F32),
-            pltpu.SemaphoreType.DMA((3,)),
-            pltpu.SemaphoreType.DMA((28,)),
-            pltpu.SemaphoreType.DMA((24,)),
+            pltpu.SemaphoreType.DMA((5,)),
+            pltpu.SemaphoreType.DMA((35,)),
+            pltpu.SemaphoreType.DMA((31,)),
         ],
         compiler_params=pltpu.CompilerParams(
             collective_id=0, has_side_effects=True, vmem_limit_bytes=VMEM_LIMIT
         ),
         name="gather",
-    )(points, modes, pressure, area, center, nodes, ids)
+    )(*(pltpu.with_memory_space_constraint(v, pltpu.HBM) for v in (points, modes, pressure, area, center, nodes, ids)))
 
 
 VMEM_LIMIT = 24 << 20
@@ -321,11 +345,11 @@
 
 def pair_kernel(
     role,
-    ids,
-    more_ids,
-    counts,
-    motion,
-    inverse_mass,
+    ids_hbm,
+    more_ids_hbm,
+    counts_hbm,
+    motion_hbm,
+    inverse_mass_hbm,
     raw,
     nodes,
     more_nodes,
@@ -342,38 +366,36 @@
     right,
     sums,
     unit_of,
+    ids,
+    more_ids,
+    counts,
+    motion,
+    inverse_mass,
+    fetch,
 ):
     lines = LINES + MORE
-    heavy = role[0] == 1
+    sources = (ids_hbm, more_ids_hbm, counts_hbm, motion_hbm, inverse_mass_hbm)
+    fetches = [
+        pltpu.make_async_copy(src, dst, fetch.at[i])
+        for i, (src, dst) in enumerate(zip(sources, (ids, more_ids, counts, motion, inverse_mass)))
+    ]
+    for copy in fetches:
+        copy.start()
+    heavy = role[0]
+    light = 1 - heavy
+    z = (role[1] >> 1) & (ZS - 1)
     sub = iota((8, 128), 0)
 
-    def unpack(t, carry):
-        total, n = carry
-        v = [regroup(raw[t, r]) for r in range(3)]
+    def unpack(t, total):
+        at = (t & ~(ZS - 1)) | ((t - z + 4) & (ZS - 1))
+        v = [regroup(raw[at, r]) for r in range(3)]
         for r in range(3):
             feats[t, pl.ds(8 * r, 8), :] = v[r]
-        i = t // 2
-        kept = jnp.minimum(jnp.where(i < 8, i, jnp.where(i < 15, (i - 7) * 8, i + 42)), LINES - 1)
-        q = t // 4
-        hp, hr = jnp.minimum(q // 7, 1), q % 7 + 1
-        line1 = jnp.where(heavy, kept, t)
-        line2 = jnp.where(heavy, kept, LINES + hp * 8 + hr)
-        start1 = jnp.where(heavy, 8 * (t % 2), 0)
-        keep = jnp.where(t < 44, 4, 0)
-        code1, code2 = line1 * NTILE, line2 * NTILE
-        for e in range(4):
-            unit_of[n + e] = code1 + ids[line1, start1 + e]
-        n = n + jnp.where(heavy, keep, counts[t // 8, t % 8])
-        quarter = 4 * (t % 4)
-        more_line = hp * 8 + hr
-        for e in range(4):
-            unit_of[n + e] = code2 + jnp.where(heavy, ids[kept, start1 + 4 + e], more_ids[more_line, quarter + e])
-        n = n + jnp.where(heavy, keep, jnp.where(t < 56, 4, 0))
-        return total + v[2], n
-
-    total, n = lax.fori_loop(0, NTILE, unpack, (jnp.zeros((8, 128), F32), 0), unroll=4)
-    for e in range(BLOCK):
-        unit_of[n + e] = lines * NTILE
+        return total + v[2]
+
+    total = lax.fori_loop(0, NTILE, unpack, jnp.zeros((8, 128), F32), unroll=4)
+    for copy in fetches:
+        copy.wait()
     total = jnp.broadcast_to(total[5:6, :], (8, 128))
     for by in (16, 32, 64):
         total = total + pltpu.roll(total, by, 1)
@@ -384,31 +406,55 @@
         state[k] = (motion[k] + TIME_STEP * acceleration)[0, 0]
         rigid.append((TIME_STEP * motion[k] + 0.5 * TIME_STEP * TIME_STEP * acceleration)[0:3])
 
-    wide = iota((128, 64), 1) < 32
-
-    def prepare(t, _):
-        parts = control_rows(feats[t, 0:8, :])
-        columns = jnp.transpose(jnp.concatenate(parts + parts, axis=0), (1, 0))
-        left_a[t] = jnp.where(wide, columns, 0.0).astype(BF16)
-        left_b[t] = jnp.where(wide, 0.0, columns).astype(BF16)
-        c = jnp.zeros((3, 128), F32)
-        for k in range(6):
-            c = c + rigid[k] * feats[t, 3 + 3 * k : 6 + 3 * k, :]
-        c = c * (1.0 / 256.0)
-        c = jnp.concatenate([c, c, jnp.zeros((2, 128), F32)], axis=0)
-        c_hi = c.astype(BF16).astype(F32)
-        c = jnp.where(sub < 3, c_hi, c - c_hi)
-        zero = jnp.zeros((8, 128), F32)
-        mix_a[t] = jnp.concatenate([c, zero], axis=0).astype(BF16)
-        mix_b[t] = jnp.concatenate([zero, c], axis=0).astype(BF16)
-        right[t] = node_rows(nodes, t // 8, t % 8)
-        sums[t] = zero
-        return 0
-
-    lax.fori_loop(0, NTILE, prepare, 0, unroll=4)
+    first_half = jnp.where(iota((128, 64), 1) < 32, 1.0, 0.0).astype(BF16)
+
+    def prepare(i, n):
+        q = jnp.minimum(i, 13)
+        more_line = q + jnp.where(q < 7, 1, 2)
+        more_code = (LINES + more_line) << 6
+        more_count = jnp.where(i < 14, 4 * light, 0)
+        for u in range(4):
+            t = 4 * i + u
+            for e in range(4):
+                unit_of[n + e] = (t << 6) + ids[t, e]
+            n = n + light * counts[i >> 1, ((i & 1) << 2) + u]
+            for e in range(4):
+                unit_of[n + e] = more_code + more_ids[more_line, 4 * u + e]
+            n = n + more_count
+
+            parts = control_rows(feats[t, 0:8, :])
+            columns = jnp.transpose(jnp.concatenate(parts + parts, axis=0), (1, 0)).astype(BF16)
+            left = columns * first_half
+            left_a[t] = left
+            left_b[t] = columns - left
+            c = jnp.zeros((3, 128), F32)
+            for k in range(6):
+                c = c + rigid[k] * feats[t, 3 + 3 * k : 6 + 3 * k, :]
+            c = c * (1.0 / 256.0)
+            c = jnp.concatenate([c, c, jnp.zeros((2, 128), F32)], axis=0)
+            c_hi = c.astype(BF16).astype(F32)
+            c = jnp.where(sub < 3, c_hi, c - c_hi)
+            zero = jnp.zeros((8, 128), F32)
+            mix_a[t] = jnp.concatenate([c, zero], axis=0).astype(BF16)
+            mix_b[t] = jnp.concatenate([zero, c], axis=0).astype(BF16)
+            right[t] = node_rows(nodes, i >> 1, ((i & 1) << 2) + u)
+            sums[t] = zero
+        return n
+
+    n = lax.fori_loop(0, NTILE // 4, prepare, jnp.int32(0))
+
+    def keep(i, n):
+        line = jnp.where(i < 8, i, jnp.where(i < 15, (i - 7) << 3, i + 42))
+        for e in range(16):
+            unit_of[n + e] = (line << 6) + ids[line, e]
+        return n + 16
+
+    n = lax.fori_loop(0, 22 * heavy, keep, n)
+    for e in range(BLOCK):
+        unit_of[n + e] = lines * NTILE
 
     def prepare_more(i, _):
-        right[LINES + i] = node_rows(more_nodes, i // 8, i % 8)
+        right[LINES + i] = node_rows(more_nodes, i >> 3, i & 7)
         sums[LINES + i] = jnp.zeros((8, 128), F32)
         return 0
 
@@ -421,8 +467,9 @@
     def block(g, _):
         for u in range(0, BLOCK, 2):
             i = g * BLOCK + u
-            t1, t2 = unit_of[i] % NTILE, unit_of[i + 1] % NTILE
-            l1, l2 = unit_of[i] // NTILE, unit_of[i + 1] // NTILE
+            c1, c2 = unit_of[i], unit_of[i + 1]
+            t1, t2 = c1 & (NTILE - 1), c2 & (NTILE - 1)
+            l1, l2 = c1 >> 6, c2 >> 6
             rhs = jnp.concatenate(
                 [jnp.concatenate([right[l1], gap], axis=1), jnp.concatenate([gap, right[l2]], axis=1)], axis=0
             )
@@ -442,25 +489,16 @@
             sums[l2] += out[8:16, 128:256]
         return 0
 
-    lax.fori_loop(0, (n + BLOCK - 1) // BLOCK, block, 0)
-
-    def finish(i, _):
+    lax.fori_loop(0, (n + BLOCK - 1) >> 5, block, 0)
+
+    for i in range(lines):
         v = sums[i]
         v = v + pltpu.roll(v, 5, 0)
         for c in range(3):
-            shift[c, i // 8, pl.ds(i % 8, 1), :] = v[c : c + 1, :]
-        return 0
-
-    lax.fori_loop(0, LINES, finish, 0, unroll=8)
-
-    def finish_more(i, _):
-        v = sums[LINES + i]
-        v = v + pltpu.roll(v, 5, 0)
-        for c in range(3):
-            more_shift[c, i // 8, pl.ds(i % 8, 1), :] = v[c : c + 1, :]
-        return 0
-
-    lax.fori_loop(0, MORE, finish_more, 0, unroll=8)
+            if i < LINES:
+                shift[c, i // 8, i % 8 : i % 8 + 1, :] = v[c : c + 1, :]
+            else:
+                more_shift[c, i // 8 - 8, i % 8 : i % 8 + 1, :] = v[c : c + 1, :]
     for c in range(3):
         plane_edge[0, c] = nodes[c, 0]
         plane_edge[1, c] = nodes[c, 0] + shift[c, 0]
@@ -487,7 +525,7 @@
             jax.ShapeDtypeStruct((2, 3, 8, 128), F32),
             jax.ShapeDtypeStruct((6,), F32),
         ),
-        in_specs=[smem] * 6 + [vmem] * 3,
+        in_specs=[smem] + [pl.BlockSpec(memory_space=pltpu.HBM)] * 5 + [vmem] * 3,
         out_specs=(vmem,) * 4 + (smem,),
         scratch_shapes=[
             pltpu.VMEM((NTILE, 24, 128), F32),
@@ -498,6 +536,12 @@
             pltpu.VMEM((lines + 1, 32, 128), BF16),
             pltpu.VMEM((lines + 1, 8, 128), F32),
             pltpu.SMEM((units,), jnp.int32),
+            pltpu.SMEM((LINES, 16), jnp.int32),
+            pltpu.SMEM((MORE, 16), jnp.int32),
+            pltpu.SMEM((8, 8), jnp.int32),
+            pltpu.SMEM((6,), F32),
+            pltpu.SMEM((6,), F32),
+            pltpu.SemaphoreType.DMA((5,)),
         ],
         compiler_params=pltpu.CompilerParams(vmem_limit_bytes=VMEM_LIMIT),
         name="pairs",
@@ -669,7 +713,7 @@
     tile_count,
 ):
     raw, more_nodes, more_ids = gather(
-        control_points, control_modes, face_pressure.reshape(-1, 128), face_area, face_center, node_points, tile_list
+        control_points, control_modes.T, face_pressure.reshape(-1, 128), face_area, face_center, node_points, tile_list
     )
     role = jnp.stack(
         [is_heavy().astype(jnp.int32), lax.axis_index("slab").astype(jnp.int32), lax.axis_index("ctrl").astype(jnp.int32)]
@@ -678,9 +722,7 @@
         role,
         tile_list.reshape(LINES, 16),
         more_ids.reshape(MORE, 16),
-        tile_count,
-        motion,
-        inverse_mass,
+        *(pltpu.with_memory_space_constraint(v, pltpu.HBM) for v in (tile_count, motion, inverse_mass)),
         raw.reshape(NTILE, 3, 8, 128),
         node_points,
         more_nodes,

time: 75 us -> 63.3 us (0.84)
  Pallas kernels: 69.8 us -> 62.1 us
  local copies, waits for them, and re-layouts: 4.04 us -> 0.01 us
    pallas_call x1, Pallas kernels: 26.8 us -> 20.5 us  [pair_sums(): pl.pallas_call(pair_kernel, out_shape=(jax.ShapeDtypeStruct((3, 8, 8, 128...]
    unnamed x21 -> x4, local copies, waits for them, and re-layouts: 4.04 us -> 0.01 us
    pallas_call x1, Pallas kernels: 36.5 us -> 34.5 us  [gather(): pl.pallas_call(gather_kernel, out_shape=(jax.ShapeDtypeStruct((XS, ZS, 3,...]
where the time goes in v5:
time: 63.3 us; the launch traced here: 62.9 us
  Pallas kernels  62.1 us (98%)
  between operations  0.68 us (1%)
    pallas_call x1, Pallas kernels, gather(): pl.pallas_call(gather_kernel, out_shape=(jax.ShapeDtypeStruct((XS, ZS, 3,...  34.5 us
    pallas_call x1, Pallas kernels, pair_sums(): pl.pallas_call(pair_kernel, out_shape=(jax.ShapeDtypeStruct((3, 8, 8, 128...  20.5 us
    pallas_call x1, Pallas kernels, exchange(): pl.pallas_call(exchange_kernel, out_shape=(jax.ShapeDtypeStruct((3, 3, 2,...  5.73 us
    pallas_call x1, Pallas kernels, volumes(): pl.pallas_call(volume_kernel, out_shape=(jax.ShapeDtypeStruct((3, 8, 8, 1...  1.39 us

profile of v5, /device:TPU:1, one launch (start us, length us, event | category | flops | bytes accessed | tf_op | source)
XLA Modules:
  0.0 62.9 jit_solution(5922682741076328314)
XLA Ops:
  0.6 0.1 pad_add_fusion.role
  0.7 0.0 copy-start
  0.7 0.0 copy-start.1
  0.7 34.5 %gather.1 = (f32[4,16,3,8,1,128]{5,4,3,2,1,0:T(1,128)S(1)}, f32[3,2,8,128]{3,2,1,0:T(8,128)S(1)}, s32[2,8,16]{2,1,0:T(8,128)S(1)}) custom-call(f32[3,16]{1,0:T(4,128)} %points_hbm.1, f32[16,18]{1,0:T(8,128)} %bitcast.12, f32[32,128]{1,0:T(8,128)} %bitcast.11, f32[3,4096]{1,0:T(4,128)} %area_hbm.1, f32[3,4096]{1,0:T(4,128)} %center_hbm.1, ...), custom_call_target="tpu_custom_call" | custom-call | tf_op jit(solution)/shard_map/gather/pallas_call | solution.py:256
  35.3 0.0 copy-done
  35.3 0.0 copy-done.1
  35.3 20.5 %pairs.1 = (f32[3,8,8,128]{3,2,1,0:T(8,128)S(1)}, f32[3,2,8,128]{3,2,1,0:T(8,128)S(1)}, f32[2,3,8,128]{3,2,1,0:T(8,128)S(1)}, f32[2,3,8,128]{3,2,1,0:T(8,128)S(1)}, f32[6]{0:T(128)}) custom-call(s32[3]{0:T(128)S(1)} %pad_add_fusion.role, s32[64,16]{1,0:T(8,128)S(1)} %bitcast.9, s32[16,16]{1,0:T(8,128)S(1)} %bitcast.10, s32[8,8]{1,0:T(8,128)} %counts_hbm.1, ...), custom_call_target="tpu_custom_call" | custom-call | tf_op jit(solution)/shard_map/pairs/pallas_call | solution.py:519
  55.8 5.7 %exchange.1 = (f32[3,3,2,8,128]{4,3,2,1,0:T(8,128)S(1)}, f32[2,3,8,128]{3,2,1,0:T(8,128)S(1)}, f32[2,3,8,128]{3,2,1,0:T(8,128)S(1)}, f32[2,3,8,128]{3,2,1,0:T(8,128)S(1)}) custom-call(f32[3,2,8,128]{3,2,1,0:T(8,128)S(1)} %get-tuple-element.23.more_shift, f32[2,3,8,128]{3,2,1,0:T(8,128)S(1)} %get-tuple-element.24.plane_edge, ...), custom_call_target="tpu_custom_call" | custom-call | tf_op jit(solution)/shard_map/exchange/pallas_call | solution.py:617
  61.5 1.4 %volumes.1 = (f32[3,8,8,128]{3,2,1,0:T(8,128)}, f32[8,8,128]{2,1,0:T(8,128)}, f32[8,8,128]{2,1,0:T(8,128)}) custom-call(s32[3]{0:T(128)S(1)} %pad_add_fusion.role, f32[3,8,8,128]{3,2,1,0:T(8,128)S(1)} %copy-done, f32[3,8,8,128]{3,2,1,0:T(8,128)S(1)} %get-tuple-element.22.shift, f32[3,3,2,8,128]{4,3,2,1,0:T(8,128)S(1)} %get-tuple-element.26.back, ...), custom_call_target="tpu_custom_call" | custom-call | tf_op jit(solution)/shard_map/volumes/pallas_call | solution.py:689
Async XLA Ops:
  0.7 34.6 %copy-start = (f32[3,8,8,128]{3,2,1,0:T(8,128)S(1)}, f32[3,8,8,128]{3,2,1,0:T(8,128)}, u32[]{:S(2)}) copy-start(f32[3,8,8,128]{3,2,1,0:T(8,128)} %nodes.5) | copy-start | bytes 294916
  0.7 34.6 %copy-start.1 = (s32[8,8,16]{2,1,0:T(8,128)S(1)}, s32[8,8,16]{2,1,0:T(8,128)}, u32[]{:S(2)}) copy-start(s32[8,8,16]{2,1,0:T(8,128)} %ids.1) | copy-start | bytes 12292

commit v6 on v5

--- a/solution.py
+++ b/solution.py
@@ -40,17 +40,82 @@
     return 2 - z // 8
 
 
+def split3(value):
+    hi = value.astype(BF16).astype(F32)
+    rest = value - hi
+    mid = rest.astype(BF16).astype(F32)
+    return hi, mid, rest - mid
+
+
+def regroup(v):
+    sub = iota((8, 128), 0)
+    grp = iota((8, 128), 1) // 16
+    for bit in (1, 2, 4):
+        below = pltpu.roll(pltpu.roll(v, 8 - bit, 0), 16 * bit, 1)
+        above = pltpu.roll(pltpu.roll(v, bit, 0), 128 - 16 * bit, 1) if bit < 4 else below
+        low = (sub & bit) == 0
+        same = low == ((grp & bit) == 0)
+        v = jnp.where(same, v, jnp.where(low, below, above))
+    return v
+
+
+def node_rows(nodes, p, r):
+    sub = iota((8, 128), 0)
+    x = [nodes[c, p, pl.ds(r, 1), :] for c in range(3)]
+    square = x[0] * x[0] + x[1] * x[1] + x[2] * x[2]
+    rows = jnp.where((sub == 0) | (sub == 3), -2.0 * x[0], 0.0)
+    rows = jnp.where((sub == 1) | (sub == 4), -2.0 * x[1], rows)
+    rows = jnp.where((sub == 2) | (sub == 5), -2.0 * x[2], rows)
+    rows = jnp.where(sub == 7, square, rows)
+    hi, mid, lo = split3(rows)
+    one = sub == 6
+    second = (sub >= 3) & (sub < 6)
+    parts = [
+        jnp.where(one, 1.0, jnp.where(second, mid, hi)),
+        jnp.where(one, 1.0, jnp.where(sub < 3, hi, mid)),
+        jnp.where(one, 1.0, jnp.where(second, hi, lo)),
+        jnp.zeros((8, 128), F32),
+    ]
+    return jnp.concatenate(parts, axis=0).astype(BF16)
+
+
+def control_rows(p):
+    sub = iota((8, 128), 0)
+    p = jnp.where(sub < 3, p, 0.0)
+    square = jnp.sum(p * p, axis=0, keepdims=True)
+    rows = p + pltpu.roll(p, 3, 0) + jnp.where(sub == 6, square, 0.0)
+    hi, mid, lo = split3(rows)
+    one = sub == 7
+    parts = [
+        jnp.where(one, 1.0, hi),
+        jnp.where(one, 1.0, mid),
+        jnp.where(one, 1.0, jnp.where(sub < 3, hi, lo)),
+        jnp.zeros((8, 128), F32),
+    ]
+    return parts
+
+
+LINES = 64
+MORE = 16
+
+
 def gather_kernel(
     points_hbm,
     modes_hbm,
     pressure_hbm,
     area_hbm,
     center_hbm,
+    nodes_hbm,
+    ids,
+    more_ids,
+    feats,
+    left_a,
+    left_b,
+    right,
+    total,
+    buf,
     nodes,
-    ids,
-    buf,
     more_nodes,
-    more_ids,
     points,
     modes,
     pressure,
@@ -68,10 +133,10 @@
     plane = [(i * core, i * (1 - core)) for i in range(1, 4)]
     turned = [(i * (1 - core), i * core) for i in range(1, 4)]
 
-    sources = (points_hbm, modes_hbm, pressure_hbm, area_hbm, center_hbm)
+    sources = (points_hbm, modes_hbm, pressure_hbm, area_hbm, center_hbm, nodes_hbm)
     fetches = [
         pltpu.make_async_copy(src, dst, fetch.at[i])
-        for i, (src, dst) in enumerate(zip(sources, (points, modes, pressure, area, center)))
+        for i, (src, dst) in enumerate(zip(sources, (points, modes, pressure, area, center, nodes)))
     ]
     for copy in fetches:
         copy.start()
@@ -118,11 +183,11 @@
     lane = iota((6, 128), 1)
     row = iota((6, 128), 0)
     loads = jnp.sum(jnp.where(lane == row + LOAD_LANE, sums, 0.0), axis=0, keepdims=True)
-    own[0] = packed[0]
-    own[1] = packed[1]
-    own[2] = packed[2] + loads
+    own[0:1, :] = packed[0]
+    own[1:2, :] = packed[1]
+    own[2:3, :] = packed[2] + loads
     for r in range(3):
-        buf[x, 4, r, group] = own[r]
+        buf[x, 4, r, pl.ds(group, 1), :] = own[r : r + 1, :]
 
     pl.semaphore_wait(barrier, len(greet))
 
@@ -132,7 +197,7 @@
         target = device(heavy_x(z) + 1 + h, y, z, core)
         parts = []
         for i, (src, dst) in enumerate(
-            ((nodes.at[:, pl.ds(src_plane, 2)], more_nodes), (ids.at[pl.ds(src_plane, 2)], more_ids))
+            ((nodes_hbm.at[:, pl.ds(src_plane, 2)], more_nodes), (ids.at[pl.ds(src_plane, 2)], more_ids))
         ):
             parts.append(
                 pltpu.make_async_remote_copy(
@@ -175,6 +240,13 @@
             for copy in hand(h, 1 + 2 * h):
                 copy.start()
 
+    def line(i, _):
+        right[i] = node_rows(nodes, i >> 3, i & 7)
+        return 0
+
+    lax.fori_loop(0, LINES, line, 0, unroll=4)
+    right[LINES + MORE] = jnp.zeros((32, 128), BF16)
+
     far = []
     for d in (1, 2, 3, 4):
         near[d].wait_recv()
@@ -218,6 +290,22 @@
     def across(part):
         ref = buf.at[:, halves[part], :, pl.ds(core * YS, YS)]
         return put(ref, ref, 27 + part, device(x, y, z, 1 - core))
+
+    half = jnp.where(iota((128, 64), 1) < 32, 1.0, 0.0).astype(BF16)
+
+    def unpack(j, carry):
+        for xx in range(XS):
+            t = xx * ZS + ((j + z + ZS - 4) & (ZS - 1))
+            v = [regroup(buf[xx, j, r]) for r in range(3)]
+            for r in range(3):
+                feats[t, pl.ds(8 * r, 8), :] = v[r]
+            parts = control_rows(v[0])
+            columns = jnp.transpose(jnp.concatenate(parts + parts, axis=0), (1, 0)).astype(BF16)
+            left = columns * half
+            left_a[t] = left
+            left_b[t] = columns - left
+            carry = carry + v[2]
+        return carry
 
     first_near = first(0)
     for copy in first_near:
@@ -231,10 +319,24 @@
     second(1, True)
     second(0, False)
     across_near = across(0)
+
+    @pl.when(jnp.logical_not(heavy))
+    def _():
+        for copy in hand(0, 1):
+            copy.wait_recv()
+
+        def more(i, _):
+            right[LINES + i] = node_rows(more_nodes, i >> 3, i & 7)
+            return 0
+
+        lax.fori_loop(0, MORE, more, 0, unroll=4)
+
+    across_near.wait_recv()
+    loads = lax.fori_loop(0, 9, unpack, jnp.zeros((8, 128), F32))
     second(1, False)
     across_far = across(1)
-    across_near.wait_recv()
     across_far.wait_recv()
+    total[...] = lax.fori_loop(9, ZS, unpack, loads)
     for copy in pending:
         copy.wait_send()
 
@@ -243,11 +345,6 @@
         for h in range(3):
             for copy in hand(h, 1 + 2 * h):
                 copy.wait_send()
-
-    @pl.when(jnp.logical_not(heavy))
-    def _():
-        for copy in hand(0, 1):
-            copy.wait_recv()
 
 
 def gather(points, modes, pressure, area, center, nodes, ids):
@@ -256,13 +353,19 @@
     return pl.pallas_call(
         gather_kernel,
         out_shape=(
-            jax.ShapeDtypeStruct((XS, ZS, 3, 8, 1, 128), F32),
-            jax.ShapeDtypeStruct((3, 2, 8, 128), F32),
             jax.ShapeDtypeStruct((2, 8, 16), jnp.int32),
+            jax.ShapeDtypeStruct((NTILE, 24, 128), F32),
+            jax.ShapeDtypeStruct((NTILE, 128, 64), BF16),
+            jax.ShapeDtypeStruct((NTILE, 128, 64), BF16),
+            jax.ShapeDtypeStruct((LINES + MORE + 1, 32, 128), BF16),
+            jax.ShapeDtypeStruct((8, 128), F32),
         ),
         in_specs=[pl.BlockSpec(memory_space=pltpu.HBM)] * 7,
-        out_specs=(vmem, hbm, hbm),
+        out_specs=(hbm,) + (vmem,) * 5,
         scratch_shapes=[
+            pltpu.VMEM((XS, ZS, 3, 8, 128), F32),
+            pltpu.VMEM(nodes.shape, F32),
+            pltpu.VMEM((3, 2, 8, 128), F32),
             pltpu.VMEM(points.shape, F32),
             pltpu.VMEM(modes.shape, F32),
             pltpu.VMEM(pressure.shape, F32),
@@ -270,8 +373,8 @@
             pltpu.VMEM(center.shape, F32),
             pltpu.VMEM((24, 128), F32),
             pltpu.VMEM((16, 128), F32),
-            pltpu.VMEM((3, 1, 128), F32),
-            pltpu.SemaphoreType.DMA((5,)),
+            pltpu.VMEM((3, 128), F32),
+            pltpu.SemaphoreType.DMA((6,)),
             pltpu.SemaphoreType.DMA((35,)),
             pltpu.SemaphoreType.DMA((31,)),
         ],
@@ -285,61 +388,6 @@
 VMEM_LIMIT = 24 << 20
 
 
-def split3(value):
-    hi = value.astype(BF16).astype(F32)
-    rest = value - hi
-    mid = rest.astype(BF16).astype(F32)
-    return hi, mid, rest - mid
-
-
-def regroup(v):
-    sub = iota((8, 128), 0)
-    grp = iota((8, 128), 1) // 16
-    for bit in (1, 2, 4):
-        below = pltpu.roll(pltpu.roll(v, 8 - bit, 0), 16 * bit, 1)
-        above = pltpu.roll(pltpu.roll(v, bit, 0), 128 - 16 * bit, 1) if bit < 4 else below
-        low = (sub & bit) == 0
-        same = low == ((grp & bit) == 0)
-        v = jnp.where(same, v, jnp.where(low, below, above))
-    return v
-
-
-def node_rows(nodes, p, r):
-    sub = iota((8, 128), 0)
-    x = [nodes[c, p, pl.ds(r, 1), :] for c in range(3)]
-    square = x[0] * x[0] + x[1] * x[1] + x[2] * x[2]
-    rows = jnp.where((sub == 0) | (sub == 3), -2.0 * x[0], 0.0)
-    rows = jnp.where((sub == 1) | (sub == 4), -2.0 * x[1], rows)
-    rows = jnp.where((sub == 2) | (sub == 5), -2.0 * x[2], rows)
-    rows = jnp.where(sub == 7, square, rows)
-    hi, mid, lo = split3(rows)
-    one = sub == 6
-    second = (sub >= 3) & (sub < 6)
-    parts = [
-        jnp.where(one, 1.0, jnp.where(second, mid, hi)),
-        jnp.where(one, 1.0, jnp.where(sub < 3, hi, mid)),
-        jnp.where(one, 1.0, jnp.where(second, hi, lo)),
-        jnp.zeros((8, 128), F32),
-    ]
-    return jnp.concatenate(parts, axis=0).astype(BF16)
-
-
-def control_rows(p):
-    sub = iota((8, 128), 0)
-    p = jnp.where(sub < 3, p, 0.0)
-    square = jnp.sum(p * p, axis=0, keepdims=True)
-    rows = p + pltpu.roll(p, 3, 0) + jnp.where(sub == 6, square, 0.0)
-    hi, mid, lo = split3(rows)
-    one = sub == 7
-    parts = [
-        jnp.where(one, 1.0, hi),
-        jnp.where(one, 1.0, mid),
-        jnp.where(one, 1.0, jnp.where(sub < 3, hi, lo)),
-        jnp.zeros((8, 128), F32),
-    ]
-    return parts
-
-
 BLOCK = 32
 
 
@@ -350,20 +398,19 @@
     counts_hbm,
     motion_hbm,
     inverse_mass_hbm,
-    raw,
+    total_ref,
+    feats,
+    left_a,
+    left_b,
+    right,
     nodes,
-    more_nodes,
     shift,
     more_shift,
     plane_edge,
     row_edge,
     state,
-    feats,
-    left_a,
-    left_b,
     mix_a,
     mix_b,
-    right,
     sums,
     unit_of,
     ids,
@@ -383,20 +430,11 @@
         copy.start()
     heavy = role[0]
     light = 1 - heavy
-    z = (role[1] >> 1) & (ZS - 1)
     sub = iota((8, 128), 0)
 
-    def unpack(t, total):
-        at = (t & ~(ZS - 1)) | ((t - z + 4) & (ZS - 1))
-        v = [regroup(raw[at, r]) for r in range(3)]
-        for r in range(3):
-            feats[t, pl.ds(8 * r, 8), :] = v[r]
-        return total + v[2]
-
-    total = lax.fori_loop(0, NTILE, unpack, jnp.zeros((8, 128), F32), unroll=4)
     for copy in fetches:
         copy.wait()
-    total = jnp.broadcast_to(total[5:6, :], (8, 128))
+    total = jnp.broadcast_to(total_ref[5:6, :], (8, 128))
     for by in (16, 32, 64):
         total = total + pltpu.roll(total, by, 1)
     rigid = []
@@ -405,8 +443,6 @@
         acceleration = inverse_mass[k] * load + GRAVITY[k]
         state[k] = (motion[k] + TIME_STEP * acceleration)[0, 0]
         rigid.append((TIME_STEP * motion[k] + 0.5 * TIME_STEP * TIME_STEP * acceleration)[0:3])
-
-    first_half = jnp.where(iota((128, 64), 1) < 32, 1.0, 0.0).astype(BF16)
 
     def prepare(i, n):
         q = jnp.minimum(i, 13)
@@ -422,11 +458,6 @@
                 unit_of[n + e] = more_code + more_ids[more_line, 4 * u + e]
             n = n + more_count
 
-            parts = control_rows(feats[t, 0:8, :])
-            columns = jnp.transpose(jnp.concatenate(parts + parts, axis=0), (1, 0)).astype(BF16)
-            left = columns * first_half
-            left_a[t] = left
-            left_b[t] = columns - left
             c = jnp.zeros((3, 128), F32)
             for k in range(6):
                 c = c + rigid[k] * feats[t, 3 + 3 * k : 6 + 3 * k, :]
@@ -437,7 +468,6 @@
             zero = jnp.zeros((8, 128), F32)
             mix_a[t] = jnp.concatenate([c, zero], axis=0).astype(BF16)
             mix_b[t] = jnp.concatenate([zero, c], axis=0).astype(BF16)
-            right[t] = node_rows(nodes, i >> 1, ((i & 1) << 2) + u)
             sums[t] = zero
         return n
 
@@ -453,13 +483,8 @@
     for e in range(BLOCK):
         unit_of[n + e] = lines * NTILE
 
-    def prepare_more(i, _):
-        right[LINES + i] = node_rows(more_nodes, i >> 3, i & 7)
-        sums[LINES + i] = jnp.zeros((8, 128), F32)
-        return 0
-
-    lax.fori_loop(0, MORE, prepare_more, 0, unroll=4)
-    right[lines] = jnp.zeros((32, 128), BF16)
+    for i in range(LINES, lines):
+        sums[i] = jnp.zeros((8, 128), F32)
     sums[lines] = jnp.zeros((8, 128), F32)
 
     gap = jnp.zeros((32, 128), BF16)
@@ -507,11 +532,7 @@
             row_edge[1, c, p : p + 1, :] = nodes[c, p, 0:1, :] + shift[c, p, 0:1, :]
 
 
-LINES = 64
-MORE = 16
-
-
-def pair_sums(role, ids, more_ids, counts, motion, inverse_mass, raw, nodes, more_nodes):
+def pair_sums(role, ids, more_ids, counts, motion, inverse_mass, total, feats, left_a, left_b, right, nodes):
     vmem = pl.BlockSpec(memory_space=pltpu.VMEM)
     smem = pl.BlockSpec(memory_space=pltpu.SMEM)
     lines = LINES + MORE
@@ -525,15 +546,11 @@
             jax.ShapeDtypeStruct((2, 3, 8, 128), F32),
             jax.ShapeDtypeStruct((6,), F32),
         ),
-        in_specs=[smem] + [pl.BlockSpec(memory_space=pltpu.HBM)] * 5 + [vmem] * 3,
+        in_specs=[smem] + [pl.BlockSpec(memory_space=pltpu.HBM)] * 5 + [vmem] * 6,
         out_specs=(vmem,) * 4 + (smem,),
         scratch_shapes=[
-            pltpu.VMEM((NTILE, 24, 128), F32),
-            pltpu.VMEM((NTILE, 128, 64), BF16),
-            pltpu.VMEM((NTILE, 128, 64), BF16),
             pltpu.VMEM((NTILE, 16, 128), BF16),
             pltpu.VMEM((NTILE, 16, 128), BF16),
-            pltpu.VMEM((lines + 1, 32, 128), BF16),
             pltpu.VMEM((lines + 1, 8, 128), F32),
             pltpu.SMEM((units,), jnp.int32),
             pltpu.SMEM((LINES, 16), jnp.int32),
@@ -545,7 +562,7 @@
         ],
         compiler_params=pltpu.CompilerParams(vmem_limit_bytes=VMEM_LIMIT),
         name="pairs",
-    )(role, ids, more_ids, counts, motion, inverse_mass, raw, nodes, more_nodes)
+    )(role, ids, more_ids, counts, motion, inverse_mass, total, feats, left_a, left_b, right, nodes)
 
 
 def exchange_kernel(more_shift, plane_edge, row_edge, back, planes, rows, corners, send, recv):
@@ -712,7 +729,7 @@
     tile_list,
     tile_count,
 ):
-    raw, more_nodes, more_ids = gather(
+    more_ids, feats, left_a, left_b, right, total = gather(
         control_points, control_modes.T, face_pressure.reshape(-1, 128), face_area, face_center, node_points, tile_list
     )
     role = jnp.stack(
@@ -723,9 +740,12 @@
         tile_list.reshape(LINES, 16),
         more_ids.reshape(MORE, 16),
         *(pltpu.with_memory_space_constraint(v, pltpu.HBM) for v in (tile_count, motion, inverse_mass)),
-        raw.reshape(NTILE, 3, 8, 128),
+        total,
+        feats,
+        left_a,
+        left_b,
+        right,
         node_points,
-        more_nodes,
     )
     back, planes, rows, corners = exchange(more_shift, plane_edge, row_edge)
     node_shift, volume, change = volumes(role, node_points, shift, back, planes, rows, corners)

time: 63.3 us -> 64.1 us (1.013)
  local copies, waits for them, and re-layouts: 0.01 us -> 1.65 us
  Pallas kernels: 62.1 us -> 61.4 us
    pallas_call x1, Pallas kernels: 20.5 us -> 17.9 us  [pair_sums(): pl.pallas_call(pair_kernel, out_shape=(jax.ShapeDtypeStruct((3, 8, 8, 128...]
    pallas_call x1, Pallas kernels: 34.5 us -> 37 us  [gather(): pl.pallas_call(gather_kernel, out_shape=(jax.ShapeDtypeStruct((2, 8, 16),...]
    unnamed x4 -> x6, local copies, waits for them, and re-layouts: 0.01 us -> 1.65 us
where the time goes in v6:
time: 64.1 us; the launch traced here: 63.8 us
  Pallas kernels  61.4 us (96%)
  local copies, waits for them, and re-layouts  1.65 us (3%)
  between operations  0.68 us (1%)
    pallas_call x1, Pallas kernels, gather(): pl.pallas_call(gather_kernel, out_shape=(jax.ShapeDtypeStruct((2, 8, 16),...  37 us
    pallas_call x1, Pallas kernels, pair_sums(): pl.pallas_call(pair_kernel, out_shape=(jax.ShapeDtypeStruct((3, 8, 8, 128...  17.9 us
    pallas_call x1, Pallas kernels, exchange(): pl.pallas_call(exchange_kernel, out_shape=(jax.ShapeDtypeStruct((3, 3, 2,...  5.16 us
    unnamed x6, local copies, waits for them, and re-layouts  1.65 us
    pallas_call x1, Pallas kernels, volumes(): pl.pallas_call(volume_kernel, out_shape=(jax.ShapeDtypeStruct((3, 8, 8, 1...  1.38 us

profile of v6, /device:TPU:1, one launch (start us, length us, event | category | flops | bytes accessed | tf_op | source)
XLA Modules:
  0.0 63.8 jit_solution(4464999953772012955)
XLA Ops:
  0.6 0.1 pad_add_fusion.role
  0.7 37.0 %gather.1 = (s32[2,8,16]{2,1,0:T(8,128)S(1)}, f32[64,24,128]{2,1,0:T(8,128)S(1)}, bf16[64,128,64]{2,1,0:T(8,128)(2,1)S(1)}, bf16[64,128,64]{2,1,0:T(8,128)(2,1)S...) custom-call(f32[3,16]{1,0:T(4,128)} %points_hbm.1, f32[16,18]{1,0:T(8,128)} %bitcast.10, f32[32,128]{1,0:T(8,128)} %bitcast.9, ...), custom_call_target="tpu_custom_call" | custom-call | tf_op jit(solution)/shard_map/gather/pallas_call | solution.py:353
  37.7 0.0 copy-start
  37.7 0.9 %copy-done = f32[3,8,8,128]{3,2,1,0:T(8,128)S(1)} copy-done((f32[3,8,8,128]{3,2,1,0:T(8,128)S(1)}, f32[3,8,8,128]{3,2,1,0:T(8,128)}, u32[]{:S(2)}) %copy-start) | copy-done | bytes 98328
  38.6 0.0 copy-start.2
  38.6 0.8 %copy-done.2 = s32[8,8,16]{2,1,0:T(8,128)S(1)} copy-done((s32[8,8,16]{2,1,0:T(8,128)S(1)}, s32[8,8,16]{2,1,0:T(8,128)}, u32[]{:S(2)}) %copy-start.2) | copy-done | bytes 4120
  39.4 0.0 copy-start.1
  39.4 17.9 %pairs.1 = (f32[3,8,8,128]{3,2,1,0:T(8,128)S(1)}, f32[3,2,8,128]{3,2,1,0:T(8,128)S(1)}, f32[2,3,8,128]{3,2,1,0:T(8,128)S(1)}, f32[2,3,8,128]{3,2,1,0:T(8,128)S(1)}, f32[6]{0:T(128)}) custom-call(s32[3]{0:T(128)S(1)} %pad_add_fusion.role, s32[64,16]{1,0:T(8,128)S(1)} %bitcast.7, s32[16,16]{1,0:T(8,128)S(1)} %bitcast.8, s32[8,8]{1,0:T(8,128)} %counts_hbm.1, ...), custom_call_target="tpu_custom_call" | custom-call | tf_op jit(solution)/shard_map/pairs/pallas_call | solution.py:540
  57.3 5.2 %exchange.1 = (f32[3,3,2,8,128]{4,3,2,1,0:T(8,128)S(1)}, f32[2,3,8,128]{3,2,1,0:T(8,128)S(1)}, f32[2,3,8,128]{3,2,1,0:T(8,128)S(1)}, f32[2,3,8,128]{3,2,1,0:T(8,128)S(1)}) custom-call(f32[3,2,8,128]{3,2,1,0:T(8,128)S(1)} %get-tuple-element.29.more_shift, f32[2,3,8,128]{3,2,1,0:T(8,128)S(1)} %get-tuple-element.30.plane_edge, ...), custom_call_target="tpu_custom_call" | custom-call | tf_op jit(solution)/shard_map/exchange/pallas_call | solution.py:634
  62.4 0.0 copy-done.1
  62.4 1.4 %volumes.1 = (f32[3,8,8,128]{3,2,1,0:T(8,128)}, f32[8,8,128]{2,1,0:T(8,128)}, f32[8,8,128]{2,1,0:T(8,128)}) custom-call(s32[3]{0:T(128)S(1)} %pad_add_fusion.role, f32[3,8,8,128]{3,2,1,0:T(8,128)S(1)} %copy-done.1, f32[3,8,8,128]{3,2,1,0:T(8,128)S(1)} %get-tuple-element.28.shift, f32[3,3,2,8,128]{4,3,2,1,0:T(8,128)S(1)} %get-tuple-element.32.back, ...), custom_call_target="tpu_custom_call" | custom-call | tf_op jit(solution)/shard_map/volumes/pallas_call | solution.py:706
Async XLA Ops:
  37.7 0.9 %copy-start = (f32[3,8,8,128]{3,2,1,0:T(8,128)S(1)}, f32[3,8,8,128]{3,2,1,0:T(8,128)}, u32[]{:S(2)}) copy-start(f32[3,8,8,128]{3,2,1,0:T(8,128)} %nodes.3) | copy-start | bytes 294916
  38.6 0.8 %copy-start.2 = (s32[8,8,16]{2,1,0:T(8,128)S(1)}, s32[8,8,16]{2,1,0:T(8,128)}, u32[]{:S(2)}) copy-start(s32[8,8,16]{2,1,0:T(8,128)} %ids.1) | copy-start | bytes 12292
  39.4 23.1 %copy-start.1 = (f32[3,8,8,128]{3,2,1,0:T(8,128)S(1)}, f32[3,8,8,128]{3,2,1,0:T(8,128)}, u32[]{:S(2)}) copy-start(f32[3,8,8,128]{3,2,1,0:T(8,128)} %nodes.3) | copy-start | bytes 294916

commit v7 on v6

--- a/solution.py
+++ b/solution.py
@@ -106,13 +106,18 @@
     area_hbm,
     center_hbm,
     nodes_hbm,
-    ids,
-    more_ids,
+    ids_hbm,
+    counts_hbm,
+    motion_hbm,
+    inverse_mass_hbm,
+    all_ids,
+    counts,
     feats,
     left_a,
     left_b,
     right,
-    total,
+    rigid,
+    accelerations,
     buf,
     nodes,
     more_nodes,
@@ -124,6 +129,8 @@
     pack,
     turn,
     own,
+    motion,
+    inverse_mass,
     fetch,
     send,
     recv,
@@ -133,10 +140,22 @@
     plane = [(i * core, i * (1 - core)) for i in range(1, 4)]
     turned = [(i * (1 - core), i * core) for i in range(1, 4)]
 
-    sources = (points_hbm, modes_hbm, pressure_hbm, area_hbm, center_hbm, nodes_hbm)
+    sources = (
+        points_hbm,
+        modes_hbm,
+        pressure_hbm,
+        area_hbm,
+        center_hbm,
+        nodes_hbm,
+        ids_hbm,
+        counts_hbm,
+        motion_hbm,
+        inverse_mass_hbm,
+    )
+    kept = all_ids.at[pl.ds(0, 8)]
+    targets = (points, modes, pressure, area, center, nodes, kept, counts, motion, inverse_mass)
     fetches = [
-        pltpu.make_async_copy(src, dst, fetch.at[i])
-        for i, (src, dst) in enumerate(zip(sources, (points, modes, pressure, area, center, nodes)))
+        pltpu.make_async_copy(src, dst, fetch.at[i]) for i, (src, dst) in enumerate(zip(sources, targets))
     ]
     for copy in fetches:
         copy.start()
@@ -197,7 +216,7 @@
         target = device(heavy_x(z) + 1 + h, y, z, core)
         parts = []
         for i, (src, dst) in enumerate(
-            ((nodes_hbm.at[:, pl.ds(src_plane, 2)], more_nodes), (ids.at[pl.ds(src_plane, 2)], more_ids))
+            ((nodes_hbm.at[:, pl.ds(src_plane, 2)], more_nodes), (ids_hbm.at[pl.ds(src_plane, 2)], all_ids.at[pl.ds(8, 2)]))
         ):
             parts.append(
                 pltpu.make_async_remote_copy(
@@ -332,11 +351,19 @@
         lax.fori_loop(0, MORE, more, 0, unroll=4)
 
     across_near.wait_recv()
-    loads = lax.fori_loop(0, 9, unpack, jnp.zeros((8, 128), F32))
+    loads = lax.fori_loop(0, 5, unpack, jnp.zeros((8, 128), F32))
     second(1, False)
     across_far = across(1)
+    loads = lax.fori_loop(5, 9, unpack, loads)
     across_far.wait_recv()
-    total[...] = lax.fori_loop(9, ZS, unpack, loads)
+    loads = lax.fori_loop(9, ZS, unpack, loads)
+    total = jnp.broadcast_to(loads[5:6, :], (8, 128))
+    for by in (16, 32, 64):
+        total = total + pltpu.roll(total, by, 1)
+    for k in range(6):
+        acceleration = inverse_mass[k] * jnp.broadcast_to(total[:, k : k + 1], (8, 128)) + GRAVITY[k]
+        accelerations[k] = acceleration
+        rigid[k] = TIME_STEP * motion[k] + 0.5 * TIME_STEP * TIME_STEP * acceleration
     for copy in pending:
         copy.wait_send()
 
@@ -347,21 +374,23 @@
                 copy.wait_send()
 
 
-def gather(points, modes, pressure, area, center, nodes, ids):
+def gather(*arrays):
+    points, modes, pressure, area, center, nodes, ids, counts, motion, inverse_mass = arrays
     vmem = pl.BlockSpec(memory_space=pltpu.VMEM)
-    hbm = pl.BlockSpec(memory_space=pl.ANY)
     return pl.pallas_call(
         gather_kernel,
         out_shape=(
-            jax.ShapeDtypeStruct((2, 8, 16), jnp.int32),
+            jax.ShapeDtypeStruct((10, 8, 16), jnp.int32),
+            jax.ShapeDtypeStruct((8, 8), jnp.int32),
             jax.ShapeDtypeStruct((NTILE, 24, 128), F32),
             jax.ShapeDtypeStruct((NTILE, 128, 64), BF16),
             jax.ShapeDtypeStruct((NTILE, 128, 64), BF16),
             jax.ShapeDtypeStruct((LINES + MORE + 1, 32, 128), BF16),
-            jax.ShapeDtypeStruct((8, 128), F32),
+            jax.ShapeDtypeStruct((6, 8, 128), F32),
+            jax.ShapeDtypeStruct((6, 8, 128), F32),
         ),
-        in_specs=[pl.BlockSpec(memory_space=pltpu.HBM)] * 7,
-        out_specs=(hbm,) + (vmem,) * 5,
+        in_specs=[pl.BlockSpec(memory_space=pltpu.HBM)] * 10,
+        out_specs=(vmem,) * 8,
         scratch_shapes=[
             pltpu.VMEM((XS, ZS, 3, 8, 128), F32),
             pltpu.VMEM(nodes.shape, F32),
@@ -374,7 +403,9 @@
             pltpu.VMEM((24, 128), F32),
             pltpu.VMEM((16, 128), F32),
             pltpu.VMEM((3, 128), F32),
-            pltpu.SemaphoreType.DMA((6,)),
+            pltpu.SMEM((6,), F32),
+            pltpu.SMEM((6,), F32),
+            pltpu.SemaphoreType.DMA((10,)),
             pltpu.SemaphoreType.DMA((35,)),
             pltpu.SemaphoreType.DMA((31,)),
         ],
@@ -382,28 +413,37 @@
             collective_id=0, has_side_effects=True, vmem_limit_bytes=VMEM_LIMIT
         ),
         name="gather",
-    )(*(pltpu.with_memory_space_constraint(v, pltpu.HBM) for v in (points, modes, pressure, area, center, nodes, ids)))
+    )(*(pltpu.with_memory_space_constraint(v, pltpu.HBM) for v in arrays))
 
 
 VMEM_LIMIT = 24 << 20
 
 
 BLOCK = 32
+
+
+def weights(s):
+    s = jnp.minimum(jnp.maximum(s, 1e-30), 16.0)
+    d = s * lax.rsqrt(s)
+    v = 4.0 - d
+    v = v * v
+    k = v * v * (1.0 + d)
+    hi = k.astype(BF16)
+    return jnp.concatenate([hi, (k - hi.astype(F32)).astype(BF16)], axis=0)
 
 
 def pair_kernel(
     role,
-    ids_hbm,
-    more_ids_hbm,
-    counts_hbm,
+    ids_vmem,
+    counts_vmem,
     motion_hbm,
-    inverse_mass_hbm,
-    total_ref,
+    nodes_hbm,
+    rigid,
+    accelerations,
     feats,
     left_a,
     left_b,
     right,
-    nodes,
     shift,
     more_shift,
     plane_edge,
@@ -412,110 +452,92 @@
     mix_a,
     mix_b,
     sums,
+    nodes,
     unit_of,
     ids,
-    more_ids,
     counts,
     motion,
-    inverse_mass,
     fetch,
 ):
     lines = LINES + MORE
-    sources = (ids_hbm, more_ids_hbm, counts_hbm, motion_hbm, inverse_mass_hbm)
+    sources = (ids_vmem, counts_vmem, motion_hbm, nodes_hbm)
     fetches = [
         pltpu.make_async_copy(src, dst, fetch.at[i])
-        for i, (src, dst) in enumerate(zip(sources, (ids, more_ids, counts, motion, inverse_mass)))
+        for i, (src, dst) in enumerate(zip(sources, (ids, counts, motion, nodes)))
     ]
     for copy in fetches:
         copy.start()
     heavy = role[0]
     light = 1 - heavy
     sub = iota((8, 128), 0)
-
-    for copy in fetches:
+    zero = jnp.zeros((8, 128), F32)
+
+    for i in range(lines + 1):
+        sums[i] = zero
+    for copy in fetches[:2]:
         copy.wait()
-    total = jnp.broadcast_to(total_ref[5:6, :], (8, 128))
-    for by in (16, 32, 64):
-        total = total + pltpu.roll(total, by, 1)
-    rigid = []
-    for k in range(6):
-        load = jnp.broadcast_to(total[:, k : k + 1], (8, 128))
-        acceleration = inverse_mass[k] * load + GRAVITY[k]
-        state[k] = (motion[k] + TIME_STEP * acceleration)[0, 0]
-        rigid.append((TIME_STEP * motion[k] + 0.5 * TIME_STEP * TIME_STEP * acceleration)[0:3])
-
-    def prepare(i, n):
-        q = jnp.minimum(i, 13)
-        more_line = q + jnp.where(q < 7, 1, 2)
-        more_code = (LINES + more_line) << 6
-        more_count = jnp.where(i < 14, 4 * light, 0)
-        for u in range(4):
-            t = 4 * i + u
-            for e in range(4):
-                unit_of[n + e] = (t << 6) + ids[t, e]
-            n = n + light * counts[i >> 1, ((i & 1) << 2) + u]
-            for e in range(4):
-                unit_of[n + e] = more_code + more_ids[more_line, 4 * u + e]
-            n = n + more_count
-
-            c = jnp.zeros((3, 128), F32)
-            for k in range(6):
-                c = c + rigid[k] * feats[t, 3 + 3 * k : 6 + 3 * k, :]
-            c = c * (1.0 / 256.0)
-            c = jnp.concatenate([c, c, jnp.zeros((2, 128), F32)], axis=0)
-            c_hi = c.astype(BF16).astype(F32)
-            c = jnp.where(sub < 3, c_hi, c - c_hi)
-            zero = jnp.zeros((8, 128), F32)
-            mix_a[t] = jnp.concatenate([c, zero], axis=0).astype(BF16)
-            mix_b[t] = jnp.concatenate([zero, c], axis=0).astype(BF16)
-            sums[t] = zero
+
+    def prepare(t, n):
+        for e in range(4):
+            unit_of[n + e] = (t << 6) + ids[t, e]
+        n = n + light * counts[t >> 3, t & 7]
+        c = jnp.zeros((3, 128), F32)
+        for k in range(6):
+            c = c + rigid[k, 0:3, :] * feats[t, 3 + 3 * k : 6 + 3 * k, :]
+        c = c * (1.0 / 256.0)
+        c = jnp.concatenate([c, c, jnp.zeros((2, 128), F32)], axis=0)
+        c_hi = c.astype(BF16).astype(F32)
+        c = jnp.where(sub < 3, c_hi, c - c_hi)
+        mix_a[t] = jnp.concatenate([c, zero], axis=0).astype(BF16)
+        mix_b[t] = jnp.concatenate([zero, c], axis=0).astype(BF16)
         return n
 
-    n = lax.fori_loop(0, NTILE // 4, prepare, jnp.int32(0))
-
-    def keep(i, n):
-        line = jnp.where(i < 8, i, jnp.where(i < 15, (i - 7) << 3, i + 42))
+    n = lax.fori_loop(0, NTILE, prepare, jnp.int32(0), unroll=8)
+
+    gap = jnp.zeros((32, 128), BF16)
+
+    def pair(t1, t2, rhs):
+        s = jnp.dot(left_a[t1] + left_b[t2], rhs, preferred_element_type=F32)
+        m = mix_a[t1] + mix_b[t2]
+        return jnp.dot(jnp.concatenate([m, m], axis=1), weights(s), preferred_element_type=F32)
+
+    def beside(l1, l2):
+        return jnp.concatenate(
+            [jnp.concatenate([right[l1], gap], axis=1), jnp.concatenate([gap, right[l2]], axis=1)], axis=0
+        )
+
+    def full_line(i):
+        own = jnp.where(i < 8, i, jnp.where(i < 15, (i - 7) << 3, i + 42))
+        return jnp.where(heavy == 1, own, LINES + i + jnp.where(i < 7, 1, 2))
+
+    def full(b, _):
+        l1, l2 = full_line(2 * b), full_line(2 * b + 1)
         for e in range(16):
-            unit_of[n + e] = (line << 6) + ids[line, e]
-        return n + 16
-
-    n = lax.fori_loop(0, 22 * heavy, keep, n)
+            out = pair(ids[l1, e], ids[l2, e], beside(l1, l2))
+            sums[l1] += out[0:8, 0:128]
+            sums[l2] += out[8:16, 128:256]
+        return 0
+
+    lax.fori_loop(0, jnp.where(heavy == 1, 11, 7), full, 0)
     for e in range(BLOCK):
-        unit_of[n + e] = lines * NTILE
-
-    for i in range(LINES, lines):
-        sums[i] = jnp.zeros((8, 128), F32)
-    sums[lines] = jnp.zeros((8, 128), F32)
-
-    gap = jnp.zeros((32, 128), BF16)
+        unit_of[n + e] = lines << 6
 
     def block(g, _):
         for u in range(0, BLOCK, 2):
             i = g * BLOCK + u
             c1, c2 = unit_of[i], unit_of[i + 1]
-            t1, t2 = c1 & (NTILE - 1), c2 & (NTILE - 1)
             l1, l2 = c1 >> 6, c2 >> 6
-            rhs = jnp.concatenate(
-                [jnp.concatenate([right[l1], gap], axis=1), jnp.concatenate([gap, right[l2]], axis=1)], axis=0
-            )
-            s = jnp.dot(left_a[t1] + left_b[t2], rhs, preferred_element_type=F32)
-            s = jnp.minimum(jnp.maximum(s, 1e-30), 16.0)
-            d = s * lax.rsqrt(s)
-            v = 4.0 - d
-            v = v * v
-            k = v * v * (1.0 + d)
-            hi = k.astype(BF16)
-            lo = (k - hi.astype(F32)).astype(BF16)
-            m = mix_a[t1] + mix_b[t2]
-            out = jnp.dot(
-                jnp.concatenate([m, m], axis=1), jnp.concatenate([hi, lo], axis=0), preferred_element_type=F32
-            )
+            out = pair(c1 & (NTILE - 1), c2 & (NTILE - 1), beside(l1, l2))
             sums[l1] += out[0:8, 0:128]
             sums[l2] += out[8:16, 128:256]
         return 0
 
     lax.fori_loop(0, (n + BLOCK - 1) >> 5, block, 0)
 
+    for copy in fetches[2:]:
+        copy.wait()
+    for k in range(6):
+        state[k] = motion[k] + TIME_STEP * accelerations[k][0, 0]
     for i in range(lines):
         v = sums[i]
         v = v + pltpu.roll(v, 5, 0)
@@ -532,11 +554,11 @@
             row_edge[1, c, p : p + 1, :] = nodes[c, p, 0:1, :] + shift[c, p, 0:1, :]
 
 
-def pair_sums(role, ids, more_ids, counts, motion, inverse_mass, total, feats, left_a, left_b, right, nodes):
+def pair_sums(role, ids, counts, motion, nodes, rigid, accelerations, feats, left_a, left_b, right):
     vmem = pl.BlockSpec(memory_space=pltpu.VMEM)
     smem = pl.BlockSpec(memory_space=pltpu.SMEM)
     lines = LINES + MORE
-    units = 4 * LINES + 14 * 16 + 2 * BLOCK
+    units = 4 * LINES + 2 * BLOCK
     return pl.pallas_call(
         pair_kernel,
         out_shape=(
@@ -546,23 +568,22 @@
             jax.ShapeDtypeStruct((2, 3, 8, 128), F32),
             jax.ShapeDtypeStruct((6,), F32),
         ),
-        in_specs=[smem] + [pl.BlockSpec(memory_space=pltpu.HBM)] * 5 + [vmem] * 6,
+        in_specs=[smem, vmem, vmem] + [pl.BlockSpec(memory_space=pltpu.HBM)] * 2 + [vmem] * 6,
         out_specs=(vmem,) * 4 + (smem,),
         scratch_shapes=[
             pltpu.VMEM((NTILE, 16, 128), BF16),
             pltpu.VMEM((NTILE, 16, 128), BF16),
             pltpu.VMEM((lines + 1, 8, 128), F32),
+            pltpu.VMEM((3, 8, 8, 128), F32),
             pltpu.SMEM((units,), jnp.int32),
-            pltpu.SMEM((LINES, 16), jnp.int32),
-            pltpu.SMEM((MORE, 16), jnp.int32),
+            pltpu.SMEM((LINES + MORE, 16), jnp.int32),
             pltpu.SMEM((8, 8), jnp.int32),
             pltpu.SMEM((6,), F32),
-            pltpu.SMEM((6,), F32),
-            pltpu.SemaphoreType.DMA((5,)),
+            pltpu.SemaphoreType.DMA((4,)),
         ],
         compiler_params=pltpu.CompilerParams(vmem_limit_bytes=VMEM_LIMIT),
         name="pairs",
-    )(role, ids, more_ids, counts, motion, inverse_mass, total, feats, left_a, left_b, right, nodes)
+    )(role, ids, counts, motion, nodes, rigid, accelerations, feats, left_a, left_b, right)
 
 
 def exchange_kernel(more_shift, plane_edge, row_edge, back, planes, rows, corners, send, recv):
@@ -729,23 +750,32 @@
     tile_list,
     tile_count,
 ):
-    more_ids, feats, left_a, left_b, right, total = gather(
-        control_points, control_modes.T, face_pressure.reshape(-1, 128), face_area, face_center, node_points, tile_list
+    all_ids, counts, feats, left_a, left_b, right, rigid, accelerations = gather(
+        control_points,
+        control_modes.T,
+        face_pressure.reshape(-1, 128),
+        face_area,
+        face_center,
+        node_points,
+        tile_list,
+        tile_count,
+        motion,
+        inverse_mass,
     )
     role = jnp.stack(
         [is_heavy().astype(jnp.int32), lax.axis_index("slab").astype(jnp.int32), lax.axis_index("ctrl").astype(jnp.int32)]
     )
     shift, more_shift, plane_edge, row_edge, new_state = pair_sums(
         role,
-        tile_list.reshape(LINES, 16),
-        more_ids.reshape(MORE, 16),
-        *(pltpu.with_memory_space_constraint(v, pltpu.HBM) for v in (tile_count, motion, inverse_mass)),
-        total,
+        all_ids.reshape(LINES + MORE, 16),
+        counts,
+        *(pltpu.with_memory_space_constraint(v, pltpu.HBM) for v in (motion, node_points)),
+        rigid,
+        accelerations,
         feats,
         left_a,
         left_b,
         right,
-        node_points,
     )
     back, planes, rows, corners = exchange(more_shift, plane_edge, row_edge)
     node_shift, volume, change = volumes(role, node_points, shift, back, planes, rows, corners)

time: 64.1 us -> 61.7 us (0.963)
  local copies, waits for them, and re-layouts: 1.65 us -> 0.01 us
  Pallas kernels: 61.4 us -> 60.7 us
    pallas_call x1, Pallas kernels: 17.9 us -> 15.8 us  [pair_sums(): pl.pallas_call(pair_kernel, out_shape=(jax.ShapeDtypeStruct((3, 8, 8, 128...]
    unnamed x6 -> x2, local copies, waits for them, and re-layouts: 1.65 us -> 0.01 us
    pallas_call x1, Pallas kernels: 5.16 us -> 6.23 us  [exchange(): pl.pallas_call(exchange_kernel, out_shape=(jax.ShapeDtypeStruct((3, 3, 2,...]
where the time goes in v7:
time: 61.7 us; the launch traced here: 61.5 us
  Pallas kernels  60.7 us (98%)
  between operations  0.68 us (1%)
    pallas_call x1, Pallas kernels, gather(): pl.pallas_call(gather_kernel, out_shape=(jax.ShapeDtypeStruct((10, 8, 16)...  37.3 us
    pallas_call x1, Pallas kernels, pair_sums(): pl.pallas_call(pair_kernel, out_shape=(jax.ShapeDtypeStruct((3, 8, 8, 128...  15.8 us
    pallas_call x1, Pallas kernels, exchange(): pl.pallas_call(exchange_kernel, out_shape=(jax.ShapeDtypeStruct((3, 3, 2,...  6.23 us
    pallas_call x1, Pallas kernels, volumes(): pl.pallas_call(volume_kernel, out_shape=(jax.ShapeDtypeStruct((3, 8, 8, 1...  1.38 us

profile of v7, /device:TPU:1, one launch (start us, length us, event | category | flops | bytes accessed | tf_op | source)
XLA Modules:
  0.0 61.5 jit_solution(17430725011590782776)
XLA Ops:
  0.6 0.1 pad_add_fusion.role
  0.7 37.3 %gather.1 = (s32[10,8,16]{2,1,0:T(8,128)S(1)}, s32[8,8]{1,0:T(8,128)S(1)}, f32[64,24,128]{2,1,0:T(8,128)S(1)}, bf16[64,128,64]{2,1,0:T(8,128)(2,1)S(1)}, bf16[64...) custom-call(f32[3,16]{1,0:T(4,128)} %points_hbm.1, ...), custom_call_target="tpu_custom_call" | custom-call | tf_op jit(solution)/shard_map/gather/pallas_call | solution.py:380
  38.0 0.0 copy-start
  38.0 15.8 %pairs.1 = (f32[3,8,8,128]{3,2,1,0:T(8,128)S(1)}, f32[3,2,8,128]{3,2,1,0:T(8,128)S(1)}, f32[2,3,8,128]{3,2,1,0:T(8,128)S(1)}, f32[2,3,8,128]{3,2,1,0:T(8,128)S(1)}, f32[6]{0:T(128)}) custom-call(s32[3]{0:T(128)S(1)} %pad_add_fusion.role, s32[80,16]{1,0:T(8,128)S(1)} %bitcast.6, s32[8,8]{1,0:T(8,128)S(1)} %get-tuple-element.25.counts_vmem, f32[6]{0:T(128)} %motion_hbm.3, ...), custom_call_target="tpu_custom_call" | custom-call | tf_op jit(solution)/shard_map/pairs/pallas_call | solution.py:562
  53.8 6.2 %exchange.1 = (f32[3,3,2,8,128]{4,3,2,1,0:T(8,128)S(1)}, f32[2,3,8,128]{3,2,1,0:T(8,128)S(1)}, f32[2,3,8,128]{3,2,1,0:T(8,128)S(1)}, f32[2,3,8,128]{3,2,1,0:T(8,128)S(1)}) custom-call(f32[3,2,8,128]{3,2,1,0:T(8,128)S(1)} %get-tuple-element.33.more_shift, f32[2,3,8,128]{3,2,1,0:T(8,128)S(1)} %get-tuple-element.34.plane_edge, ...), custom_call_target="tpu_custom_call" | custom-call | tf_op jit(solution)/shard_map/exchange/pallas_call | solution.py:655
  60.1 0.0 copy-done
  60.1 1.4 %volumes.1 = (f32[3,8,8,128]{3,2,1,0:T(8,128)}, f32[8,8,128]{2,1,0:T(8,128)}, f32[8,8,128]{2,1,0:T(8,128)}) custom-call(s32[3]{0:T(128)S(1)} %pad_add_fusion.role, f32[3,8,8,128]{3,2,1,0:T(8,128)S(1)} %copy-done, f32[3,8,8,128]{3,2,1,0:T(8,128)S(1)} %get-tuple-element.32.shift, f32[3,3,2,8,128]{4,3,2,1,0:T(8,128)S(1)} %get-tuple-element.36.back, ...), custom_call_target="tpu_custom_call" | custom-call | tf_op jit(solution)/shard_map/volumes/pallas_call | solution.py:727
Async XLA Ops:
  38.0 22.0 %copy-start = (f32[3,8,8,128]{3,2,1,0:T(8,128)S(1)}, f32[3,8,8,128]{3,2,1,0:T(8,128)}, u32[]{:S(2)}) copy-start(f32[3,8,8,128]{3,2,1,0:T(8,128)} %nodes.1) | copy-start | bytes 294916

commit v8 on v7

--- a/solution.py
+++ b/solution.py
@@ -24,11 +24,11 @@
 
 def place():
     slab = lax.axis_index("slab")
-    return slab // (ZS * CORES), lax.axis_index("ctrl"), (slab // CORES) % ZS, slab % CORES
+    return slab >> 5, lax.axis_index("ctrl"), (slab >> 1) & (ZS - 1), slab & 1
 
 
 def device(x, y, z, core):
-    return {"slab": (x % XS * ZS + z % ZS) * CORES + core, "ctrl": y % YS}
+    return {"slab": ((x & (XS - 1)) << 5) + ((z & (ZS - 1)) << 1) + core, "ctrl": y & (YS - 1)}
 
 
 def is_heavy():
@@ -37,7 +37,7 @@
 
 
 def heavy_x(z):
-    return 2 - z // 8
+    return 2 - (z >> 3)
 
 
 def split3(value):
@@ -160,9 +160,11 @@
     for copy in fetches:
         copy.start()
 
+    along = {d: device(x, y, z + d, core) for d in (4, -4, 3, -3, 2, -2, 1, -1)}
+    peers = [device(x + dx, y + dy, z, core) for dx, dy in plane]
+    crossing = [device(x + dx, y + dy, z, core) for dx, dy in turned]
     barrier = pltpu.get_barrier_semaphore()
-    greet = [device(x, y, z + d, core) for d in (4, -4, 3, -3, 2, -2, 1, -1)]
-    greet += [device(x + dx, y + dy, z, core) for dx, dy in plane + turned]
+    greet = list(along.values()) + peers + crossing
     greet += [device(x, y, z, 1 - core)]
     for target in greet:
         pl.semaphore_signal(barrier, inc=1, device_id=target, device_id_type=MESH)
@@ -250,8 +252,8 @@
 
     near = {}
     for d in (4, 3, 2, 1):
-        near[d] = put(own, slot(4 - d), d - 1, device(x, y, z + d, core))
-        near[-d] = put(own, slot(4 + d), d + 3, device(x, y, z - d, core))
+        near[d] = put(own, slot(4 - d), d - 1, along[d])
+        near[-d] = put(own, slot(4 + d), d + 3, along[-d])
 
     @pl.when(heavy)
     def _():
@@ -269,22 +271,21 @@
     far = []
     for d in (1, 2, 3, 4):
         near[d].wait_recv()
-        far.append(put(slot(4 - d), slot(16 - d), d + 7, device(x, y, z + 4, core)))
+        far.append(put(slot(4 - d), slot(16 - d), d + 7, along[4]))
         near[-d].wait_recv()
         if d < 4:
-            far.append(put(slot(4 + d), slot(8 + d), d + 11, device(x, y, z - 4, core)))
+            far.append(put(slot(4 + d), slot(8 + d), d + 11, along[-4]))
 
     halves = (pl.ds(0, 9), pl.ds(9, 7))
 
     def first(part):
         ref = buf.at[x, halves[part], :, group]
         return [
-            put(ref, ref, 15 + 3 * part + i, device(x + dx, y + dy, z, core)) for i, (dx, dy) in enumerate(plane)
+            put(ref, ref, 15 + 3 * part + i, peer) for i, peer in enumerate(peers)
         ]
 
     def second(part, start):
-        for i, (dx, dy) in enumerate(turned):
-            target = device(x + dx, y + dy, z, core)
+        for i, target in enumerate(crossing):
 
             def make(ref, i=i, target=target):
                 return pltpu.make_async_remote_copy(
@@ -522,9 +523,9 @@
     for e in range(BLOCK):
         unit_of[n + e] = lines << 6
 
-    def block(g, _):
-        for u in range(0, BLOCK, 2):
-            i = g * BLOCK + u
+    def block(start, units):
+        for u in range(0, units, 2):
+            i = start + u
             c1, c2 = unit_of[i], unit_of[i + 1]
             l1, l2 = c1 >> 6, c2 >> 6
             out = pair(c1 & (NTILE - 1), c2 & (NTILE - 1), beside(l1, l2))
@@ -532,7 +533,9 @@
             sums[l2] += out[8:16, 128:256]
         return 0
 
-    lax.fori_loop(0, (n + BLOCK - 1) >> 5, block, 0)
+    whole = (n + BLOCK // 2 - 1) >> 5
+    lax.fori_loop(0, whole, lambda g, _: block(g * BLOCK, BLOCK), 0)
+    lax.fori_loop(0, jnp.where(n > whole * BLOCK, 1, 0), lambda g, _: block(whole * BLOCK, BLOCK // 2), 0)
 
     for copy in fetches[2:]:
         copy.wait()
@@ -593,7 +596,7 @@
     last = XS * ZS * CORES
 
     def at(ds, dy):
-        return {"slab": (slab + ds + last) % last, "ctrl": (y + dy + YS) % YS}
+        return {"slab": (slab + ds) & (last - 1), "ctrl": (y + dy) & (YS - 1)}
 
     barrier = pltpu.get_barrier_semaphore()
     greet = [at(1, 0), at(-1, 0), at(0, 1), at(0, -1), at(1, 1), at(-1, -1)]
@@ -622,7 +625,7 @@
             device_id_type=MESH,
         )
 
-    mine = (x - heavy_x(z) + 3) % XS
+    mine = (x - heavy_x(z) + 3) & (XS - 1)
 
     @pl.when(jnp.logical_not(heavy))
     def _():

time: 61.7 us -> 61.4 us (level)
  no operation moved by 1% of the time
where the time goes in v8:
time: 61.4 us; the launch traced here: 61.2 us
  Pallas kernels  60.4 us (98%)
  between operations  0.68 us (1%)
    pallas_call x1, Pallas kernels, gather(): pl.pallas_call(gather_kernel, out_shape=(jax.ShapeDtypeStruct((10, 8, 16)...  37.2 us
    pallas_call x1, Pallas kernels, pair_sums(): pl.pallas_call(pair_kernel, out_shape=(jax.ShapeDtypeStruct((3, 8, 8, 128...  15.8 us
    pallas_call x1, Pallas kernels, exchange(): pl.pallas_call(exchange_kernel, out_shape=(jax.ShapeDtypeStruct((3, 3, 2,...  6.02 us
    pallas_call x1, Pallas kernels, volumes(): pl.pallas_call(volume_kernel, out_shape=(jax.ShapeDtypeStruct((3, 8, 8, 1...  1.38 us

profile of v8, /device:TPU:1, one launch (start us, length us, event | category | flops | bytes accessed | tf_op | source)
XLA Modules:
  0.0 61.2 jit_solution(9478141217000932358)
XLA Ops:
  0.6 0.1 pad_add_fusion.role
  0.7 37.2 %gather.1 = (s32[10,8,16]{2,1,0:T(8,128)S(1)}, s32[8,8]{1,0:T(8,128)S(1)}, f32[64,24,128]{2,1,0:T(8,128)S(1)}, bf16[64,128,64]{2,1,0:T(8,128)(2,1)S(1)}, bf16[64...) custom-call(f32[3,16]{1,0:T(4,128)} %points_hbm.1, ...), custom_call_target="tpu_custom_call" | custom-call | tf_op jit(solution)/shard_map/gather/pallas_call | solution.py:381
  38.0 0.0 copy-start
  38.0 15.8 %pairs.1 = (f32[3,8,8,128]{3,2,1,0:T(8,128)S(1)}, f32[3,2,8,128]{3,2,1,0:T(8,128)S(1)}, f32[2,3,8,128]{3,2,1,0:T(8,128)S(1)}, f32[2,3,8,128]{3,2,1,0:T(8,128)S(1)}, f32[6]{0:T(128)}) custom-call(s32[3]{0:T(128)S(1)} %pad_add_fusion.role, s32[80,16]{1,0:T(8,128)S(1)} %bitcast.6, s32[8,8]{1,0:T(8,128)S(1)} %get-tuple-element.25.counts_vmem, f32[6]{0:T(128)} %motion_hbm.3, ...), custom_call_target="tpu_custom_call" | custom-call | tf_op jit(solution)/shard_map/pairs/pallas_call | solution.py:565
  53.8 6.0 %exchange.1 = (f32[3,3,2,8,128]{4,3,2,1,0:T(8,128)S(1)}, f32[2,3,8,128]{3,2,1,0:T(8,128)S(1)}, f32[2,3,8,128]{3,2,1,0:T(8,128)S(1)}, f32[2,3,8,128]{3,2,1,0:T(8,128)S(1)}) custom-call(f32[3,2,8,128]{3,2,1,0:T(8,128)S(1)} %get-tuple-element.33.more_shift, f32[2,3,8,128]{3,2,1,0:T(8,128)S(1)} %get-tuple-element.34.plane_edge, ...), custom_call_target="tpu_custom_call" | custom-call | tf_op jit(solution)/shard_map/exchange/pallas_call | solution.py:658
  59.8 0.0 copy-done
  59.8 1.4 %volumes.1 = (f32[3,8,8,128]{3,2,1,0:T(8,128)}, f32[8,8,128]{2,1,0:T(8,128)}, f32[8,8,128]{2,1,0:T(8,128)}) custom-call(s32[3]{0:T(128)S(1)} %pad_add_fusion.role, f32[3,8,8,128]{3,2,1,0:T(8,128)S(1)} %copy-done, f32[3,8,8,128]{3,2,1,0:T(8,128)S(1)} %get-tuple-element.32.shift, f32[3,3,2,8,128]{4,3,2,1,0:T(8,128)S(1)} %get-tuple-element.36.back, ...), custom_call_target="tpu_custom_call" | custom-call | tf_op jit(solution)/shard_map/volumes/pallas_call | solution.py:730
Async XLA Ops:
  38.0 21.8 %copy-start = (f32[3,8,8,128]{3,2,1,0:T(8,128)S(1)}, f32[3,8,8,128]{3,2,1,0:T(8,128)}, u32[]{:S(2)}) copy-start(f32[3,8,8,128]{3,2,1,0:T(8,128)} %nodes.1) | copy-start | bytes 294916

commit v9 on v8

--- a/solution.py
+++ b/solution.py
@@ -313,6 +313,8 @@
 
     half = jnp.where(iota((128, 64), 1) < 32, 1.0, 0.0).astype(BF16)
 
+    unit = jnp.where(iota((128, 128), 0) == iota((128, 128), 1), 1.0, 0.0).astype(BF16)
+
     def unpack(j, carry):
         for xx in range(XS):
             t = xx * ZS + ((j + z + ZS - 4) & (ZS - 1))
@@ -320,7 +322,12 @@
             for r in range(3):
                 feats[t, pl.ds(8 * r, 8), :] = v[r]
             parts = control_rows(v[0])
-            columns = jnp.transpose(jnp.concatenate(parts + parts, axis=0), (1, 0)).astype(BF16)
+            columns = lax.dot_general(
+                unit,
+                jnp.concatenate(parts + parts, axis=0).astype(BF16),
+                (((1,), (1,)), ((), ())),
+                preferred_element_type=F32,
+            ).astype(BF16)
             left = columns * half
             left_a[t] = left
             left_b[t] = columns - left
@@ -511,15 +518,21 @@
         own = jnp.where(i < 8, i, jnp.where(i < 15, (i - 7) << 3, i + 42))
         return jnp.where(heavy == 1, own, LINES + i + jnp.where(i < 7, 1, 2))
 
-    def full(b, _):
-        l1, l2 = full_line(2 * b), full_line(2 * b + 1)
+    def full(i):
+        l1, l2 = full_line(i), full_line(i + 1)
         for e in range(16):
             out = pair(ids[l1, e], ids[l2, e], beside(l1, l2))
             sums[l1] += out[0:8, 0:128]
             sums[l2] += out[8:16, 128:256]
+
+    def four(b, _):
+        full(4 * b)
+        full(4 * b + 2)
         return 0
 
-    lax.fori_loop(0, jnp.where(heavy == 1, 11, 7), full, 0)
+    fours = jnp.where(heavy == 1, 5, 3)
+    lax.fori_loop(0, fours, four, 0)
+    full(4 * fours)
     for e in range(BLOCK):
         unit_of[n + e] = lines << 6
 
@@ -533,8 +546,10 @@
             sums[l2] += out[8:16, 128:256]
         return 0
 
+    twos = n >> 6
+    lax.fori_loop(0, twos, lambda g, _: block(g * 2 * BLOCK, 2 * BLOCK), 0)
     whole = (n + BLOCK // 2 - 1) >> 5
-    lax.fori_loop(0, whole, lambda g, _: block(g * BLOCK, BLOCK), 0)
+    lax.fori_loop(2 * twos, whole, lambda g, _: block(g * BLOCK, BLOCK), 0)
     lax.fori_loop(0, jnp.where(n > whole * BLOCK, 1, 0), lambda g, _: block(whole * BLOCK, BLOCK // 2), 0)
 
     for copy in fetches[2:]:

time: 61.4 us -> 60.8 us (level)
    pallas_call x1, Pallas kernels: 15.8 us -> 14.8 us  [pair_sums(): pl.pallas_call(pair_kernel, out_shape=(jax.ShapeDtypeStruct((3, 8, 8, 128...]
where the time goes in v9:
time: 60.8 us; the launch traced here: 60.6 us
  Pallas kernels  59.8 us (98%)
  between operations  0.68 us (1%)
    pallas_call x1, Pallas kernels, gather(): pl.pallas_call(gather_kernel, out_shape=(jax.ShapeDtypeStruct((10, 8, 16)...  37.8 us
    pallas_call x1, Pallas kernels, pair_sums(): pl.pallas_call(pair_kernel, out_shape=(jax.ShapeDtypeStruct((3, 8, 8, 128...  14.8 us
    pallas_call x1, Pallas kernels, exchange(): pl.pallas_call(exchange_kernel, out_shape=(jax.ShapeDtypeStruct((3, 3, 2,...  5.91 us
    pallas_call x1, Pallas kernels, volumes(): pl.pallas_call(volume_kernel, out_shape=(jax.ShapeDtypeStruct((3, 8, 8, 1...  1.38 us

profile of v9, /device:TPU:1, one launch (start us, length us, event | category | flops | bytes accessed | tf_op | source)
XLA Modules:
  0.0 60.6 jit_solution(5192171559893671008)
XLA Ops:
  0.6 0.1 pad_add_fusion.role
  0.7 37.8 %gather.1 = (s32[10,8,16]{2,1,0:T(8,128)S(1)}, s32[8,8]{1,0:T(8,128)S(1)}, f32[64,24,128]{2,1,0:T(8,128)S(1)}, bf16[64,128,64]{2,1,0:T(8,128)(2,1)S(1)}, bf16[64...) custom-call(f32[3,16]{1,0:T(4,128)} %points_hbm.1, ...), custom_call_target="tpu_custom_call" | custom-call | tf_op jit(solution)/shard_map/gather/pallas_call | solution.py:388
  38.5 0.0 copy-start
  38.5 14.8 %pairs.1 = (f32[3,8,8,128]{3,2,1,0:T(8,128)S(1)}, f32[3,2,8,128]{3,2,1,0:T(8,128)S(1)}, f32[2,3,8,128]{3,2,1,0:T(8,128)S(1)}, f32[2,3,8,128]{3,2,1,0:T(8,128)S(1)}, f32[6]{0:T(128)}) custom-call(s32[3]{0:T(128)S(1)} %pad_add_fusion.role, s32[80,16]{1,0:T(8,128)S(1)} %bitcast.6, s32[8,8]{1,0:T(8,128)S(1)} %get-tuple-element.25.counts_vmem, f32[6]{0:T(128)} %motion_hbm.3, ...), custom_call_target="tpu_custom_call" | custom-call | tf_op jit(solution)/shard_map/pairs/pallas_call | solution.py:580
  53.3 5.9 %exchange.1 = (f32[3,3,2,8,128]{4,3,2,1,0:T(8,128)S(1)}, f32[2,3,8,128]{3,2,1,0:T(8,128)S(1)}, f32[2,3,8,128]{3,2,1,0:T(8,128)S(1)}, f32[2,3,8,128]{3,2,1,0:T(8,128)S(1)}) custom-call(f32[3,2,8,128]{3,2,1,0:T(8,128)S(1)} %get-tuple-element.33.more_shift, f32[2,3,8,128]{3,2,1,0:T(8,128)S(1)} %get-tuple-element.34.plane_edge, ...), custom_call_target="tpu_custom_call" | custom-call | tf_op jit(solution)/shard_map/exchange/pallas_call | solution.py:673
  59.2 0.0 copy-done
  59.2 1.4 %volumes.1 = (f32[3,8,8,128]{3,2,1,0:T(8,128)}, f32[8,8,128]{2,1,0:T(8,128)}, f32[8,8,128]{2,1,0:T(8,128)}) custom-call(s32[3]{0:T(128)S(1)} %pad_add_fusion.role, f32[3,8,8,128]{3,2,1,0:T(8,128)S(1)} %copy-done, f32[3,8,8,128]{3,2,1,0:T(8,128)S(1)} %get-tuple-element.32.shift, f32[3,3,2,8,128]{4,3,2,1,0:T(8,128)S(1)} %get-tuple-element.36.back, ...), custom_call_target="tpu_custom_call" | custom-call | tf_op jit(solution)/shard_map/volumes/pallas_call | solution.py:745
Async XLA Ops:
  38.5 20.7 %copy-start = (f32[3,8,8,128]{3,2,1,0:T(8,128)S(1)}, f32[3,8,8,128]{3,2,1,0:T(8,128)}, u32[]{:S(2)}) copy-start(f32[3,8,8,128]{3,2,1,0:T(8,128)} %nodes.1) | copy-start | bytes 294916

commit v10 on v9

--- a/solution.py
+++ b/solution.py
@@ -313,8 +313,6 @@
 
     half = jnp.where(iota((128, 64), 1) < 32, 1.0, 0.0).astype(BF16)
 
-    unit = jnp.where(iota((128, 128), 0) == iota((128, 128), 1), 1.0, 0.0).astype(BF16)
-
     def unpack(j, carry):
         for xx in range(XS):
             t = xx * ZS + ((j + z + ZS - 4) & (ZS - 1))
@@ -322,12 +320,7 @@
             for r in range(3):
                 feats[t, pl.ds(8 * r, 8), :] = v[r]
             parts = control_rows(v[0])
-            columns = lax.dot_general(
-                unit,
-                jnp.concatenate(parts + parts, axis=0).astype(BF16),
-                (((1,), (1,)), ((), ())),
-                preferred_element_type=F32,
-            ).astype(BF16)
+            columns = jnp.transpose(jnp.concatenate(parts + parts, axis=0), (1, 0)).astype(BF16)
             left = columns * half
             left_a[t] = left
             left_b[t] = columns - left

time: 60.8 us -> 60.1 us (0.988)
  Pallas kernels: 59.8 us -> 58.9 us
where the time goes in v10:
time: 60.1 us; the launch traced here: 59.6 us
  Pallas kernels  58.9 us (98%)
  between operations  0.68 us (1%)
    pallas_call x1, Pallas kernels, gather(): pl.pallas_call(gather_kernel, out_shape=(jax.ShapeDtypeStruct((10, 8, 16)...  37.2 us
    pallas_call x1, Pallas kernels, pair_sums(): pl.pallas_call(pair_kernel, out_shape=(jax.ShapeDtypeStruct((3, 8, 8, 128...  14.8 us
    pallas_call x1, Pallas kernels, exchange(): pl.pallas_call(exchange_kernel, out_shape=(jax.ShapeDtypeStruct((3, 3, 2,...  5.47 us
    pallas_call x1, Pallas kernels, volumes(): pl.pallas_call(volume_kernel, out_shape=(jax.ShapeDtypeStruct((3, 8, 8, 1...  1.38 us

profile of v10, /device:TPU:1, one launch (start us, length us, event | category | flops | bytes accessed | tf_op | source)
XLA Modules:
  0.0 59.6 jit_solution(15293799924173832399)
XLA Ops:
  0.6 0.1 pad_add_fusion.role
  0.7 37.2 %gather.1 = (s32[10,8,16]{2,1,0:T(8,128)S(1)}, s32[8,8]{1,0:T(8,128)S(1)}, f32[64,24,128]{2,1,0:T(8,128)S(1)}, bf16[64,128,64]{2,1,0:T(8,128)(2,1)S(1)}, bf16[64...) custom-call(f32[3,16]{1,0:T(4,128)} %points_hbm.1, ...), custom_call_target="tpu_custom_call" | custom-call | tf_op jit(solution)/shard_map/gather/pallas_call | solution.py:381
  38.0 0.0 copy-start
  38.0 14.8 %pairs.1 = (f32[3,8,8,128]{3,2,1,0:T(8,128)S(1)}, f32[3,2,8,128]{3,2,1,0:T(8,128)S(1)}, f32[2,3,8,128]{3,2,1,0:T(8,128)S(1)}, f32[2,3,8,128]{3,2,1,0:T(8,128)S(1)}, f32[6]{0:T(128)}) custom-call(s32[3]{0:T(128)S(1)} %pad_add_fusion.role, s32[80,16]{1,0:T(8,128)S(1)} %bitcast.6, s32[8,8]{1,0:T(8,128)S(1)} %get-tuple-element.25.counts_vmem, f32[6]{0:T(128)} %motion_hbm.3, ...), custom_call_target="tpu_custom_call" | custom-call | tf_op jit(solution)/shard_map/pairs/pallas_call | solution.py:573
  52.8 5.5 %exchange.1 = (f32[3,3,2,8,128]{4,3,2,1,0:T(8,128)S(1)}, f32[2,3,8,128]{3,2,1,0:T(8,128)S(1)}, f32[2,3,8,128]{3,2,1,0:T(8,128)S(1)}, f32[2,3,8,128]{3,2,1,0:T(8,128)S(1)}) custom-call(f32[3,2,8,128]{3,2,1,0:T(8,128)S(1)} %get-tuple-element.33.more_shift, f32[2,3,8,128]{3,2,1,0:T(8,128)S(1)} %get-tuple-element.34.plane_edge, ...), custom_call_target="tpu_custom_call" | custom-call | tf_op jit(solution)/shard_map/exchange/pallas_call | solution.py:666
  58.2 0.0 copy-done
  58.3 1.4 %volumes.1 = (f32[3,8,8,128]{3,2,1,0:T(8,128)}, f32[8,8,128]{2,1,0:T(8,128)}, f32[8,8,128]{2,1,0:T(8,128)}) custom-call(s32[3]{0:T(128)S(1)} %pad_add_fusion.role, f32[3,8,8,128]{3,2,1,0:T(8,128)S(1)} %copy-done, f32[3,8,8,128]{3,2,1,0:T(8,128)S(1)} %get-tuple-element.32.shift, f32[3,3,2,8,128]{4,3,2,1,0:T(8,128)S(1)} %get-tuple-element.36.back, ...), custom_call_target="tpu_custom_call" | custom-call | tf_op jit(solution)/shard_map/volumes/pallas_call | solution.py:738
Async XLA Ops:
  38.0 20.3 %copy-start = (f32[3,8,8,128]{3,2,1,0:T(8,128)S(1)}, f32[3,8,8,128]{3,2,1,0:T(8,128)}, u32[]{:S(2)}) copy-start(f32[3,8,8,128]{3,2,1,0:T(8,128)} %nodes.1) | copy-start | bytes 294916
